TPU v7x, 256 devices: a whole 4x4x8 slice. The times are simulated.
256 devices in a mesh: grp: 8 (over y, core), dev: 32 (over z, x).
Axes of the slice: x: 4, y: 4, z: 8, core: 2. Of those that a mesh axis runs over, the one named last changes fastest.
Arguments:
- objective: float32 [8, 32, 1024, 256], P('grp', 'dev'), may hold values from -24 to 24
- schur: float32 [8, 32, 1024, 1024], P('grp', 'dev')
- local_inverse: float32 [8, 32, 1024, 1024], P('grp', 'dev')
- coarse_basis: float32 [8, 32, 64, 1024], P('grp', 'dev'), may hold values from -0.09375 to 0.09375
- coarse_inverse: float32 [8, 32, 32, 8192], P(None, 'dev', None, 'grp')
- stiffness: int32 [8, 32, 1024], P('grp', 'dev'), may hold values from 1 to 8
- face_rows: int32 [8, 32, 4, 256], P('grp', 'dev'), may hold values from -1 to 1023, as said below
- coarse_map: int32 [8, 32, 64], P('grp', 'dev'), may hold values from 0 to 255
Outputs:
- adjoint: float32 [8, 32, 1024, 256], P('grp', 'dev')
Inputs may be any that keep to these rules, and one draw needn't show every extreme that they name: `face_rows`: slot k of face p names the local row of the k-th row that the subdomain shares with its neighbour across face p, or -1; the live slots of a face come first, and the neighbour lists the same shared rows in the same order in its opposite face. The live slots of a subdomain name its rows 0 to n - 1 once each, n at most 1024, and at least one subdomain has all 1024 rows. Faces at the ends of the layout are empty; a face that joins two subdomains has 1 to 256 rows. `coarse_map`: entry e of subdomain (g, d) names the coarse dof (e // 32, d, e % 32), owned by the subdomain at grp index e // 32 of the same dev index.
All inputs are finite; a program needn't handle non-finite values.
Results may differ from a plain program's by a relative error of at most 0.0003.
Values sent between devices are 32-bit elements; how exact they have to be, the bound alone decides.
No kernel may reach another device: no remote copies, remote signals or barrier semaphores. Data moves between devices by JAX's collectives and lax.ppermute only.
A program may use at most 64 MiB of HBM per device.

v0:
```python
import jax
import jax.numpy as jnp
from jax import lax
from jax.sharding import PartitionSpec as P

INTERFACE = 1024
FACE_ROWS = 256
OWNED = 32
SWEEPS = 2


def padded(value, sides, width):
    for axis, dim in sides:
        size, length = (lax.axis_size(axis), value.shape[dim])
        up = [(i, (i + 1) % size) for i in range(size - 1)]
        down = [(j, i) for i, j in up]
        last = lax.slice_in_dim(value, length - width, length, axis=dim)
        initial = lax.slice_in_dim(value, 0, width, axis=dim)
        before = lax.ppermute(last, axis, up)
        after = lax.ppermute(initial, axis, down)
        value = jnp.concatenate([before, value, after], axis=dim)
    return value


def contract_first(left, right):
    return lax.dot_general(
        left,
        right,
        (((0,), (0,)), ((), ())),
        precision=lax.Precision.HIGHEST,
        preferred_element_type=jnp.float32,
    )


def on_device(
    objective, schur, local_inverse, coarse_basis, coarse_inverse, stiffness, face_rows, coarse_map
):
    highest = lax.Precision.HIGHEST
    schur_block = schur[0, 0]
    local_block = local_inverse[0, 0]
    basis_rows = coarse_basis[0, 0]
    inverse_tile = coarse_inverse.reshape(-1, coarse_inverse.shape[3])
    slot_rows = face_rows[0, 0]
    local_map = coarse_map[0, 0]
    gradient = objective[0, 0]
    slot_count = 4 * FACE_ROWS
    slot_index = jnp.where(slot_rows < 0, INTERFACE, slot_rows).reshape(-1)
    empty_map = jnp.full((INTERFACE,), slot_count, jnp.int32)
    inverse = empty_map.at[slot_index].set(jnp.arange(slot_count, dtype=jnp.int32), mode="drop")
    live_rows = (inverse < slot_count).astype(jnp.float32)[:, None]

    def neighbour(values):
        packed = jnp.take(values, slot_index, axis=0, mode="fill", fill_value=0)
        packed = packed.reshape(4, FACE_ROWS, values.shape[-1])
        packet = jnp.stack([jnp.stack([packed[2], packed[1]]), jnp.stack([packed[0], packed[3]])])
        extended = padded(packet, (("grp", 0), ("dev", 1)), 1)
        received = jnp.stack([extended[1, 0], extended[2, 3], extended[0, 2], extended[3, 1]])
        received = received.reshape(slot_count, values.shape[-1])
        return jnp.take(received, inverse, axis=0, mode="fill", fill_value=0)

    multiplicity = stiffness[0, 0].astype(jnp.float32)[:, None]
    weight = live_rows * multiplicity / (multiplicity + neighbour(multiplicity))
    column_rows = inverse_tile.shape[0]
    onehot = (local_map[:, None] == jnp.arange(column_rows, dtype=jnp.int32)[None, :]).astype(
        jnp.float32
    )
    dev_position = lax.axis_index("dev")
    adjoint = jnp.zeros(gradient.shape, jnp.float32)
    for sweep_index in range(SWEEPS):
        if sweep_index == 0:
            remain = gradient
        else:
            remain = gradient - contract_first(schur_block, adjoint)
        residual = live_rows * (remain + neighbour(remain))
        weighted = weight * residual
        local_terms = jnp.dot(
            basis_rows, weighted, precision=highest, preferred_element_type=jnp.float32
        )
        spread_terms = contract_first(onehot, local_terms)
        column_residual = lax.psum(spread_terms, "grp")
        partial_sums = contract_first(inverse_tile, column_residual)
        summed = lax.psum(partial_sums, "dev")
        owned_part = lax.dynamic_slice_in_dim(summed, dev_position * OWNED, OWNED, 0)
        column_solution = lax.all_gather(owned_part, "grp", axis=0, tiled=True)
        local_solution = jnp.dot(
            onehot, column_solution, precision=highest, preferred_element_type=jnp.float32
        )
        correction = contract_first(basis_rows, local_solution)
        update = weight * (contract_first(local_block, weighted) + correction)
        adjoint = adjoint + update + neighbour(update)
    return adjoint[None, None]


def solution(mesh):
    return jax.shard_map(
        on_device,
        mesh=mesh,
        in_specs=(
            P("grp", "dev", None, None),
            P("grp", "dev", None, None),
            P("grp", "dev", None, None),
            P("grp", "dev", None, None),
            P(None, "dev", None, "grp"),
            P("grp", "dev", None),
            P("grp", "dev", None, None),
            P("grp", "dev", None),
        ),
        out_specs=P("grp", "dev", None, None),
        check_vma=False,
    )
```

profile of v0, /device:TPU:14, one launch (start us, length us, event | category | flops | bytes accessed | tf_op | source)
XLA Modules:
  0.0 766.2 jit_solution(6774467022367490812)
XLA Ops:
  41.0 5.8 collective-permute-start.6
  55.4 15.2 %collective-permute-done.6 = f32[4,1,256,256]{3,2,1,0:T(8,128)} collective-permute-done((f32[4,1,256,256]{3,2,1,0:T(8,128)}, f32[4,1,256,256]{3,2,1,0:T(8,128)}, u32[]{:S(2)}, u32[]{:S(2)}) %collective-permute-start.6) | collective-permute-done | bytes 1048608 | tf_op jit(solution)/shard_map/ppermute | solution.py:19
  71.5 9.8 %collective-permute-done.7 = f32[4,1,256,256]{3,2,1,0:T(8,128)S(1)} collective-permute-done((f32[4,1,256,256]{3,2,1,0:T(8,128)S(1)}, f32[4,1,256,256]{3,2,1,0:T(8,128)S(1)}, u32[]{:S(2)}, u32[]{:S(2)}) %collective-permute-start.7) | collective-permute-done | bytes 1048608 | tf_op jit(solution)/shard_map/ppermute | solution.py:20
  81.4 4.7 gather_fusion.3
  90.1 66.4 %all-reduce.5.cloned.1.call-done = f32[256,256]{1,0:T(8,128)} async-done(((f32[256,256]{1,0:T(8,128)}), f32[256,256]{1,0:T(8,128)}) %all-reduce.5.cloned.1.call-update) | async-done | bytes 262160 | tf_op jit(solution)/shard_map/psum | solution.py:80
  159.5 150.0 %all-reduce.7.cloned.1.call-done = f32[1024,256]{0,1:T(8,128)} async-done(((f32[1024,256]{0,1:T(8,128)}), f32[1024,256]{0,1:T(8,128)}) %all-reduce.7.cloned.1.call-update) | async-done | bytes 1048592 | tf_op jit(solution)/shard_map/psum | solution.py:82
  311.2 13.3 %all_gather.6 = f32[256,256]{1,0:T(8,128)S(1)} all-gather(f32[32,256]{1,0:T(8,128)} %copy.36), channel_id=1, replica_groups=mesh['grp'=8,'dev'=32] {'grp'}, dimensions={0}, use_global_device_ids=true | all-gather | bytes 294912 | tf_op jit(solution)/shard_map/all_gather | solution.py:84
  326.4 6.9 fusion.12
  334.9 4.7 gather_fusion.4
  345.8 4.7 collective-permute-done.9
  360.6 19.8 %collective-permute-done.10 = f32[4,1,256,256]{3,2,1,0:T(8,128)S(1)} collective-permute-done((f32[4,1,256,256]{3,2,1,0:T(8,128)S(1)}, f32[4,1,256,256]{3,2,1,0:T(8,128)S(1)}, u32[]{:S(2)}, u32[]{:S(2)}) %collective-permute-start.10) | collective-permute-done | bytes 1048608 | tf_op jit(solution)/shard_map/ppermute | solution.py:19
  380.4 5.8 collective-permute-done.11
  386.4 4.7 gather_fusion.5
  393.6 6.4 fusion.27
  400.4 4.7 gather_fusion.6
  425.5 19.1 %collective-permute-done.14 = f32[4,1,256,256]{3,2,1,0:T(8,128)S(1)} collective-permute-done((f32[4,1,256,256]{3,2,1,0:T(8,128)S(1)}, f32[4,1,256,256]{3,2,1,0:T(8,128)S(1)}, u32[]{:S(2)}, u32[]{:S(2)}) %collective-permute-start.14) | collective-permute-done | bytes 1048608 | tf_op jit(solution)/shard_map/ppermute | solution.py:19
  448.7 4.7 gather_fusion.7
  457.3 62.6 %all-reduce.9.cloned.1.call-done = f32[256,256]{1,0:T(8,128)} async-done(((f32[256,256]{1,0:T(8,128)}), f32[256,256]{1,0:T(8,128)}) %all-reduce.9.cloned.1.call-update) | async-done | bytes 262160 | tf_op jit(solution)/shard_map/psum | solution.py:80
  523.0 149.5 %all-reduce.11.cloned.1.call-done = f32[1024,256]{0,1:T(8,128)} async-done(((f32[1024,256]{0,1:T(8,128)}), f32[1024,256]{0,1:T(8,128)}) %all-reduce.11.cloned.1.call-update) | async-done | bytes 1048592 | tf_op jit(solution)/shard_map/psum | solution.py:82
  674.1 13.1 %all_gather.7 = f32[256,256]{1,0:T(8,128)S(1)} all-gather(f32[32,256]{1,0:T(8,128)} %copy.41), channel_id=1, replica_groups=mesh['grp'=8,'dev'=32] {'grp'}, dimensions={0}, use_global_device_ids=true | all-gather | bytes 294912 | tf_op jit(solution)/shard_map/all_gather | solution.py:84
  689.2 6.9 fusion.21
  706.2 4.7 collective-permute-done.17
  721.1 19.8 %collective-permute-done.18 = f32[4,1,256,256]{3,2,1,0:T(8,128)S(1)} collective-permute-done((f32[4,1,256,256]{3,2,1,0:T(8,128)S(1)}, f32[4,1,256,256]{3,2,1,0:T(8,128)S(1)}, u32[]{:S(2)}, u32[]{:S(2)}) %collective-permute-start.18) | collective-permute-done | bytes 1048608 | tf_op jit(solution)/shard_map/ppermute | solution.py:19
  740.8 5.8 collective-permute-done.19
  (163 shorter events, 143.1 us)
Async XLA Ops:
  6.5 149.9 %all-reduce.5.cloned.1.call-start = ((), (), s32[]{:S(2)}) async-start(), calls=%async_computation | async-start | bytes 524288 | tf_op jit(solution)/shard_map/psum | solution.py:80
  12.6 19.6 %collective-permute-start.1 = (f32[1,2,256,1]{2,1,3,0:T(2,128)S(1)}, f32[1,2,256,1]{2,1,3,0:T(2,128)S(1)}, u32[]{:S(2)}, u32[]{:S(2)}) collective-permute-start(f32[1,2,256,1]{2,1,3,0:T(2,128)S(1)} %maximum_bitcast_fusion.9), channel_id=1, source_target_pairs={{32,0},{64,32},{96,64},{128,96},{160,128},{192,160},{224,192},{33,... | collective-permute-start | bytes 6152 | tf_op jit(solution)/shard_map/ppermute | solution.py:20
  14.5 17.7 %collective-permute-start = (f32[1,2,256,1]{2,1,3,0:T(2,128)S(1)}, f32[1,2,256,1]{2,1,3,0:T(2,128)S(1)}, u32[]{:S(2)}, u32[]{:S(2)}) collective-permute-start(f32[1,2,256,1]{2,1,3,0:T(2,128)S(1)} %maximum_bitcast_fusion.8), channel_id=1, source_target_pairs={{0,32},{32,64},{64,96},{96,128},{128,160},{160,192},{192,224},{1,3... | collective-permute-start | bytes 6152 | tf_op jit(solution)/shard_map/ppermute | solution.py:19
  21.6 16.6 %collective-permute-start.5 = (f32[1,2,256,256]{3,2,1,0:T(8,128)}, f32[1,2,256,256]{3,2,1,0:T(8,128)}, u32[]{:S(2)}, u32[]{:S(2)}) collective-permute-start(f32[1,2,256,256]{3,2,1,0:T(8,128)} %maximum_bitcast_fusion.1), channel_id=1, source_target_pairs={{32,0},{64,32},{96,64},{128,96},{160,128},{192,160},{224,192},{33,... | collective-permute-start | bytes 1572872 | tf_op jit(solution)/shard_map/ppermute | solution.py:20
  25.6 12.6 %collective-permute-start.4 = (f32[1,2,256,256]{3,2,1,0:T(8,128)}, f32[1,2,256,256]{3,2,1,0:T(8,128)}, u32[]{:S(2)}, u32[]{:S(2)}) collective-permute-start(f32[1,2,256,256]{3,2,1,0:T(8,128)} %maximum_bitcast_fusion), channel_id=1, source_target_pairs={{0,32},{32,64},{64,96},{96,128},{128,160},{160,192},{192,224},{1,3... | collective-permute-start | bytes 1572872 | tf_op jit(solution)/shard_map/ppermute | solution.py:19
  32.3 5.9 collective-permute-start.2
  36.0 10.8 %collective-permute-start.3 = (f32[4,1,256,1]{2,1,3,0:T(1,128)S(1)}, f32[4,1,256,1]{2,1,3,0:T(1,128)S(1)}, u32[]{:S(2)}, u32[]{:S(2)}) collective-permute-start(f32[4,1,256,1]{2,1,3,0:T(1,128)S(1)} %get-tuple-element.38), channel_id=1, source_target_pairs={{1,0},{2,1},{3,2},{4,3},{5,4},{6,5},{7,6},{8,7},{9,8},{10,9},{11,1... | collective-permute-start | bytes 12296 | tf_op jit(solution)/shard_map/ppermute | solution.py:20
  41.0 29.5 %collective-permute-start.6 = (f32[4,1,256,256]{3,2,1,0:T(8,128)}, f32[4,1,256,256]{3,2,1,0:T(8,128)}, u32[]{:S(2)}, u32[]{:S(2)}) collective-permute-start(f32[4,1,256,256]{3,2,1,0:T(8,128)} %get-tuple-element.19), channel_id=1, source_target_pairs={{0,1},{1,2},{2,3},{3,4},{4,5},{5,6},{6,7},{7,8},{8,9},{9,10},{10,1... | collective-permute-start | bytes 3145736 | tf_op jit(solution)/shard_map/ppermute | solution.py:19
  51.4 29.9 %collective-permute-start.7 = (f32[4,1,256,256]{3,2,1,0:T(8,128)S(1)}, f32[4,1,256,256]{3,2,1,0:T(8,128)S(1)}, u32[]{:S(2)}, u32[]{:S(2)}) collective-permute-start(f32[4,1,256,256]{3,2,1,0:T(8,128)S(1)} %get-tuple-element.20), channel_id=1, source_target_pairs={{1,0},{2,1},{3,2},{4,3},{5,4},{6,5},{7,6},{8,7},{9,8},{10,9},{11,1... | collective-permute-start | bytes 3145736 | tf_op jit(solution)/shard_map/ppermute | solution.py:20
  90.0 219.4 %all-reduce.7.cloned.1.call-start = ((), (), s32[]{:S(2)}) async-start(), calls=%async_computation.1 | async-start | bytes 2097152 | tf_op jit(solution)/shard_map/psum | solution.py:82
  159.4 360.6 %all-reduce.9.cloned.1.call-start = ((), (), s32[]{:S(2)}) async-start(), calls=%async_computation.2 | async-start | bytes 524288 | tf_op jit(solution)/shard_map/psum | solution.py:80
  341.1 9.4 %collective-permute-start.9 = (f32[1,2,256,256]{3,2,1,0:T(8,128)S(1)}, f32[1,2,256,256]{3,2,1,0:T(8,128)S(1)}, u32[]{:S(2)}, u32[]{:S(2)}) collective-permute-start(f32[1,2,256,256]{3,2,1,0:T(8,128)S(1)} %maximum_bitcast_fusion.3), channel_id=1, source_target_pairs={{32,0},{64,32},{96,64},{128,96},{160,128},{192,160},{224,192},{33,... | collective-permute-start | bytes 1572872 | tf_op jit(solution)/shard_map/ppermute | solution.py:20
  343.9 10.5 %collective-permute-start.8 = (f32[1,2,256,256]{3,2,1,0:T(8,128)S(1)}, f32[1,2,256,256]{3,2,1,0:T(8,128)S(1)}, u32[]{:S(2)}, u32[]{:S(2)}) collective-permute-start(f32[1,2,256,256]{3,2,1,0:T(8,128)S(1)} %maximum_bitcast_fusion.2), channel_id=1, source_target_pairs={{0,32},{32,64},{64,96},{96,128},{128,160},{160,192},{192,224},{1,3... | collective-permute-start | bytes 1572872 | tf_op jit(solution)/shard_map/ppermute | solution.py:19
  354.6 25.8 %collective-permute-start.10 = (f32[4,1,256,256]{3,2,1,0:T(8,128)S(1)}, f32[4,1,256,256]{3,2,1,0:T(8,128)S(1)}, u32[]{:S(2)}, u32[]{:S(2)}) collective-permute-start(f32[4,1,256,256]{3,2,1,0:T(8,128)S(1)} %get-tuple-element.17), channel_id=1, source_target_pairs={{0,1},{1,2},{2,3},{3,4},{4,5},{5,6},{6,7},{7,8},{8,9},{9,10},{10,1... | collective-permute-start | bytes 3145736 | tf_op jit(solution)/shard_map/ppermute | solution.py:19
  358.7 27.6 %collective-permute-start.11 = (f32[4,1,256,256]{3,2,1,0:T(8,128)S(1)}, f32[4,1,256,256]{3,2,1,0:T(8,128)S(1)}, u32[]{:S(2)}, u32[]{:S(2)}) collective-permute-start(f32[4,1,256,256]{3,2,1,0:T(8,128)S(1)} %get-tuple-element.18), channel_id=1, source_target_pairs={{1,0},{2,1},{3,2},{4,3},{5,4},{6,5},{7,6},{8,7},{9,8},{10,9},{11,1... | collective-permute-start | bytes 3145736 | tf_op jit(solution)/shard_map/ppermute | solution.py:20
  406.6 8.6 %collective-permute-start.13 = (f32[1,2,256,256]{3,2,1,0:T(8,128)S(1)}, f32[1,2,256,256]{3,2,1,0:T(8,128)S(1)}, u32[]{:S(2)}, u32[]{:S(2)}) collective-permute-start(f32[1,2,256,256]{3,2,1,0:T(8,128)S(1)} %maximum_bitcast_fusion.5), channel_id=1, source_target_pairs={{32,0},{64,32},{96,64},{128,96},{160,128},{192,160},{224,192},{33,... | collective-permute-start | bytes 1572872 | tf_op jit(solution)/shard_map/ppermute | solution.py:20
  408.6 10.5 %collective-permute-start.12 = (f32[1,2,256,256]{3,2,1,0:T(8,128)S(1)}, f32[1,2,256,256]{3,2,1,0:T(8,128)S(1)}, u32[]{:S(2)}, u32[]{:S(2)}) collective-permute-start(f32[1,2,256,256]{3,2,1,0:T(8,128)S(1)} %maximum_bitcast_fusion.4), channel_id=1, source_target_pairs={{0,32},{32,64},{64,96},{96,128},{128,160},{160,192},{192,224},{1,3... | collective-permute-start | bytes 1572872 | tf_op jit(solution)/shard_map/ppermute | solution.py:19
  419.3 25.3 %collective-permute-start.14 = (f32[4,1,256,256]{3,2,1,0:T(8,128)S(1)}, f32[4,1,256,256]{3,2,1,0:T(8,128)S(1)}, u32[]{:S(2)}, u32[]{:S(2)}) collective-permute-start(f32[4,1,256,256]{3,2,1,0:T(8,128)S(1)} %get-tuple-element.15), channel_id=1, source_target_pairs={{0,1},{1,2},{2,3},{3,4},{4,5},{5,6},{6,7},{7,8},{8,9},{9,10},{10,1... | collective-permute-start | bytes 3145736 | tf_op jit(solution)/shard_map/ppermute | solution.py:19
  421.3 27.4 %collective-permute-start.15 = (f32[4,1,256,256]{3,2,1,0:T(8,128)S(1)}, f32[4,1,256,256]{3,2,1,0:T(8,128)S(1)}, u32[]{:S(2)}, u32[]{:S(2)}) collective-permute-start(f32[4,1,256,256]{3,2,1,0:T(8,128)S(1)} %get-tuple-element.16), channel_id=1, source_target_pairs={{1,0},{2,1},{3,2},{4,3},{5,4},{6,5},{7,6},{8,7},{9,8},{10,9},{11,1... | collective-permute-start | bytes 3145736 | tf_op jit(solution)/shard_map/ppermute | solution.py:20
  457.3 215.2 %all-reduce.11.cloned.1.call-start = ((), (), s32[]{:S(2)}) async-start(), calls=%async_computation.3 | async-start | bytes 2097152 | tf_op jit(solution)/shard_map/psum | solution.py:82
  701.5 9.4 %collective-permute-start.17 = (f32[1,2,256,256]{3,2,1,0:T(8,128)S(1)}, f32[1,2,256,256]{3,2,1,0:T(8,128)S(1)}, u32[]{:S(2)}, u32[]{:S(2)}) collective-permute-start(f32[1,2,256,256]{3,2,1,0:T(8,128)S(1)} %maximum_bitcast_fusion.7), channel_id=1, source_target_pairs={{32,0},{64,32},{96,64},{128,96},{160,128},{192,160},{224,192},{33,... | collective-permute-start | bytes 1572872 | tf_op jit(solution)/shard_map/ppermute | solution.py:20
  704.3 10.5 %collective-permute-start.16 = (f32[1,2,256,256]{3,2,1,0:T(8,128)S(1)}, f32[1,2,256,256]{3,2,1,0:T(8,128)S(1)}, u32[]{:S(2)}, u32[]{:S(2)}) collective-permute-start(f32[1,2,256,256]{3,2,1,0:T(8,128)S(1)} %maximum_bitcast_fusion.6), channel_id=1, source_target_pairs={{0,32},{32,64},{64,96},{96,128},{128,160},{160,192},{192,224},{1,3... | collective-permute-start | bytes 1572872 | tf_op jit(solution)/shard_map/ppermute | solution.py:19
  715.0 25.8 %collective-permute-start.18 = (f32[4,1,256,256]{3,2,1,0:T(8,128)S(1)}, f32[4,1,256,256]{3,2,1,0:T(8,128)S(1)}, u32[]{:S(2)}, u32[]{:S(2)}) collective-permute-start(f32[4,1,256,256]{3,2,1,0:T(8,128)S(1)} %get-tuple-element.13), channel_id=1, source_target_pairs={{0,1},{1,2},{2,3},{3,4},{4,5},{5,6},{6,7},{7,8},{8,9},{9,10},{10,1... | collective-permute-start | bytes 3145736 | tf_op jit(solution)/shard_map/ppermute | solution.py:19
  719.1 27.6 %collective-permute-start.19 = (f32[4,1,256,256]{3,2,1,0:T(8,128)S(1)}, f32[4,1,256,256]{3,2,1,0:T(8,128)S(1)}, u32[]{:S(2)}, u32[]{:S(2)}) collective-permute-start(f32[4,1,256,256]{3,2,1,0:T(8,128)S(1)} %get-tuple-element.14), channel_id=1, source_target_pairs={{1,0},{2,1},{3,2},{4,3},{5,4},{6,5},{7,6},{8,7},{9,8},{10,9},{11,1... | collective-permute-start | bytes 3145736 | tf_op jit(solution)/shard_map/ppermute | solution.py:20
  (15 other events, 245.1 us)
Sparse Core Ops, SparseCore 0:
  90.1 66.2 all-reduce.4
  160.3 149.1 all-reduce.6
  457.4 62.5 all-reduce.8
  523.3 149.1 all-reduce.10
where the time goes:
time: 767 us; the launch traced here: 766 us
  waiting for transfers between devices  553 us (72%)
  local copies, waits for them, and re-layouts  72.2 us (9%)
  starting transfers between devices  54.6 us (7%)
  matrix products  34.6 us (5%)
  blocking collectives  26.3 us (3%)
  between operations  14 us (2%)
  other arithmetic  11.2 us (1%)
    psum x2, waiting for transfers between devices, on_device(): summed = lax.psum(partial_sums, 'dev')  300 us
    psum x2, waiting for transfers between devices, on_device(): column_residual = lax.psum(spread_terms, 'grp')  129 us
    ppermute x10, waiting for transfers between devices, padded(): before = lax.ppermute(last, axis, up)  85.5 us
    ppermute x10, waiting for transfers between devices, padded(): after = lax.ppermute(initial, axis, down)  39.2 us
    gather x9, local copies, waits for them, and re-layouts, neighbour(): return jnp.take(received, inverse, axis=0, mode='fill', fill_value=0)  31.6 us
    dot_general x9, matrix products, contract_first(): lax.dot_general(left, right, (((0,), (0,)), ((), ())), precision=lax.Prec...  30.5 us
    ppermute x10, starting transfers between devices, padded(): before = lax.ppermute(last, axis, up)  30.1 us
    all_gather x2, blocking collectives, on_device(): column_solution = lax.all_gather(owned_part, 'grp', axis=0, tiled=True)  26.3 us
  transfers between devices with their start and end apart: 24, of which 18 were waited for; matrix products, arithmetic and copies ran while one was open for 3% of the time, Pallas kernels for 0%

commit v1 on v0

v1 whole, which is shorter than its diff:
```python
import functools

import jax
import jax.numpy as jnp
from jax import lax
from jax.experimental import pallas as pl
from jax.experimental.pallas import tpu as pltpu
from jax.sharding import PartitionSpec as P

INTERFACE = 1024
FACE_ROWS = 256
COLUMNS = 256
OWNED = 32
LOCAL = 64
SWEEPS = 2
X_SIZE = 4
TILE = 256
FACES = 4
TERM_ROWS = LOCAL + 8
MULT_ROWS = COLUMNS + 8
LIFT_ROWS = COLUMNS + LOCAL

NN = (((1,), (0,)), ((), ()))
NT = (((1,), (1,)), ((), ()))
TN = (((0,), (0,)), ((), ()))

VMEM = pl.BlockSpec(memory_space=pltpu.VMEM)
SMEM = pl.BlockSpec(memory_space=pltpu.SMEM)


def shaped(*shape, dtype=jnp.float32):
    return jax.ShapeDtypeStruct(shape, dtype)


def params():
    return pltpu.CompilerParams(vmem_limit_bytes=40 << 20)


def cost(flops, moved):
    return pl.CostEstimate(flops=flops, bytes_accessed=moved, transcendentals=0)


def split(value):
    high = value.astype(jnp.bfloat16)
    low = (value - high.astype(jnp.float32)).astype(jnp.bfloat16)
    return high, low


def mul(left, right, dims):
    return lax.dot_general(left, right, dims, preferred_element_type=jnp.float32)


def mul3(left, right, dims):
    left_high, left_low = left
    right_high, right_low = right
    return (
        mul(left_high, right_low, dims)
        + mul(left_low, right_high, dims)
        + mul(left_high, right_high, dims)
    )


def row_tile(slots_ref, t):
    rows = lax.broadcasted_iota(jnp.int32, (TILE, INTERFACE), 0) + t * TILE
    return (rows == slots_ref[...]).astype(jnp.float32).astype(jnp.bfloat16)


def tile_at(t):
    return pl.ds(pl.multiple_of(t * TILE, TILE), TILE)


def face_at(p):
    return slice(p * FACE_ROWS, (p + 1) * FACE_ROWS)


def pack_kernel(slots_ref, objective_ref, small_ref, basis_ref, *rest):
    outs, (acc, acc_small) = rest[:FACES], rest[FACES:]
    acc[...] = jnp.zeros_like(acc)
    acc_small[...] = jnp.zeros_like(acc_small)

    @pl.loop(0, INTERFACE // TILE)
    def _(t):
        onehot = row_tile(slots_ref, t)
        high, low = split(objective_ref[tile_at(t), :].T)
        acc[...] += mul(high, onehot, NN) + mul(low, onehot, NN)
        high, low = split(small_ref[:, tile_at(t)])
        acc_small[...] += mul(high, onehot, NN) + mul(low, onehot, NN)

    basis_ref[...] = acc_small[:LOCAL]
    for p in range(FACES):
        outs[p][:COLUMNS] = acc[:, face_at(p)]
        outs[p][COLUMNS:] = acc_small[LOCAL:, face_at(p)]


def pack_call(slots, objective, small):
    return pl.pallas_call(
        pack_kernel,
        out_shape=[shaped(LOCAL, INTERFACE)] + [shaped(MULT_ROWS, FACE_ROWS)] * FACES,
        in_specs=[VMEM] * 3,
        out_specs=[VMEM] * 5,
        scratch_shapes=[
            pltpu.VMEM((COLUMNS, INTERFACE), jnp.float32),
            pltpu.VMEM((TERM_ROWS, INTERFACE), jnp.float32),
        ],
        compiler_params=params(),
        cost_estimate=cost(3 << 30, 4 << 20),
        name="pack",
    )(slots, objective, small)


def weigh_kernel(first, *refs):
    here, there = refs[:FACES], refs[FACES : 2 * FACES]
    basis_ref, map_ref = refs[2 * FACES : 2 * FACES + 2]
    weighted_ref, terms_ref = refs[2 * FACES + 2 : 2 * FACES + 4]
    terms = jnp.zeros((LOCAL, COLUMNS), jnp.float32)
    for p in range(FACES):
        mine = here[p][COLUMNS : COLUMNS + 1]
        total = mine + there[p][COLUMNS : COLUMNS + 1]
        weight = jnp.where(total > 0, mine / jnp.maximum(total, 1.0), 0.0)
        weighted = weight * (here[p][:COLUMNS] + there[p][:COLUMNS])
        weighted_ref[:, face_at(p)] = weighted
        basis = basis_ref[:, face_at(p)]
        terms = terms + mul3(split(basis), split(weighted), NT)
        if first:
            weight_ref, lift_ref = refs[2 * FACES + 4 :]
            weight_ref[:, face_at(p)] = jnp.broadcast_to(weight, (8, FACE_ROWS))
            lift_ref[:, face_at(p)] = basis * weight
    terms_ref[:LOCAL] = terms
    terms_ref[LOCAL:] = map_ref[...]


def weigh_call(here, there, basis, map_row, first):
    out = [shaped(COLUMNS, INTERFACE), shaped(TERM_ROWS, COLUMNS)]
    if first:
        out += [shaped(8, INTERFACE), shaped(LOCAL, INTERFACE)]
    return pl.pallas_call(
        functools.partial(weigh_kernel, first),
        out_shape=out,
        in_specs=[VMEM] * (2 * FACES + 2),
        out_specs=[VMEM] * len(out),
        compiler_params=params(),
        cost_estimate=cost(100 << 20, 3 << 20),
        name="weigh",
    )(*here, *there, basis, map_row)


def coarse_kernel(n_grp, nz, nx, x_ref, half_ref, other_ref, high_ref, low_ref, *rest):
    outs, scratch = rest[:nx], rest[nx]
    dofs = n_grp * OWNED
    column = jnp.zeros((dofs, COLUMNS), jnp.float32)
    rows = lax.broadcasted_iota(jnp.int32, (dofs, LOCAL), 0).astype(jnp.float32)
    for ref in (half_ref, other_ref):
        for j in range(n_grp // 2):
            at = j * TERM_ROWS
            names = ref[at + LOCAL : at + LOCAL + 1, :LOCAL]
            onehot = (rows == names).astype(jnp.float32).astype(jnp.bfloat16)
            high, low = split(ref[at : at + LOCAL, :])
            column = column + mul(onehot, high, NN) + mul(onehot, low, NN)
    right = split(column)
    chunk = nx * OWNED
    x_pos = x_ref[0]

    @pl.loop(0, nz)
    def _(z):
        at = pl.ds(pl.multiple_of(z * chunk, chunk), chunk)
        scratch[...] = mul3((high_ref[at, :], low_ref[at, :]), right, NN)
        for k in range(nx):
            start = pl.multiple_of((x_pos ^ k) * OWNED, OWNED)
            outs[k][pl.ds(pl.multiple_of(z * OWNED, OWNED), OWNED), :] = scratch[
                pl.ds(start, OWNED), :
            ]


def coarse_call(x_pos, half, other, high, low, n_grp, nz, nx):
    return pl.pallas_call(
        functools.partial(coarse_kernel, n_grp, nz, nx),
        out_shape=[shaped(nz * OWNED, COLUMNS)] * nx,
        in_specs=[SMEM] + [VMEM] * 4,
        out_specs=[VMEM] * nx,
        scratch_shapes=[pltpu.VMEM((nx * OWNED, COLUMNS), jnp.float32)],
        compiler_params=params(),
        cost_estimate=cost(600 << 20, 3 << 20),
        name="coarse",
    )(x_pos, half, other, high, low)


def fetch_kernel(wanted_ref, half_ref, other_ref, *outs):
    count = half_ref.shape[0]
    ids = lax.broadcasted_iota(jnp.int32, (LOCAL, count), 1)
    left, right = split(half_ref[...]), split(other_ref[...])
    for i, out in enumerate(outs):
        wanted = wanted_ref[i * LOCAL : (i + 1) * LOCAL, :]
        near = (wanted == ids).astype(jnp.float32).astype(jnp.bfloat16)
        far = (wanted == ids + count).astype(jnp.float32).astype(jnp.bfloat16)
        out[...] = (
            mul(near, left[0], NN)
            + mul(far, right[0], NN)
            + mul(near, left[1], NN)
            + mul(far, right[1], NN)
        )


def fetch_call(wanted, half, other):
    return pl.pallas_call(
        fetch_kernel,
        out_shape=[shaped(LOCAL, COLUMNS)] * 3,
        in_specs=[VMEM] * 3,
        out_specs=[VMEM] * 3,
        compiler_params=params(),
        cost_estimate=cost(100 << 20, 1 << 20),
        name="fetch",
    )(wanted, half, other)


def unpack(slots_ref, value, high_ref, low_ref):
    high, low = split(value)

    @pl.loop(0, INTERFACE // TILE)
    def _(t):
        onehot = row_tile(slots_ref, t)
        rows = mul(high, onehot, NT) + mul(low, onehot, NT)
        high_ref[:, tile_at(t)], low_ref[:, tile_at(t)] = split(rows)


def apply_tile(slots_ref, matrix_ref, high_ref, low_ref, acc):
    step = pl.program_id(0)

    @pl.when(step == 0)
    def _():
        acc[...] = jnp.zeros_like(acc)

    rows = mul3((high_ref[...], low_ref[...]), split(matrix_ref[...]), NN)
    high, low = split(rows)
    onehot = row_tile(slots_ref, step)
    acc[...] += mul(high, onehot, NN) + mul(low, onehot, NN)


def whole(shape):
    return pl.BlockSpec(shape, lambda i: (0,) * len(shape))


def columns_of(shape):
    return pl.BlockSpec((shape[0], TILE), lambda i: (0, i))


APPLY_SCRATCH = [
    pltpu.VMEM((COLUMNS, INTERFACE), jnp.bfloat16),
    pltpu.VMEM((COLUMNS, INTERFACE), jnp.bfloat16),
    pltpu.VMEM((COLUMNS, INTERFACE), jnp.float32),
]


def local_kernel(first, slots_ref, weighted_ref, matrix_ref, weight_ref, lift_ref, *rest):
    outs, (high, low, acc) = rest[:FACES], rest[FACES:]
    step = pl.program_id(0)

    @pl.when(step == 0)
    def _():
        unpack(slots_ref, weighted_ref[...], high, low)

    apply_tile(slots_ref, matrix_ref, high, low, acc)

    @pl.when(step == pl.num_programs(0) - 1)
    def _():
        for p in range(FACES):
            outs[p][:COLUMNS] = weight_ref[:1, face_at(p)] * acc[:, face_at(p)]
            if first:
                outs[p][COLUMNS:] = lift_ref[:, face_at(p)]


def local_call(slots, weighted, matrix, weight, lift, first):
    out = [shaped(LIFT_ROWS if first else COLUMNS, FACE_ROWS)] * FACES
    return pl.pallas_call(
        functools.partial(local_kernel, first),
        grid=(INTERFACE // TILE,),
        out_shape=out,
        in_specs=[
            whole(slots.shape),
            whole(weighted.shape),
            columns_of(matrix.shape),
            whole(weight.shape),
            whole(lift.shape),
        ],
        out_specs=[whole(o.shape) for o in out],
        scratch_shapes=APPLY_SCRATCH,
        compiler_params=params(),
        cost_estimate=cost(4 << 30, 8 << 20),
        name="local",
    )(slots, weighted, matrix, weight, lift)


def adjoint_face(p, near, far, lift_near, lift_far, own, around):
    change = mul3(own, split(lift_near[p][...]), TN)
    change = change + mul3(split(around[p][...]), split(lift_far[p][...]), TN)
    return near[p][...] + far[p][...] + change


def middle_kernel(slots_ref, *refs):
    groups = [refs[i * FACES : (i + 1) * FACES] for i in range(6)]
    near, far, lift_near, lift_far, around, gradient = groups
    own_ref, matrix_ref, adjoint_ref = refs[6 * FACES : 6 * FACES + 3]
    outs, (high, low, acc) = refs[6 * FACES + 3 : 7 * FACES + 3], refs[7 * FACES + 3 :]
    step = pl.program_id(0)

    @pl.when(step == 0)
    def _():
        own = split(own_ref[...])
        for p in range(FACES):
            adjoint_ref[:, face_at(p)] = adjoint_face(
                p, near, far, lift_near, lift_far, own, around
            )
        unpack(slots_ref, adjoint_ref[...], high, low)

    apply_tile(slots_ref, matrix_ref, high, low, acc)

    @pl.when(step == pl.num_programs(0) - 1)
    def _():
        for p in range(FACES):
            outs[p][:COLUMNS] = gradient[p][:COLUMNS] - acc[:, face_at(p)]
            outs[p][COLUMNS:] = gradient[p][COLUMNS:]


def top(i):
    return (0, 0)


def tail(i):
    return (COLUMNS // LOCAL, 0)


def update_specs():
    body = pl.BlockSpec((COLUMNS, FACE_ROWS), top)
    lift = pl.BlockSpec((LOCAL, FACE_ROWS), tail)
    around = pl.BlockSpec((LOCAL, COLUMNS), top)
    return [body] * (2 * FACES) + [lift] * (2 * FACES) + [around] * FACES


def middle_call(slots, near, far, lift_near, lift_far, around, gradient, own, matrix):
    out = [shaped(COLUMNS, INTERFACE)] + [shaped(MULT_ROWS, FACE_ROWS)] * FACES
    return pl.pallas_call(
        middle_kernel,
        grid=(INTERFACE // TILE,),
        out_shape=out,
        in_specs=[whole(slots.shape)]
        + update_specs()
        + [whole(gradient[0].shape)] * FACES
        + [whole(own.shape), columns_of(matrix.shape)],
        out_specs=[whole(o.shape) for o in out],
        scratch_shapes=APPLY_SCRATCH,
        compiler_params=params(),
        cost_estimate=cost(4 << 30, 12 << 20),
        name="middle",
    )(slots, *near, *far, *lift_near, *lift_far, *around, *gradient, own, matrix)


def last_kernel(slots_ref, *refs):
    groups = [refs[i * FACES : (i + 1) * FACES] for i in range(5)]
    near, far, lift_near, lift_far, around = groups
    own_ref, adjoint_ref, out_ref, high, low = refs[5 * FACES :]
    step = pl.program_id(0)

    @pl.when(step == 0)
    def _():
        own = split(own_ref[...])
        for p in range(FACES):
            value = adjoint_ref[:, face_at(p)] + adjoint_face(
                p, near, far, lift_near, lift_far, own, around
            )
            high[:, face_at(p)], low[:, face_at(p)] = split(value)

    onehot = row_tile(slots_ref, step)
    out_ref[...] = mul(onehot, high[...], NT) + mul(onehot, low[...], NT)


def last_call(slots, near, far, lift_near, lift_far, around, own, adjoint):
    return pl.pallas_call(
        last_kernel,
        grid=(INTERFACE // TILE,),
        out_shape=shaped(INTERFACE, COLUMNS),
        in_specs=[whole(slots.shape)]
        + update_specs()
        + [whole(own.shape), whole(adjoint.shape)],
        out_specs=pl.BlockSpec((TILE, COLUMNS), lambda i: (i, 0)),
        scratch_shapes=APPLY_SCRATCH[:2],
        compiler_params=params(),
        cost_estimate=cost(1 << 30, 6 << 20),
        name="last",
    )(slots, *near, *far, *lift_near, *lift_far, *around, own, adjoint)


def on_device(
    objective, schur, local_inverse, coarse_basis, coarse_inverse, stiffness, face_rows, coarse_map
):
    n_grp, n_dev = lax.axis_size("grp"), lax.axis_size("dev")
    nx = X_SIZE
    nz = n_dev // nx
    grp = lax.axis_index("grp")
    x_pos = (lax.axis_index("dev") % nx).astype(jnp.int32).reshape(1)
    z_groups = [[z * nx + x for z in range(nz)] for x in range(nx)]
    half_size = n_grp // 2

    def place(other):
        j = other ^ grp
        return j // 2 + half_size * (j % 2)

    def swap(value, axis, k):
        size = lax.axis_size(axis)
        return lax.ppermute(value, axis, [(i, i ^ k) for i in range(size)])

    def group_gather(value):
        parts = [value] + [swap(value, "grp", k) for k in range(2, n_grp, 2)]
        half = jnp.concatenate(parts, axis=0)
        return half, swap(half, "grp", 1)

    def pairs(axis):
        return [(i, i + 1) for i in range(lax.axis_size(axis) - 1)]

    def back(axis):
        return [(i + 1, i) for i in range(lax.axis_size(axis) - 1)]

    def exchange(faces):
        return [
            lax.ppermute(faces[1], "dev", pairs("dev")),
            lax.ppermute(faces[0], "dev", back("dev")),
            lax.ppermute(faces[3], "grp", pairs("grp")),
            lax.ppermute(faces[2], "grp", back("grp")),
        ]

    slots = face_rows[0, 0].reshape(1, -1)
    local_map = coarse_map[0, 0]
    multiplicity = jnp.pad(stiffness[0].astype(jnp.float32), ((0, 7), (0, 0)))
    small = jnp.concatenate([coarse_basis[0, 0], multiplicity], axis=0)
    basis, *gradient = pack_call(slots, objective[0, 0], small)
    arrived = exchange(gradient)

    map_row = jnp.zeros((8, COLUMNS), jnp.float32)
    map_row = map_row.at[0, :LOCAL].set(local_map.astype(jnp.float32))
    tile = coarse_inverse.reshape(-1, coarse_inverse.shape[3]).T
    tile_high = lax.reduce_precision(tile, 8, 7)
    tile_low = (tile - tile_high).astype(jnp.bfloat16)
    tile_high = tile_high.astype(jnp.bfloat16)

    weighted, terms, weight, lift = weigh_call(gradient, arrived, basis, map_row, True)
    wanted = None
    adjoint = None
    lift_near = lift_far = None
    for sweep in range(SWEEPS):
        first = sweep == 0
        half, other = group_gather(terms)
        if first:
            maps = jnp.concatenate([half, other], axis=0).reshape(n_grp, TERM_ROWS, COLUMNS)
            maps = maps[:, LOCAL, :LOCAL]
            above = lax.dynamic_slice_in_dim(maps, place(jnp.maximum(grp - 1, 0)), 1, 0)[0]
            below = lax.dynamic_slice_in_dim(maps, place(jnp.minimum(grp + 1, n_grp - 1)), 1, 0)[0]
            wanted = jnp.concatenate([local_map, above.astype(jnp.int32), below.astype(jnp.int32)])
            wanted = (place(wanted // OWNED) * OWNED + wanted % OWNED)[:, None]
        blocks = coarse_call(x_pos, half, other, tile_high, tile_low, n_grp, nz, nx)
        sent = [swap(blocks[k], "dev", k) for k in (2, 1, 3)]
        near = local_call(slots, weighted, local_inverse[0, 0], weight, lift, first)
        total = blocks[0] + sent[0] + sent[1] + sent[2]
        total = lax.all_to_all(
            total.reshape(nz, OWNED, COLUMNS), "dev", 0, 0, axis_index_groups=z_groups, tiled=True
        )
        owned = total.sum(0)
        far = exchange(near)
        if first:
            lift_near, lift_far = near, far
        own, above, below = fetch_call(wanted, *group_gather(owned))
        around = [
            lax.ppermute(own, "dev", pairs("dev")),
            lax.ppermute(own, "dev", back("dev")),
            above,
            below,
        ]
        if first:
            adjoint, *remain = middle_call(
                slots, near, far, lift_near, lift_far, around, gradient, own, schur[0, 0]
            )
            weighted, terms = weigh_call(remain, exchange(remain), basis, map_row, False)
        else:
            out = last_call(slots, near, far, lift_near, lift_far, around, own, adjoint)
    return out[None, None]


def solution(mesh):
    return jax.shard_map(
        on_device,
        mesh=mesh,
        in_specs=(
            P("grp", "dev", None, None),
            P("grp", "dev", None, None),
            P("grp", "dev", None, None),
            P("grp", "dev", None, None),
            P(None, "dev", None, "grp"),
            P("grp", "dev", None),
            P("grp", "dev", None, None),
            P("grp", "dev", None),
        ),
        out_specs=P("grp", "dev", None, None),
        check_vma=False,
    )
```

time: 767 us -> 242 us (0.32)
  waiting for transfers between devices: 553 us -> 47.4 us
  local copies, waits for them, and re-layouts: 72.2 us -> 24.2 us
  starting transfers between devices: 54.6 us -> 101 us
  Pallas kernels: 0 us -> 39.7 us
  matrix products: 34.6 us -> 0 us
  between operations: 14 us -> 0.78 us
    psum x4 -> x0, waiting for transfers between devices: 429 us -> none  [the longest x2 300 us: on_device(): summed = lax.psum(partial_sums, 'dev')]
    ppermute x20 -> x42, waiting for transfers between devices: 125 us -> 47.4 us  [the longest x22 33.9 us: swap(): return lax.ppermute(value, axis, [(i, i ^ k) for i in range(size)])]
    gather x14 -> x0, local copies, waits for them, and re-layouts: 52.3 us -> none  [the longest x9 31.6 us: neighbour(): return jnp.take(received, inverse, axis=0, mode='fill', fill_value=0)]
    pallas_call x0 -> x11, Pallas kernels: none -> 39.7 us  [the longest x2 16.7 us: local_call(): pl.pallas_call(functools.partial(local_kernel, first), grid=(INTERFACE //...]
    ppermute x20 -> x42, starting transfers between devices: 54.5 us -> 92.9 us  [the longest x22 27.2 us: swap(): return lax.ppermute(value, axis, [(i, i ^ k) for i in range(size)])]
    dot_general x13 -> x0, matrix products: 34.6 us -> none  [the longest x9 30.5 us: contract_first(): lax.dot_general(left, right, (((0,), (0,)), ((), ())), precision=lax.Prec...]
    all_gather x2 -> x0, blocking collectives: 26.3 us -> none  [on_device(): column_solution = lax.all_gather(owned_part, 'grp', axis=0, tiled=True)]
    unnamed x33 -> x83, local copies, waits for them, and re-layouts: 1.18 us -> 23.7 us
  transfers between devices with their start and end apart: 24 -> 43, of which waited for: 18 -> 24; matrix products, arithmetic and copies ran while one was open for 3% -> 1% of each run, Pallas kernels for 0% -> 7%
where the time goes in v1:
time: 242 us; the launch traced here: 238 us
  starting transfers between devices  101 us (42%)
  waiting for transfers between devices  47.4 us (20%)
  Pallas kernels  39.7 us (16%)
  local copies, waits for them, and re-layouts  24.2 us (10%)
  blocking collectives  20.4 us (8%)
  other arithmetic  3.97 us (2%)
    ppermute x22, waiting for transfers between devices, swap(): return lax.ppermute(value, axis, [(i, i ^ k) for i in range(size)])  33.9 us
    ppermute x22, starting transfers between devices, swap(): return lax.ppermute(value, axis, [(i, i ^ k) for i in range(size)])  27.2 us
    unnamed x83, local copies, waits for them, and re-layouts  23.7 us
    ppermute x4, starting transfers between devices, exchange(): lax.ppermute(faces[1], 'dev', pairs('dev'))  23.7 us
    all_to_all x1, blocking collectives, on_device(): lax.all_to_all(total.reshape(nz, OWNED, COLUMNS), 'dev', 0, 0, axis_index...  20.4 us
    pallas_call x2, Pallas kernels, local_call(): pl.pallas_call(functools.partial(local_kernel, first), grid=(INTERFACE //...  16.7 us
    ppermute x2, starting transfers between devices, on_device(): lax.ppermute(own, 'dev', pairs('dev'))  12.3 us
    pallas_call x1, Pallas kernels, middle_call(): pl.pallas_call(middle_kernel, grid=(INTERFACE // TILE,), out_shape=out, i...  9.28 us
  transfers between devices with their start and end apart: 43, of which 24 were waited for; matrix products, arithmetic and copies ran while one was open for 1% of the time, Pallas kernels for 7%

profile of v1, /device:TPU:14, one launch (start us, length us, event | category | flops | bytes accessed | tf_op | source)
XLA Modules:
  0.0 237.8 jit_solution(16541645719711865423)
XLA Ops:
  3.6 2.8 %pack.1 = (f32[64,1024]{1,0:T(8,128)S(1)}, f32[264,256]{1,0:T(8,128)S(1)}, f32[264,256]{1,0:T(8,128)S(1)}, f32[264,256]{1,0:T(8,128)S(1)}, f32[264,256]{1,0:T(8,128)S(1)}) custom-call(s32[1,1024]{1,0:T(1,128)S(1)} %bitcast.25, f32[1024,256]{1,0:T(8,128)S(1)} %bitcast.33, f32[72,1024]{1,0:T(8,128)S(1)} %select_maximum_fusion.small_ref), custom_call_target="tpu_custom_call" | custom-call | flops 3221225472 | bytes 4194304 | tf_op jit(solution)/shard_map/pack/pallas_call | solution.py:96
  6.4 2.7 %collective-permute-start.1 = (f32[264,256]{1,0:T(8,128)S(1)}, f32[264,256]{1,0:T(8,128)S(1)}, u32[]{:S(2)}, u32[]{:S(2)}) collective-permute-start(f32[264,256]{1,0:T(8,128)S(1)} %get-tuple-element.55.refs_0_.refs_20_), channel_id=1, source_target_pairs={{1,0},{2,1},{3,2},{4,3},{5,4},{6,5},{7,6},{8,7},{9,8},{10,9},{11,1... | collective-permute-start | bytes 811016 | tf_op jit(solution)/shard_map/ppermute | solution.py:424
  9.1 5.2 %collective-permute-start = (f32[264,256]{1,0:T(8,128)S(1)}, f32[264,256]{1,0:T(8,128)S(1)}, u32[]{:S(2)}, u32[]{:S(2)}) collective-permute-start(f32[264,256]{1,0:T(8,128)S(1)} %get-tuple-element.56.refs_1_.refs_21_), channel_id=1, source_target_pairs={{0,1},{1,2},{2,3},{3,4},{4,5},{5,6},{6,7},{7,8},{8,9},{9,10},{10,1... | collective-permute-start | bytes 811016 | tf_op jit(solution)/shard_map/ppermute | solution.py:423
  20.2 3.8 %collective-permute-done.2.refs_6_ = f32[264,256]{1,0:T(8,128)S(1)} collective-permute-done((f32[264,256]{1,0:T(8,128)S(1)}, f32[264,256]{1,0:T(8,128)S(1)}, u32[]{:S(2)}, u32[]{:S(2)}) %collective-permute-start.2) | collective-permute-done | bytes 270368 | tf_op jit(solution)/shard_map/ppermute | solution.py:425
  29.8 3.1 %collective-permute-done.8 = f32[72,256]{1,0:T(8,128)S(1)} collective-permute-done((f32[72,256]{1,0:T(8,128)S(1)}, f32[72,256]{1,0:T(8,128)S(1)}, u32[]{:S(2)}, u32[]{:S(2)}) %collective-permute-start.8) | collective-permute-done | bytes 73760 | tf_op jit(solution)/shard_map/ppermute | solution.py:408
  37.6 4.0 %collective-permute-start.14 = (f32[256,256]{1,0:T(8,128)S(1)}, f32[256,256]{1,0:T(8,128)S(1)}, u32[]{:S(2)}, u32[]{:S(2)}) collective-permute-start(f32[256,256]{1,0:T(8,128)S(1)} %get-tuple-element.71), channel_id=1, source_target_pairs={{0,3},{1,2},{2,1},{3,0},{4,7},{5,6},{6,5},{7,4},{8,11},{9,10},{10,... | collective-permute-start | bytes 786440 | tf_op jit(solution)/shard_map/ppermute | solution.py:408
  41.6 6.6 %collective-permute-done.12 = f32[256,256]{1,0:T(8,128)S(1)} collective-permute-done((f32[256,256]{1,0:T(8,128)S(1)}, f32[256,256]{1,0:T(8,128)S(1)}, u32[]{:S(2)}, u32[]{:S(2)}) %collective-permute-start.12) | collective-permute-done | bytes 262176 | tf_op jit(solution)/shard_map/ppermute | solution.py:408
  49.3 3.7 %collective-permute-done.14 = f32[256,256]{1,0:T(8,128)S(1)} collective-permute-done((f32[256,256]{1,0:T(8,128)S(1)}, f32[256,256]{1,0:T(8,128)S(1)}, u32[]{:S(2)}, u32[]{:S(2)}) %collective-permute-start.14) | collective-permute-done | bytes 262176 | tf_op jit(solution)/shard_map/ppermute | solution.py:408
  53.7 8.5 %all-to-all-start = ((f32[8,32,256]{2,1,0:T(8,128)}), f32[8,32,256]{2,1,0:T(8,128)}, u32[]{:S(2)}, u32[]{:S(2)}) async-start(f32[8,32,256]{2,1,0:T(8,128)} %bitcast.12), calls=%async_computation | async-start | bytes 524288 | tf_op jit(solution)/shard_map/all_to_all | solution.py:461
  66.6 8.4 %local.2 = (f32[320,256]{1,0:T(8,128)S(1)}, f32[320,256]{1,0:T(8,128)S(1)}, f32[320,256]{1,0:T(8,128)S(1)}, f32[320,256]{1,0:T(8,128)S(1)}) custom-call(s32[1,1024]{1,0:T(1,128)S(1)} %bitcast.26, f32[256,1024]{1,0:T(8,128)S(1)} %copy-done.28, f32[1024,1024]{1,0:T(8,128)S(1)} %bitcast.31, f32[8,1024]{1,0:T(8,128)S(1)} %get-tuple-element.61.weight_ref, ...), custom_call_target="tpu_custom_call" | custom-call | flops 4294967296 | bytes 8388608 | tf_op jit(solution)/shard_map/local/pallas_call | solution.py:273
  76.9 6.0 %collective-permute-start.4 = (f32[320,256]{1,0:T(8,128)S(1)}, f32[320,256]{1,0:T(8,128)S(1)}, u32[]{:S(2)}, u32[]{:S(2)}) collective-permute-start(f32[320,256]{1,0:T(8,128)S(1)} %get-tuple-element.64.refs_1_.refs_9_), channel_id=1, source_target_pairs={{0,1},{1,2},{2,3},{3,4},{4,5},{5,6},{6,7},{7,8},{8,9},{9,10},{10,1... | collective-permute-start | bytes 983048 | tf_op jit(solution)/shard_map/ppermute | solution.py:423
  98.3 6.2 %collective-permute-start.19 = (f32[64,256]{1,0:T(8,128)S(1)}, f32[64,256]{1,0:T(8,128)S(1)}, u32[]{:S(2)}, u32[]{:S(2)}) collective-permute-start(f32[64,256]{1,0:T(8,128)S(1)} %get-tuple-element.72.refs_24_), channel_id=1, source_target_pairs={{0,1},{1,2},{2,3},{3,4},{4,5},{5,6},{6,7},{7,8},{8,9},{9,10},{10,1... | collective-permute-start | bytes 196616 | tf_op jit(solution)/shard_map/ppermute | solution.py:470
  115.2 9.3 %middle.1 = (f32[256,1024]{1,0:T(8,128)S(1)}, f32[264,256]{1,0:T(8,128)S(1)}, f32[264,256]{1,0:T(8,128)S(1)}, f32[264,256]{1,0:T(8,128)S(1)}, f32[264,256]{1,0:T(8,128)S(1)}) custom-call(s32[1,1024]{1,0:T(1,128)S(1)} %bitcast.27, f32[320,256]{1,0:T(8,128)S(1)} %get-tuple-element.63.refs_0_.refs_8_, f32[320,256]{1,0:T(8,128)S(1)} %get-tuple-element.64.refs_1_.refs_9_, ...), custom_call_target="tpu_custom_call" | custom-call | flops 4294967296 | bytes 12582912 | tf_op jit(solution)/shard_map/middle/pallas_call | solution.py:340
  126.4 6.4 %collective-permute-start.21 = (f32[264,256]{1,0:T(8,128)S(1)}, f32[264,256]{1,0:T(8,128)S(1)}, u32[]{:S(2)}, u32[]{:S(2)}) collective-permute-start(f32[264,256]{1,0:T(8,128)S(1)} %get-tuple-element.76.refs_1_), channel_id=1, source_target_pairs={{0,1},{1,2},{2,3},{3,4},{4,5},{5,6},{6,7},{7,8},{8,9},{9,10},{10,1... | collective-permute-start | bytes 811016 | tf_op jit(solution)/shard_map/ppermute | solution.py:423
  138.7 3.8 %collective-permute-done.23.refs_6_ = f32[264,256]{1,0:T(8,128)S(1)} collective-permute-done((f32[264,256]{1,0:T(8,128)S(1)}, f32[264,256]{1,0:T(8,128)S(1)}, u32[]{:S(2)}, u32[]{:S(2)}) %collective-permute-start.23) | collective-permute-done | bytes 270368 | tf_op jit(solution)/shard_map/ppermute | solution.py:425
  148.2 3.1 %collective-permute-done.29 = f32[72,256]{1,0:T(8,128)S(1)} collective-permute-done((f32[72,256]{1,0:T(8,128)S(1)}, f32[72,256]{1,0:T(8,128)S(1)}, u32[]{:S(2)}, u32[]{:S(2)}) %collective-permute-start.29) | collective-permute-done | bytes 73760 | tf_op jit(solution)/shard_map/ppermute | solution.py:408
  156.4 4.0 %collective-permute-start.35 = (f32[256,256]{1,0:T(8,128)S(1)}, f32[256,256]{1,0:T(8,128)S(1)}, u32[]{:S(2)}, u32[]{:S(2)}) collective-permute-start(f32[256,256]{1,0:T(8,128)S(1)} %get-tuple-element.88), channel_id=1, source_target_pairs={{0,3},{1,2},{2,1},{3,0},{4,7},{5,6},{6,5},{7,4},{8,11},{9,10},{10,... | collective-permute-start | bytes 786440 | tf_op jit(solution)/shard_map/ppermute | solution.py:408
  160.4 6.6 %collective-permute-done.33 = f32[256,256]{1,0:T(8,128)S(1)} collective-permute-done((f32[256,256]{1,0:T(8,128)S(1)}, f32[256,256]{1,0:T(8,128)S(1)}, u32[]{:S(2)}, u32[]{:S(2)}) %collective-permute-start.33) | collective-permute-done | bytes 262176 | tf_op jit(solution)/shard_map/ppermute | solution.py:408
  168.1 3.7 %collective-permute-done.35 = f32[256,256]{1,0:T(8,128)S(1)} collective-permute-done((f32[256,256]{1,0:T(8,128)S(1)}, f32[256,256]{1,0:T(8,128)S(1)}, u32[]{:S(2)}, u32[]{:S(2)}) %collective-permute-start.35) | collective-permute-done | bytes 262176 | tf_op jit(solution)/shard_map/ppermute | solution.py:408
  171.8 20.4 %all_to_all.10 = f32[8,32,256]{2,1,0:T(8,128)S(1)} all-to-all(f32[8,32,256]{2,1,0:T(8,128)S(1)} %bitcast.34), channel_id=1, replica_groups={{0,4,8,12,16,20,24,28},{1,5,9,13,17,21,25,29},{2,6,10,14,18,22,26,30},{..., dimensions={0} | all-to-all | bytes 524288 | tf_op jit(solution)/shard_map/all_to_all | solution.py:461
  200.8 8.3 %local.3 = (f32[256,256]{1,0:T(8,128)S(1)}, f32[256,256]{1,0:T(8,128)S(1)}, f32[256,256]{1,0:T(8,128)S(1)}, f32[256,256]{1,0:T(8,128)S(1)}) custom-call(s32[1,1024]{1,0:T(1,128)S(1)} %bitcast.28, f32[256,1024]{1,0:T(8,128)S(1)} %copy-done.30, f32[1024,1024]{1,0:T(8,128)S(1)} %bitcast.32, f32[8,1024]{1,0:T(8,128)S(1)} %get-tuple-element.61.weight_ref, ...), custom_call_target="tpu_custom_call" | custom-call | flops 4294967296 | bytes 8388608 | tf_op jit(solution)/shard_map/local/pallas_call | solution.py:273
  211.1 6.0 %collective-permute-start.25 = (f32[256,256]{1,0:T(8,128)S(1)}, f32[256,256]{1,0:T(8,128)S(1)}, u32[]{:S(2)}, u32[]{:S(2)}) collective-permute-start(f32[256,256]{1,0:T(8,128)S(1)} %get-tuple-element.81.refs_1_), channel_id=1, source_target_pairs={{0,1},{1,2},{2,3},{3,4},{4,5},{5,6},{6,7},{7,8},{8,9},{9,10},{10,1... | collective-permute-start | bytes 786440 | tf_op jit(solution)/shard_map/ppermute | solution.py:423
  225.9 6.0 %collective-permute-start.40 = (f32[64,256]{1,0:T(8,128)S(1)}, f32[64,256]{1,0:T(8,128)S(1)}, u32[]{:S(2)}, u32[]{:S(2)}) collective-permute-start(f32[64,256]{1,0:T(8,128)S(1)} %get-tuple-element.89.refs_20_), channel_id=1, source_target_pairs={{0,1},{1,2},{2,3},{3,4},{4,5},{5,6},{6,7},{7,8},{8,9},{9,10},{10,1... | collective-permute-start | bytes 196616 | tf_op jit(solution)/shard_map/ppermute | solution.py:470
  233.8 4.0 %last.1 = f32[1024,256]{1,0:T(8,128)} custom-call(s32[1,1024]{1,0:T(1,128)S(1)} %bitcast.29, f32[256,256]{1,0:T(8,128)S(1)} %get-tuple-element.80.refs_0_, f32[256,256]{1,0:T(8,128)S(1)} %get-tuple-element.81.refs_1_, f32[256,256]{1,0:T(8,128)S(1)} %get-tuple-element.82.refs_2_, f32[256,256]{1,0:T(8,128)S(1)} %get-tuple-element.83.refs_3_, ...), custom_call_target="tpu_custom_call" | custom-call | flops 1073741824 | bytes 6291456 | tf_op jit(solution)/shard_map/last/pallas_call | solution.py:376
  (177 shorter events, 94.5 us)
Async XLA Ops:
  6.4 12.3 %collective-permute-start.1 = (f32[264,256]{1,0:T(8,128)S(1)}, f32[264,256]{1,0:T(8,128)S(1)}, u32[]{:S(2)}, u32[]{:S(2)}) collective-permute-start(f32[264,256]{1,0:T(8,128)S(1)} %get-tuple-element.55.refs_0_.refs_20_), channel_id=1, source_target_pairs={{1,0},{2,1},{3,2},{4,3},{5,4},{6,5},{7,6},{8,7},{9,8},{10,9},{11,1... | collective-permute-start | bytes 811016 | tf_op jit(solution)/shard_map/ppermute | solution.py:424
  9.1 10.7 %collective-permute-start = (f32[264,256]{1,0:T(8,128)S(1)}, f32[264,256]{1,0:T(8,128)S(1)}, u32[]{:S(2)}, u32[]{:S(2)}) collective-permute-start(f32[264,256]{1,0:T(8,128)S(1)} %get-tuple-element.56.refs_1_.refs_21_), channel_id=1, source_target_pairs={{0,1},{1,2},{2,3},{3,4},{4,5},{5,6},{6,7},{7,8},{8,9},{9,10},{10,1... | collective-permute-start | bytes 811016 | tf_op jit(solution)/shard_map/ppermute | solution.py:423
  37.4 10.8 %collective-permute-start.12 = (f32[256,256]{1,0:T(8,128)S(1)}, f32[256,256]{1,0:T(8,128)S(1)}, u32[]{:S(2)}, u32[]{:S(2)}) collective-permute-start(f32[256,256]{1,0:T(8,128)S(1)} %get-tuple-element.69), channel_id=1, source_target_pairs={{0,2},{1,3},{2,0},{3,1},{4,6},{5,7},{6,4},{7,5},{8,10},{9,11},{10,... | collective-permute-start | bytes 786440 | tf_op jit(solution)/shard_map/ppermute | solution.py:408
  37.5 11.8 %collective-permute-start.13 = (f32[256,256]{1,0:T(8,128)S(1)}, f32[256,256]{1,0:T(8,128)S(1)}, u32[]{:S(2)}, u32[]{:S(2)}) collective-permute-start(f32[256,256]{1,0:T(8,128)S(1)} %get-tuple-element.70), channel_id=1, source_target_pairs={{0,1},{1,0},{2,3},{3,2},{4,5},{5,4},{6,7},{7,6},{8,9},{9,8},{10,11... | collective-permute-start | bytes 786440 | tf_op jit(solution)/shard_map/ppermute | solution.py:408
  37.6 15.4 %collective-permute-start.14 = (f32[256,256]{1,0:T(8,128)S(1)}, f32[256,256]{1,0:T(8,128)S(1)}, u32[]{:S(2)}, u32[]{:S(2)}) collective-permute-start(f32[256,256]{1,0:T(8,128)S(1)} %get-tuple-element.71), channel_id=1, source_target_pairs={{0,3},{1,2},{2,1},{3,0},{4,7},{5,6},{6,5},{7,4},{8,11},{9,10},{10,... | collective-permute-start | bytes 786440 | tf_op jit(solution)/shard_map/ppermute | solution.py:408
  53.7 29.3 %all-to-all-start = ((f32[8,32,256]{2,1,0:T(8,128)}), f32[8,32,256]{2,1,0:T(8,128)}, u32[]{:S(2)}, u32[]{:S(2)}) async-start(f32[8,32,256]{2,1,0:T(8,128)} %bitcast.12), calls=%async_computation | async-start | bytes 524288 | tf_op jit(solution)/shard_map/all_to_all | solution.py:461
  75.0 22.6 %collective-permute-start.5 = (f32[320,256]{1,0:T(8,128)S(1)}, f32[320,256]{1,0:T(8,128)S(1)}, u32[]{:S(2)}, u32[]{:S(2)}) collective-permute-start(f32[320,256]{1,0:T(8,128)S(1)} %get-tuple-element.63.refs_0_.refs_8_), channel_id=1, source_target_pairs={{1,0},{2,1},{3,2},{4,3},{5,4},{6,5},{7,6},{8,7},{9,8},{10,9},{11,1... | collective-permute-start | bytes 983048 | tf_op jit(solution)/shard_map/ppermute | solution.py:424
  76.9 27.7 %collective-permute-start.4 = (f32[320,256]{1,0:T(8,128)S(1)}, f32[320,256]{1,0:T(8,128)S(1)}, u32[]{:S(2)}, u32[]{:S(2)}) collective-permute-start(f32[320,256]{1,0:T(8,128)S(1)} %get-tuple-element.64.refs_1_.refs_9_), channel_id=1, source_target_pairs={{0,1},{1,2},{2,3},{3,4},{4,5},{5,6},{6,7},{7,8},{8,9},{9,10},{10,1... | collective-permute-start | bytes 983048 | tf_op jit(solution)/shard_map/ppermute | solution.py:423
  88.4 16.9 %collective-permute-start.7 = (f32[320,256]{1,0:T(8,128)S(1)}, f32[320,256]{1,0:T(8,128)S(1)}, u32[]{:S(2)}, u32[]{:S(2)}) collective-permute-start(f32[320,256]{1,0:T(8,128)S(1)} %get-tuple-element.65.refs_2_.refs_10_), channel_id=1, source_target_pairs={{32,0},{64,32},{96,64},{128,96},{160,128},{192,160},{224,192},{33,... | collective-permute-start | bytes 983048 | tf_op jit(solution)/shard_map/ppermute | solution.py:426
  91.4 13.9 %collective-permute-start.6 = (f32[320,256]{1,0:T(8,128)S(1)}, f32[320,256]{1,0:T(8,128)S(1)}, u32[]{:S(2)}, u32[]{:S(2)}) collective-permute-start(f32[320,256]{1,0:T(8,128)S(1)} %get-tuple-element.66.refs_3_.refs_11_), channel_id=1, source_target_pairs={{0,32},{32,64},{64,96},{96,128},{128,160},{160,192},{192,224},{1,3... | collective-permute-start | bytes 983048 | tf_op jit(solution)/shard_map/ppermute | solution.py:425
  95.6 9.6 %collective-permute-start.20 = (f32[64,256]{1,0:T(8,128)S(1)}, f32[64,256]{1,0:T(8,128)S(1)}, u32[]{:S(2)}, u32[]{:S(2)}) collective-permute-start(f32[64,256]{1,0:T(8,128)S(1)} %get-tuple-element.72.refs_24_), channel_id=1, source_target_pairs={{1,0},{2,1},{3,2},{4,3},{5,4},{6,5},{7,6},{8,7},{9,8},{10,9},{11,1... | collective-permute-start | bytes 196616 | tf_op jit(solution)/shard_map/ppermute | solution.py:471
  124.5 12.7 %collective-permute-start.22 = (f32[264,256]{1,0:T(8,128)S(1)}, f32[264,256]{1,0:T(8,128)S(1)}, u32[]{:S(2)}, u32[]{:S(2)}) collective-permute-start(f32[264,256]{1,0:T(8,128)S(1)} %get-tuple-element.75.refs_0_), channel_id=1, source_target_pairs={{1,0},{2,1},{3,2},{4,3},{5,4},{6,5},{7,6},{8,7},{9,8},{10,9},{11,1... | collective-permute-start | bytes 811016 | tf_op jit(solution)/shard_map/ppermute | solution.py:424
  126.4 11.2 %collective-permute-start.21 = (f32[264,256]{1,0:T(8,128)S(1)}, f32[264,256]{1,0:T(8,128)S(1)}, u32[]{:S(2)}, u32[]{:S(2)}) collective-permute-start(f32[264,256]{1,0:T(8,128)S(1)} %get-tuple-element.76.refs_1_), channel_id=1, source_target_pairs={{0,1},{1,2},{2,3},{3,4},{4,5},{5,6},{6,7},{7,8},{8,9},{9,10},{10,1... | collective-permute-start | bytes 811016 | tf_op jit(solution)/shard_map/ppermute | solution.py:423
  156.2 10.8 %collective-permute-start.33 = (f32[256,256]{1,0:T(8,128)S(1)}, f32[256,256]{1,0:T(8,128)S(1)}, u32[]{:S(2)}, u32[]{:S(2)}) collective-permute-start(f32[256,256]{1,0:T(8,128)S(1)} %get-tuple-element.86), channel_id=1, source_target_pairs={{0,2},{1,3},{2,0},{3,1},{4,6},{5,7},{6,4},{7,5},{8,10},{9,11},{10,... | collective-permute-start | bytes 786440 | tf_op jit(solution)/shard_map/ppermute | solution.py:408
  156.3 11.8 %collective-permute-start.34 = (f32[256,256]{1,0:T(8,128)S(1)}, f32[256,256]{1,0:T(8,128)S(1)}, u32[]{:S(2)}, u32[]{:S(2)}) collective-permute-start(f32[256,256]{1,0:T(8,128)S(1)} %get-tuple-element.87), channel_id=1, source_target_pairs={{0,1},{1,0},{2,3},{3,2},{4,5},{5,4},{6,7},{7,6},{8,9},{9,8},{10,11... | collective-permute-start | bytes 786440 | tf_op jit(solution)/shard_map/ppermute | solution.py:408
  156.4 15.4 %collective-permute-start.35 = (f32[256,256]{1,0:T(8,128)S(1)}, f32[256,256]{1,0:T(8,128)S(1)}, u32[]{:S(2)}, u32[]{:S(2)}) collective-permute-start(f32[256,256]{1,0:T(8,128)S(1)} %get-tuple-element.88), channel_id=1, source_target_pairs={{0,3},{1,2},{2,1},{3,0},{4,7},{5,6},{6,5},{7,4},{8,11},{9,10},{10,... | collective-permute-start | bytes 786440 | tf_op jit(solution)/shard_map/ppermute | solution.py:408
  192.3 24.9 %collective-permute-start.38 = (f32[32,256]{1,0:T(8,128)S(1)}, f32[32,256]{1,0:T(8,128)S(1)}, u32[]{:S(2)}, u32[]{:S(2)}) collective-permute-start(f32[32,256]{1,0:T(8,128)S(1)} %reduce_sum.19), channel_id=1, source_target_pairs={{0,192},{32,224},{64,128},{96,160},{128,64},{160,96},{192,0},{224,... | collective-permute-start | bytes 98312 | tf_op jit(solution)/shard_map/ppermute | solution.py:408
  193.7 25.4 %collective-permute-start.37 = (f32[32,256]{1,0:T(8,128)S(1)}, f32[32,256]{1,0:T(8,128)S(1)}, u32[]{:S(2)}, u32[]{:S(2)}) collective-permute-start(f32[32,256]{1,0:T(8,128)S(1)} %reduce_sum.19), channel_id=1, source_target_pairs={{0,128},{32,160},{64,192},{96,224},{128,0},{160,32},{192,64},{224,... | collective-permute-start | bytes 98312 | tf_op jit(solution)/shard_map/ppermute | solution.py:408
  195.7 25.8 %collective-permute-start.36 = (f32[32,256]{1,0:T(8,128)S(1)}, f32[32,256]{1,0:T(8,128)S(1)}, u32[]{:S(2)}, u32[]{:S(2)}) collective-permute-start(f32[32,256]{1,0:T(8,128)S(1)} %reduce_sum.19), channel_id=1, source_target_pairs={{0,64},{32,96},{64,0},{96,32},{128,192},{160,224},{192,128},{224,1... | collective-permute-start | bytes 98312 | tf_op jit(solution)/shard_map/ppermute | solution.py:408
  209.2 16.7 %collective-permute-start.26 = (f32[256,256]{1,0:T(8,128)S(1)}, f32[256,256]{1,0:T(8,128)S(1)}, u32[]{:S(2)}, u32[]{:S(2)}) collective-permute-start(f32[256,256]{1,0:T(8,128)S(1)} %get-tuple-element.80.refs_0_), channel_id=1, source_target_pairs={{1,0},{2,1},{3,2},{4,3},{5,4},{6,5},{7,6},{8,7},{9,8},{10,9},{11,1... | collective-permute-start | bytes 786440 | tf_op jit(solution)/shard_map/ppermute | solution.py:424
  211.1 20.8 %collective-permute-start.25 = (f32[256,256]{1,0:T(8,128)S(1)}, f32[256,256]{1,0:T(8,128)S(1)}, u32[]{:S(2)}, u32[]{:S(2)}) collective-permute-start(f32[256,256]{1,0:T(8,128)S(1)} %get-tuple-element.81.refs_1_), channel_id=1, source_target_pairs={{0,1},{1,2},{2,3},{3,4},{4,5},{5,6},{6,7},{7,8},{8,9},{9,10},{10,1... | collective-permute-start | bytes 786440 | tf_op jit(solution)/shard_map/ppermute | solution.py:423
  217.2 14.8 %collective-permute-start.28 = (f32[256,256]{1,0:T(8,128)S(1)}, f32[256,256]{1,0:T(8,128)S(1)}, u32[]{:S(2)}, u32[]{:S(2)}) collective-permute-start(f32[256,256]{1,0:T(8,128)S(1)} %get-tuple-element.82.refs_2_), channel_id=1, source_target_pairs={{32,0},{64,32},{96,64},{128,96},{160,128},{192,160},{224,192},{33,... | collective-permute-start | bytes 786440 | tf_op jit(solution)/shard_map/ppermute | solution.py:426
  219.1 12.8 %collective-permute-start.27 = (f32[256,256]{1,0:T(8,128)S(1)}, f32[256,256]{1,0:T(8,128)S(1)}, u32[]{:S(2)}, u32[]{:S(2)}) collective-permute-start(f32[256,256]{1,0:T(8,128)S(1)} %get-tuple-element.83.refs_3_), channel_id=1, source_target_pairs={{0,32},{32,64},{64,96},{96,128},{128,160},{160,192},{192,224},{1,3... | collective-permute-start | bytes 786440 | tf_op jit(solution)/shard_map/ppermute | solution.py:425
  223.9 8.4 %collective-permute-start.41 = (f32[64,256]{1,0:T(8,128)S(1)}, f32[64,256]{1,0:T(8,128)S(1)}, u32[]{:S(2)}, u32[]{:S(2)}) collective-permute-start(f32[64,256]{1,0:T(8,128)S(1)} %get-tuple-element.89.refs_20_), channel_id=1, source_target_pairs={{1,0},{2,1},{3,2},{4,3},{5,4},{6,5},{7,6},{8,7},{9,8},{10,9},{11,1... | collective-permute-start | bytes 196616 | tf_op jit(solution)/shard_map/ppermute | solution.py:471
  (57 other events, 581.2 us)

commit v2 on v0

v2 whole, which is shorter than its diff:
```python
import functools

import jax
import jax.numpy as jnp
from jax import lax
from jax.experimental import pallas as pl
from jax.experimental.pallas import tpu as pltpu
from jax.sharding import PartitionSpec as P

INTERFACE = 1024
FACE_ROWS = 256
COLUMNS = 256
OWNED = 32
LOCAL = 64
SWEEPS = 2
X_SIZE = 4
TILE = 256
FACES = 4
TERM_ROWS = LOCAL + 8
MULT_ROWS = COLUMNS + 8
LIFT_ROWS = COLUMNS + LOCAL

NN = (((1,), (0,)), ((), ()))
NT = (((1,), (1,)), ((), ()))
TN = (((0,), (0,)), ((), ()))

VMEM = pl.BlockSpec(memory_space=pltpu.VMEM)
SMEM = pl.BlockSpec(memory_space=pltpu.SMEM)
ANY = pl.BlockSpec(memory_space=pl.ANY)
HBM = "hbm"


def shaped(*shape, dtype=jnp.float32):
    return jax.ShapeDtypeStruct(shape, dtype)


def in_hbm(*shape, dtype=jnp.float32):
    return pltpu.HBM(shape, dtype)


def params():
    return pltpu.CompilerParams(vmem_limit_bytes=20 << 20)


def cost(flops, moved):
    return pl.CostEstimate(flops=flops, bytes_accessed=moved, transcendentals=0)


def call(kernel, name, out_shape, flops, moved, in_specs, scratch=()):
    outs = [VMEM if isinstance(o, jax.ShapeDtypeStruct) else ANY for o in out_shape]
    function = pl.pallas_call(
        kernel,
        out_shape=out_shape,
        in_specs=[ANY if spec is HBM else spec for spec in in_specs],
        out_specs=outs,
        scratch_shapes=scratch,
        compiler_params=params(),
        cost_estimate=cost(flops, moved),
        name=name,
    )

    def run(*values):
        values = [
            pltpu.with_memory_space_constraint(value, pltpu.HBM) if spec is HBM else value
            for value, spec in zip(values, in_specs)
        ]
        return function(*values)

    return run


def split(value):
    high = value.astype(jnp.bfloat16)
    low = (value - high.astype(jnp.float32)).astype(jnp.bfloat16)
    return high, low


def mul(left, right, dims):
    return lax.dot_general(left, right, dims, preferred_element_type=jnp.float32)


def mul3(left, right, dims):
    left_high, left_low = left
    right_high, right_low = right
    return (
        mul(left_high, right_low, dims)
        + mul(left_low, right_high, dims)
        + mul(left_high, right_high, dims)
    )


def folded(value):
    return value[:COLUMNS] + value[COLUMNS:]


def tile_at(t):
    return pl.ds(pl.multiple_of(t * TILE, TILE), TILE)


def face_at(p):
    return slice(p * FACE_ROWS, (p + 1) * FACE_ROWS)


def put(ref, at, value):
    ref[:COLUMNS, at], ref[COLUMNS:, at] = split(value)


PAIR = pltpu.VMEM((2 * COLUMNS, INTERFACE), jnp.bfloat16)
STEPS = INTERFACE // TILE
BASIS_AT = 2 * COLUMNS
MULT_AT = BASIS_AT + 2 * LOCAL


def fetched(source, target, sem):
    copy = pltpu.make_async_copy(source, target, sem)
    copy.start()
    return copy


def pack_kernel(
    odd_ref, slots_in, objective_in, basis_in, mult_in, basis_ref, onehot_ref, *rest
):
    outs = rest[:FACES]
    slots, staged, basis, mult, sems, left = rest[FACES:]
    slots_copy = fetched(slots_in, slots, sems.at[STEPS])
    small = [
        fetched(basis_in, basis, sems.at[STEPS + 1]),
        fetched(mult_in, mult, sems.at[STEPS + 2]),
    ]
    copies = [
        fetched(objective_in.at[t * TILE : (t + 1) * TILE], staged.at[t], sems.at[t])
        for t in range(STEPS)
    ]
    slots_copy.wait()
    odd_dev, odd_grp = odd_ref[0] == 1, odd_ref[1] == 1
    lines = [slots[p : p + 1] for p in range(FACES)]
    lines = [
        jnp.where(odd_dev, lines[0], lines[1]),
        jnp.where(odd_dev, lines[1], lines[0]),
        jnp.where(odd_grp, lines[2], lines[3]),
        jnp.where(odd_grp, lines[3], lines[2]),
    ]
    for p in range(FACES):
        rows = lax.broadcasted_iota(jnp.int32, (INTERFACE, FACE_ROWS), 0)
        onehot_ref[:, face_at(p)] = (
            (rows == lines[p]).astype(jnp.float32).astype(jnp.bfloat16)
        )
    for copy in small:
        copy.wait()
    left[BASIS_AT : BASIS_AT + LOCAL], left[BASIS_AT + LOCAL : MULT_AT] = split(basis[...])
    left[MULT_AT:] = jnp.broadcast_to(mult[...].astype(jnp.float32), (16, INTERFACE)).astype(
        jnp.bfloat16
    )
    for t in range(STEPS):
        copies[t].wait()
        at = slice(t * TILE, (t + 1) * TILE)
        left[:COLUMNS, at], left[COLUMNS:BASIS_AT, at] = split(staged[t].T)
    for p in range(FACES):
        out = mul(left[...], onehot_ref[:, face_at(p)], NN)
        outs[p][:COLUMNS] = folded(out[:BASIS_AT])
        outs[p][COLUMNS:] = out[MULT_AT : MULT_AT + 8]
        basis_ref[:, face_at(p)] = out[BASIS_AT : BASIS_AT + LOCAL] + out[BASIS_AT + LOCAL : MULT_AT]


def pack_call(odd, slots, objective, basis, mult):
    return call(
        pack_kernel,
        "pack",
        [shaped(LOCAL, INTERFACE), shaped(INTERFACE, INTERFACE, dtype=jnp.bfloat16)]
        + [shaped(MULT_ROWS, FACE_ROWS)] * FACES,
        2 << 30,
        4 << 20,
        [SMEM] + [HBM] * 4,
        scratch=[
            pltpu.VMEM((FACES, FACE_ROWS), jnp.int32),
            pltpu.VMEM((STEPS, TILE, COLUMNS), jnp.float32),
            pltpu.VMEM((LOCAL, INTERFACE), jnp.float32),
            pltpu.VMEM((1, INTERFACE), jnp.int32),
            pltpu.SemaphoreType.DMA((STEPS + 3,)),
            pltpu.VMEM((MULT_AT + 16, INTERFACE), jnp.bfloat16),
        ],
    )(odd, slots, objective, basis, mult)


def tile_kernel(tile_in, high_out, low_out, staged, sems, high, low, out_sems):
    copies = [
        fetched(tile_in.at[:, t * TILE : (t + 1) * TILE], staged.at[t], sems.at[t])
        for t in range(STEPS)
    ]
    outs = []
    for t in range(STEPS):
        copies[t].wait()
        at = slice(t * TILE, (t + 1) * TILE)
        high[at], low[at] = split(staged[t].T)
        outs.append(fetched(high.at[at], high_out.at[at], out_sems.at[0, t]))
        outs.append(fetched(low.at[at], low_out.at[at], out_sems.at[1, t]))
    for copy in outs:
        copy.wait()


def tile_call(tile):
    rows, width = tile.shape
    half = pltpu.VMEM((width, rows), jnp.bfloat16)
    return call(
        tile_kernel,
        "tile",
        [in_hbm(width, rows, dtype=jnp.bfloat16)] * 2,
        1 << 20,
        4 << 20,
        [HBM],
        scratch=[
            pltpu.VMEM((STEPS, rows, TILE), jnp.float32),
            pltpu.SemaphoreType.DMA((STEPS,)),
            half,
            half,
            pltpu.SemaphoreType.DMA((2, STEPS)),
        ],
    )(tile)


def join_kernel(*refs):
    rows = refs[0].shape[0]
    for i, ref in enumerate(refs[:-1]):
        refs[-1][i * rows : (i + 1) * rows] = ref[...]


def join_call(parts):
    rows, width = parts[0].shape
    (out,) = call(
        join_kernel,
        "join",
        [shaped(len(parts) * rows, width)],
        1 << 20,
        1 << 19,
        [VMEM] * len(parts),
    )(*parts)
    return out


def weigh_kernel(first, *refs):
    here, there = refs[:FACES], refs[FACES : 2 * FACES]
    basis_ref, map_ref = refs[2 * FACES : 2 * FACES + 2]
    weighted_out, terms_ref = refs[2 * FACES + 2 : 2 * FACES + 4]
    if first:
        weight_ref, lift_out, weighted_ref, sems, lift_ref = refs[2 * FACES + 4 :]
    else:
        weighted_ref, sems = refs[2 * FACES + 4 :]
    terms = jnp.zeros((LOCAL, COLUMNS), jnp.float32)
    copies = []
    for p in range(FACES):
        mine = here[p][COLUMNS : COLUMNS + 1]
        total = mine + there[p][COLUMNS : COLUMNS + 1]
        weight = jnp.where(total > 0, mine / jnp.maximum(total, 1.0), 0.0)
        weighted = weight * (here[p][:COLUMNS] + there[p][:COLUMNS])
        high, low = split(weighted)
        weighted_ref[:COLUMNS, face_at(p)] = high
        weighted_ref[COLUMNS:, face_at(p)] = low
        at = (slice(None), face_at(p))
        copies.append(fetched(weighted_ref.at[at], weighted_out.at[at], sems.at[p]))
        basis = basis_ref[:, face_at(p)]
        terms = terms + mul3(split(basis), (high, low), NT)
        if first:
            weight_ref[:, face_at(p)] = jnp.broadcast_to(weight, (8, FACE_ROWS))
            lift_ref[:, face_at(p)] = basis * weight
            copies.append(fetched(lift_ref.at[at], lift_out.at[at], sems.at[FACES + p]))
    terms_ref[:LOCAL] = terms
    terms_ref[LOCAL:] = map_ref[...]
    for copy in copies:
        copy.wait()


def weigh_call(here, there, basis, map_row, first):
    out = [in_hbm(2 * COLUMNS, INTERFACE, dtype=jnp.bfloat16), shaped(TERM_ROWS, COLUMNS)]
    scratch = [PAIR, pltpu.SemaphoreType.DMA((2 * FACES,))]
    if first:
        out += [shaped(8, INTERFACE), in_hbm(LOCAL, INTERFACE)]
        scratch += [pltpu.VMEM((LOCAL, INTERFACE), jnp.float32)]
    return call(
        functools.partial(weigh_kernel, first),
        "weigh",
        out,
        100 << 20,
        2 << 20,
        [VMEM] * (2 * FACES + 2),
        scratch=scratch,
    )(*here, *there, basis, map_row)


def coarse_kernel(n_grp, nz, nx, x_ref, half_ref, other_ref, high_in, low_in, *rest):
    outs, (scratch, right, high_ref, low_ref, sems) = rest[:nx], rest[nx:]
    high_copy = fetched(high_in, high_ref, sems.at[0])
    low_copy = fetched(low_in, low_ref, sems.at[1])
    dofs = n_grp * OWNED
    column = jnp.zeros((dofs, 2 * COLUMNS), jnp.float32)
    rows = lax.broadcasted_iota(jnp.int32, (dofs, LOCAL), 0).astype(jnp.float32)
    for ref in (half_ref, other_ref):
        for j in range(n_grp // 2):
            at = j * TERM_ROWS
            names = ref[at + LOCAL : at + LOCAL + 1, :LOCAL]
            onehot = (rows == names).astype(jnp.float32).astype(jnp.bfloat16)
            both = jnp.concatenate(split(ref[at : at + LOCAL, :]), axis=1)
            column = column + mul(onehot, both, NN)
    right[:, :COLUMNS], right[:, COLUMNS:] = split(column[:, :COLUMNS] + column[:, COLUMNS:])
    chunk = nx * OWNED
    per_step = TILE // chunk
    x_pos = x_ref[0]
    high_copy.wait()
    low_copy.wait()

    @pl.loop(0, nz // per_step)
    def _(step):
        at = tile_at(step)
        out = mul(high_ref[at, :], right[...], NN)
        scratch[...] = out[:, :COLUMNS] + (
            out[:, COLUMNS:] + mul(low_ref[at, :], right[:, :COLUMNS], NN)
        )
        for i in range(per_step):
            for k in range(nx):
                start = pl.multiple_of(i * chunk + (x_pos ^ k) * OWNED, OWNED)
                to = pl.multiple_of((step * per_step + i) * OWNED, OWNED)
                outs[k][pl.ds(to, OWNED), :] = scratch[pl.ds(start, OWNED), :]


def coarse_call(x_pos, half, other, high, low, n_grp, nz, nx):
    return call(
        functools.partial(coarse_kernel, n_grp, nz, nx),
        "coarse",
        [shaped(nz * OWNED, COLUMNS)] * nx,
        600 << 20,
        3 << 20,
        [SMEM] + [VMEM] * 2 + [HBM] * 2,
        scratch=[
            pltpu.VMEM((TILE, COLUMNS), jnp.float32),
            pltpu.VMEM((n_grp * OWNED, 2 * COLUMNS), jnp.bfloat16),
            pltpu.VMEM(high.shape, high.dtype),
            pltpu.VMEM(low.shape, low.dtype),
            pltpu.SemaphoreType.DMA((2,)),
        ],
    )(x_pos, half, other, high, low)


def add_kernel(*refs):
    count = len(refs) - 3
    out_ref, staged, sem = refs[count:]
    value = refs[0][...]
    for ref in refs[1:count]:
        value = value + ref[...]
    staged[...] = value
    fetched(staged, out_ref, sem).wait()


def add_call(*values):
    shape = values[0].shape
    (out,) = call(
        add_kernel,
        "add",
        [in_hbm(*shape)],
        1 << 20,
        1 << 20,
        [VMEM] * len(values),
        scratch=[pltpu.VMEM(shape, jnp.float32), pltpu.SemaphoreType.DMA],
    )(*values)
    return out


def sum_kernel(count, value_ref, out_ref):
    value = value_ref[:OWNED]
    for i in range(1, count):
        value = value + value_ref[i * OWNED : (i + 1) * OWNED]
    out_ref[...] = value


def sum_call(value):
    (out,) = call(
        functools.partial(sum_kernel, value.shape[0] // OWNED),
        "sum",
        [shaped(OWNED, COLUMNS)],
        1 << 20,
        1 << 18,
        [VMEM],
    )(value)
    return out


def fetch_kernel(n_grp, at_ref, map_ref, names_ref, half_ref, other_ref, *outs):
    dofs = n_grp * OWNED
    index = lax.broadcasted_iota(jnp.int32, (dofs, LOCAL), 0)
    block, inside = index // OWNED, index % OWNED
    block = jnp.where(block < n_grp // 2, 2 * block, 2 * block - n_grp + 1)
    ids = ((block ^ at_ref[0]) * OWNED + inside).astype(jnp.float32)
    value = jnp.concatenate([half_ref[...], other_ref[...]], axis=0)
    both = jnp.concatenate(split(value), axis=1)
    start = pl.multiple_of(at_ref[1] * TERM_ROWS + LOCAL, 8)
    names = [
        map_ref[:1, :LOCAL],
        names_ref[LOCAL : LOCAL + 1, :LOCAL],
        names_ref[pl.ds(start, 8), :][:1, :LOCAL],
    ]
    for name, out in zip(names, outs):
        onehot = (ids == name).astype(jnp.float32).astype(jnp.bfloat16)
        pair = mul(onehot, both, TN)
        out[...] = pair[:, :COLUMNS] + pair[:, COLUMNS:]


def fetch_call(at, map_row, names, half, other, n_grp):
    return call(
        functools.partial(fetch_kernel, n_grp),
        "fetch",
        [shaped(LOCAL, COLUMNS)] * 3,
        100 << 20,
        1 << 20,
        [SMEM] + [VMEM] * 4,
    )(at, map_row, names, half, other)


def matrix_copy(matrix_in, matrix, sems, t):
    at = tile_at(t)
    return pltpu.make_async_copy(matrix_in.at[:, at], matrix.at[:, at], sems.at[t])


def start_matrix(matrix_in, matrix, sems):
    for t in range(STEPS):
        matrix_copy(matrix_in, matrix, sems, t).start()


def apply(onehot_ref, matrix_in, matrix, sems, value_ref, rows_ref, result_ref):
    @pl.loop(0, STEPS)
    def _(t):
        put(rows_ref, tile_at(t), folded(mul(value_ref[...], onehot_ref[tile_at(t), :], NT)))

    @pl.loop(0, STEPS)
    def _(t):
        matrix_copy(matrix_in, matrix, sems, t).wait()
        high, low = split(matrix[:, tile_at(t)])
        out = folded(mul(rows_ref[...], high, NN)) + mul(rows_ref[:COLUMNS], low, NN)
        put(result_ref, tile_at(t), out)


MATRIX = [
    pltpu.VMEM((INTERFACE, INTERFACE), jnp.float32),
    pltpu.SemaphoreType.DMA((STEPS,)),
]


def local_kernel(first, onehot_ref, weighted_in, matrix_in, weight_ref, lift_in, *rest):
    outs = rest[:FACES]
    matrix, matrix_sems, weighted, lift, sems, rows, result, staged = rest[FACES:]
    weighted_copy = fetched(weighted_in, weighted, sems.at[0])
    start_matrix(matrix_in, matrix, matrix_sems)
    lift_copy = fetched(lift_in, lift, sems.at[1])
    weighted_copy.wait()
    apply(onehot_ref, matrix_in, matrix, matrix_sems, weighted, rows, result)
    lift_copy.wait()
    copies = []
    for p in range(FACES):
        out = folded(mul(result[...], onehot_ref[:, face_at(p)], NN))
        staged[p, :COLUMNS] = weight_ref[:1, face_at(p)] * out
        if first:
            staged[p, COLUMNS:] = lift[:, face_at(p)]
        copies.append(fetched(staged.at[p], outs[p], sems.at[2 + p]))
    for copy in copies:
        copy.wait()


def local_call(onehot, weighted, matrix, weight, lift, first):
    rows = LIFT_ROWS if first else COLUMNS
    return call(
        functools.partial(local_kernel, first),
        "local",
        [in_hbm(rows, FACE_ROWS)] * FACES,
        6 << 30,
        8 << 20,
        [VMEM, HBM, HBM, VMEM, HBM],
        scratch=MATRIX
        + [PAIR, pltpu.VMEM((LOCAL, INTERFACE), jnp.float32), pltpu.SemaphoreType.DMA((6,))]
        + [PAIR] * 2
        + [pltpu.VMEM((FACES, rows, FACE_ROWS), jnp.float32)],
    )(onehot, weighted, matrix, weight, lift)


BODY = slice(0, COLUMNS)
LIFT = slice(COLUMNS, LIFT_ROWS)


def adjoint_face(p, near, far, lift_near, lift_far, own, around):
    change = mul3(own, split(lift_near), TN)
    change = change + mul3(split(around[p][...]), split(lift_far), TN)
    return near + far + change


def middle_kernel(onehot_ref, *refs):
    groups = [refs[i * FACES : (i + 1) * FACES] for i in range(4)]
    near_in, far_in, around, gradient_in = groups
    own_ref, matrix_in, adjoint_out = refs[4 * FACES : 4 * FACES + 3]
    outs = refs[4 * FACES + 3 : 5 * FACES + 3]
    matrix, matrix_sems, near, far, gradient, sems, kept, value, rows, result = refs[
        5 * FACES + 3 :
    ]
    copies = [
        (fetched(near_in[p], near.at[p], sems.at[0, p]), fetched(far_in[p], far.at[p], sems.at[1, p]))
        for p in range(FACES)
    ]
    start_matrix(matrix_in, matrix, matrix_sems)
    gradient_copies = [
        fetched(gradient_in[p], gradient.at[p], sems.at[2, p]) for p in range(FACES)
    ]
    own = split(own_ref[...])
    kept_copies = []
    for p in range(FACES):
        for copy in copies[p]:
            copy.wait()
        adjoint = adjoint_face(
            p, near[p, BODY], far[p, BODY], near[p, LIFT], far[p, LIFT], own, around
        )
        kept[p] = adjoint
        kept_copies.append(fetched(kept.at[p], adjoint_out.at[p], sems.at[3, p]))
        put(value, face_at(p), adjoint)
    apply(onehot_ref, matrix_in, matrix, matrix_sems, value, rows, result)
    for p in range(FACES):
        gradient_copies[p].wait()
        out = folded(mul(result[...], onehot_ref[:, face_at(p)], NN))
        outs[p][:COLUMNS] = gradient[p, BODY] - out
        outs[p][COLUMNS:] = gradient[p, COLUMNS:]
    for copy in kept_copies:
        copy.wait()


def middle_call(onehot, near, far, around, gradient, own, matrix):
    lifted = pltpu.VMEM((FACES, LIFT_ROWS, FACE_ROWS), jnp.float32)
    return call(
        middle_kernel,
        "middle",
        [in_hbm(FACES, COLUMNS, FACE_ROWS)] + [shaped(MULT_ROWS, FACE_ROWS)] * FACES,
        6 << 30,
        12 << 20,
        [VMEM] + [HBM] * (2 * FACES) + [VMEM] * FACES + [HBM] * FACES + [VMEM, HBM],
        scratch=MATRIX
        + [
            lifted,
            lifted,
            pltpu.VMEM((FACES, MULT_ROWS, FACE_ROWS), jnp.float32),
            pltpu.SemaphoreType.DMA((4, FACES)),
            pltpu.VMEM((FACES, COLUMNS, FACE_ROWS), jnp.float32),
        ]
        + [PAIR] * 3,
    )(onehot, *near, *far, *around, *gradient, own, matrix)


def last_kernel(onehot_ref, *refs):
    groups = [refs[i * FACES : (i + 1) * FACES] for i in range(5)]
    near_in, far_in, lift_near_in, lift_far_in, around = groups
    own_ref, adjoint_in, out_ref = refs[5 * FACES : 5 * FACES + 3]
    near, far, adjoint, lift_near, lift_far, sems, value, staged, out_sems = refs[5 * FACES + 3 :]
    copies = []
    for p in range(FACES):
        pieces = (
            (near_in[p], near.at[p]),
            (far_in[p], far.at[p]),
            (adjoint_in.at[p], adjoint.at[p]),
            (lift_near_in[p].at[LIFT], lift_near.at[p]),
            (lift_far_in[p].at[LIFT], lift_far.at[p]),
        )
        copies.append(
            [fetched(source, to, sems.at[i, p]) for i, (source, to) in enumerate(pieces)]
        )
    own = split(own_ref[...])
    for p in range(FACES):
        for copy in copies[p]:
            copy.wait()
        out = adjoint_face(p, near[p], far[p], lift_near[p], lift_far[p], own, around)
        put(value, face_at(p), adjoint[p] + out)
    out_copies = []
    for t in range(STEPS):
        at = slice(t * TILE, (t + 1) * TILE)
        out = mul(onehot_ref[at, :], value[...], NT)
        staged[t] = out[:, :COLUMNS] + out[:, COLUMNS:]
        out_copies.append(fetched(staged.at[t], out_ref.at[at], out_sems.at[t]))
    for copy in out_copies:
        copy.wait()


def last_call(onehot, near, far, lift_near, lift_far, around, own, adjoint):
    face_block = pltpu.VMEM((FACES, COLUMNS, FACE_ROWS), jnp.float32)
    lift_block = pltpu.VMEM((FACES, LOCAL, FACE_ROWS), jnp.float32)
    (out,) = call(
        last_kernel,
        "last",
        [in_hbm(INTERFACE, COLUMNS)],
        1 << 30,
        6 << 20,
        [VMEM] + [HBM] * (4 * FACES) + [VMEM] * FACES + [VMEM, HBM],
        scratch=[
            face_block,
            face_block,
            face_block,
            lift_block,
            lift_block,
            pltpu.SemaphoreType.DMA((5, FACES)),
            PAIR,
            pltpu.VMEM((STEPS, TILE, COLUMNS), jnp.float32),
            pltpu.SemaphoreType.DMA((STEPS,)),
        ],
    )(onehot, *near, *far, *lift_near, *lift_far, *around, own, adjoint)
    return out


def on_device(
    objective, schur, local_inverse, coarse_basis, coarse_inverse, stiffness, face_rows, coarse_map
):
    n_grp, n_dev = lax.axis_size("grp"), lax.axis_size("dev")
    nx = X_SIZE
    nz = n_dev // nx
    grp = lax.axis_index("grp").astype(jnp.int32)
    dev = lax.axis_index("dev").astype(jnp.int32)
    x_pos = (dev % nx).reshape(1)
    z_groups = [[z * nx + x for z in range(nz)] for x in range(nx)]
    odd = jnp.stack([dev % 2, grp % 2])
    beyond = jnp.where(grp % 2 == 1, grp + 1, grp - 1)
    beyond = jnp.where((beyond < 0) | (beyond >= n_grp), grp ^ 1, beyond)
    at = jnp.stack([grp, (grp ^ beyond) // 2])

    def swap(value, axis, k):
        size = lax.axis_size(axis)
        return lax.ppermute(value, axis, [(i, i ^ k) for i in range(size)])

    def swap_next(value, axis):
        lower = range(1, lax.axis_size(axis) - 1, 2)
        return lax.ppermute(
            value, axis, [(i, i + 1) for i in lower] + [(i + 1, i) for i in lower]
        )

    def group_gather(value):
        parts = [value] + [swap(value, "grp", k) for k in range(2, n_grp, 2)]
        half = join_call(parts)
        return half, swap(half, "grp", 1)

    def exchange(faces):
        return [
            swap(faces[0], "dev", 1),
            swap_next(faces[1], "dev"),
            swap(faces[2], "grp", 1),
            swap_next(faces[3], "grp"),
        ]

    local_map = coarse_map[0, 0]
    basis, onehot, *gradient = pack_call(
        odd, face_rows[0, 0], objective[0, 0], coarse_basis[0, 0], stiffness[0]
    )
    tile, *gradient = lax.optimization_barrier((coarse_inverse, *gradient))
    high, low = tile_call(tile.reshape(-1, tile.shape[3]))
    arrived = exchange(gradient)

    map_row = jnp.zeros((8, COLUMNS), jnp.float32)
    map_row = map_row.at[0, :LOCAL].set(local_map.astype(jnp.float32))
    high, low, map_row = lax.optimization_barrier((high, low, map_row))

    weighted, terms, weight, lift = weigh_call(gradient, arrived, basis, map_row, True)
    names = None
    adjoint = None
    lift_near = lift_far = None
    for sweep in range(SWEEPS):
        first = sweep == 0
        half, other = group_gather(terms)
        if first:
            names = other
        blocks = coarse_call(x_pos, half, other, high, low, n_grp, nz, nx)
        sent = [swap(blocks[k], "dev", k) for k in (2, 1, 3)]
        near = local_call(onehot, weighted, local_inverse[0, 0], weight, lift, first)
        mine, *near = lax.optimization_barrier((blocks[0], *near))
        total = add_call(mine, *sent)
        total = lax.all_to_all(
            total.reshape(nz, OWNED, COLUMNS), "dev", 0, 0, axis_index_groups=z_groups, tiled=True
        )
        far = exchange(near)
        total, *far = lax.optimization_barrier((total, *far))
        owned = sum_call(total.reshape(nz * OWNED, COLUMNS))
        if first:
            lift_near, lift_far = near, far
        own, core, next_core = fetch_call(at, map_row, names, *group_gather(owned), n_grp)
        around = [swap(own, "dev", 1), swap_next(own, "dev"), core, next_core]
        if first:
            adjoint, *remain = middle_call(onehot, near, far, around, gradient, own, schur[0, 0])
            weighted, terms = weigh_call(remain, exchange(remain), basis, map_row, False)
        else:
            out = last_call(onehot, near, far, lift_near, lift_far, around, own, adjoint)
    return out[None, None]


def solution(mesh):
    return jax.shard_map(
        on_device,
        mesh=mesh,
        in_specs=(
            P("grp", "dev", None, None),
            P("grp", "dev", None, None),
            P("grp", "dev", None, None),
            P("grp", "dev", None, None),
            P(None, "dev", None, "grp"),
            P("grp", "dev", None),
            P("grp", "dev", None, None),
            P("grp", "dev", None),
        ),
        out_specs=P("grp", "dev", None, None),
        check_vma=False,
    )
```

time: 767 us -> 194 us (0.25)
  waiting for transfers between devices: 553 us -> 58.6 us
  local copies, waits for them, and re-layouts: 72.2 us -> 1.51 us
  Pallas kernels: 0 us -> 50.7 us
  matrix products: 34.6 us -> 0 us
  blocking collectives: 26.3 us -> 0 us
  starting transfers between devices: 54.6 us -> 80.1 us
  between operations: 14 us -> 0.7 us
  other arithmetic: 11.2 us -> 0.15 us
    psum x4 -> x0, waiting for transfers between devices: 429 us -> none  [the longest x2 300 us: on_device(): summed = lax.psum(partial_sums, 'dev')]
    ppermute x20 -> x42, waiting for transfers between devices: 125 us -> 58.6 us  [the longest x10 31.7 us: swap_next(): lax.ppermute(value, axis, [(i, i + 1) for i in lower] + [(i + 1, i) for i...]
    gather x14 -> x0, local copies, waits for them, and re-layouts: 52.3 us -> none  [the longest x9 31.6 us: neighbour(): return jnp.take(received, inverse, axis=0, mode='fill', fill_value=0)]
    pallas_call x0 -> x20, Pallas kernels: none -> 50.7 us  [run(): return function(*values)]
    dot_general x13 -> x0, matrix products: 34.6 us -> none  [the longest x9 30.5 us: contract_first(): lax.dot_general(left, right, (((0,), (0,)), ((), ())), precision=lax.Prec...]
    all_gather x2 -> x0, blocking collectives: 26.3 us -> none  [on_device(): column_solution = lax.all_gather(owned_part, 'grp', axis=0, tiled=True)]
    all_to_all x0 -> x2, starting transfers between devices: none -> 15.4 us  [on_device(): lax.all_to_all(total.reshape(nz, OWNED, COLUMNS), 'dev', 0, 0, axis_index...]
    ppermute x20 -> x42, starting transfers between devices: 54.5 us -> 64.7 us  [the longest x10 36.8 us: swap_next(): lax.ppermute(value, axis, [(i, i + 1) for i in lower] + [(i + 1, i) for i...]
  transfers between devices with their start and end apart: 24 -> 44, of which waited for: 18 -> 27; matrix products, arithmetic and copies ran while one was open for 3% -> 0% of each run, Pallas kernels for 0% -> 10%
where the time goes in v2:
time: 194 us; the launch traced here: 192 us
  starting transfers between devices  80.1 us (41%)
  waiting for transfers between devices  58.6 us (30%)
  Pallas kernels  50.7 us (26%)
    pallas_call x20, Pallas kernels, run(): return function(*values)  50.7 us
    ppermute x10, starting transfers between devices, swap_next(): lax.ppermute(value, axis, [(i, i + 1) for i in lower] + [(i + 1, i) for i...  36.8 us
    ppermute x10, waiting for transfers between devices, swap_next(): lax.ppermute(value, axis, [(i, i + 1) for i in lower] + [(i + 1, i) for i...  31.7 us
    ppermute x32, starting transfers between devices, swap(): return lax.ppermute(value, axis, [(i, i ^ k) for i in range(size)])  27.9 us
    ppermute x32, waiting for transfers between devices, swap(): return lax.ppermute(value, axis, [(i, i ^ k) for i in range(size)])  26.8 us
    all_to_all x2, starting transfers between devices, on_device(): lax.all_to_all(total.reshape(nz, OWNED, COLUMNS), 'dev', 0, 0, axis_index...  15.4 us
  transfers between devices with their start and end apart: 44, of which 27 were waited for; matrix products, arithmetic and copies ran while one was open for 0% of the time, Pallas kernels for 10%

profile of v2, /device:TPU:14, one launch (start us, length us, event | category | flops | bytes accessed | tf_op | source)
XLA Modules:
  0.0 191.8 jit_solution(7210483914075760964)
XLA Ops:
  0.1 3.7 %pack.1 = (f32[64,1024]{1,0:T(8,128)S(1)}, bf16[1024,1024]{1,0:T(8,128)(2,1)S(1)}, f32[264,256]{1,0:T(8,128)S(1)}, f32[264,256]{1,0:T(8,128)S(1)}, f32[264,256]{1,0:T(8,128)S(1)}, /*index=5*/f32[264,256]{1,0:T(8,128)S(1)}) custom-call(s32[2]{0:T(128)S(1)} %pad_add_fusion.odd_ref, s32[4,256]{1,0:T(4,128)} %bitcast.29, f32[1024,256]{1,0:T(8,128)} %bitcast.27, ...), custom_call_target="tpu_custom_call" | custom-call | flops 2147483648 | bytes 4194304 | tf_op jit(solution)/shard_map/pack/pallas_call | solution.py:67
  4.8 4.4 %collective-permute-start.1 = (f32[264,256]{1,0:T(8,128)S(1)}, f32[264,256]{1,0:T(8,128)S(1)}, u32[]{:S(2)}, u32[]{:S(2)}) collective-permute-start(f32[264,256]{1,0:T(8,128)S(1)} %get-tuple-element.92.refs_1_.refs_13_), channel_id=1, source_target_pairs={{1,2},{3,4},{5,6},{7,8},{9,10},{11,12},{13,14},{15,16},{17,18},{19... | collective-permute-start | bytes 811016 | tf_op jit(solution)/shard_map/ppermute | solution.py:628
  23.4 3.5 %collective-permute-done.5.refs_2_ = f32[72,256]{1,0:T(8,128)S(1)} collective-permute-done((f32[72,256]{1,0:T(8,128)S(1)}, f32[72,256]{1,0:T(8,128)S(1)}, u32[]{:S(2)}, u32[]{:S(2)}) %collective-permute-start.5) | collective-permute-done | bytes 73760 | tf_op jit(solution)/shard_map/ppermute | solution.py:624
  32.3 3.3 %collective-permute-start.10 = (f32[256,256]{1,0:T(8,128)S(1)}, f32[256,256]{1,0:T(8,128)S(1)}, u32[]{:S(2)}, u32[]{:S(2)}) collective-permute-start(f32[256,256]{1,0:T(8,128)S(1)} %get-tuple-element.118), channel_id=1, source_target_pairs={{0,3},{1,2},{2,1},{3,0},{4,7},{5,6},{6,5},{7,4},{8,11},{9,10},{10,... | collective-permute-start | bytes 786440 | tf_op jit(solution)/shard_map/ppermute | solution.py:624
  35.6 8.4 %local.2 = (f32[320,256]{1,0:T(8,128)}, f32[320,256]{1,0:T(8,128)}, f32[320,256]{1,0:T(8,128)}, f32[320,256]{1,0:T(8,128)}) custom-call(bf16[1024,1024]{1,0:T(8,128)(2,1)S(1)} %get-tuple-element.86.onehot_ref, bf16[512,1024]{1,0:T(8,128)(2,1)} %get-tuple-element.104.weighted_in, f32[1024,1024]{1,0:T(8,128)} %bitcast.25, ...), custom_call_target="tpu_custom_call" | custom-call | flops 6442450944 | bytes 8388608 | tf_op jit(solution)/shard_map/local/pallas_call | solution.py:67
  44.0 2.9 %collective-permute-done.10.refs_3_ = f32[256,256]{1,0:T(8,128)S(1)} collective-permute-done((f32[256,256]{1,0:T(8,128)S(1)}, f32[256,256]{1,0:T(8,128)S(1)}, u32[]{:S(2)}, u32[]{:S(2)}) %collective-permute-start.10) | collective-permute-done | bytes 262176 | tf_op jit(solution)/shard_map/ppermute | solution.py:624
  47.7 7.8 %all-to-all-start = ((f32[8,32,256]{2,1,0:T(8,128)}), f32[8,32,256]{2,1,0:T(8,128)S(1)}, u32[]{:S(2)}, u32[]{:S(2)}) async-start(f32[8,32,256]{2,1,0:T(8,128)} %bitcast.21), calls=%async_computation | async-start | bytes 524288 | tf_op jit(solution)/shard_map/all_to_all | solution.py:671
  55.6 5.3 %collective-permute-start.12 = (f32[320,256]{1,0:T(8,128)}, f32[320,256]{1,0:T(8,128)S(1)}, u32[]{:S(2)}, u32[]{:S(2)}) collective-permute-start(f32[320,256]{1,0:T(8,128)} %get-tuple-element.112.refs_1_.refs_9_), channel_id=1, source_target_pairs={{1,2},{3,4},{5,6},{7,8},{9,10},{11,12},{13,14},{15,16},{17,18},{19... | collective-permute-start | bytes 983048 | tf_op jit(solution)/shard_map/ppermute | solution.py:628
  61.0 3.8 %collective-permute-start.14 = (f32[320,256]{1,0:T(8,128)}, f32[320,256]{1,0:T(8,128)}, u32[]{:S(2)}, u32[]{:S(2)}) collective-permute-start(f32[320,256]{1,0:T(8,128)} %get-tuple-element.114.refs_3_.refs_11_), channel_id=1, source_target_pairs={{32,64},{96,128},{160,192},{64,32},{128,96},{192,160},{33,65},{97,... | collective-permute-start | bytes 983048 | tf_op jit(solution)/shard_map/ppermute | solution.py:628
  65.1 7.0 %collective-permute-done.12.refs_5_.refs_13_ = f32[320,256]{1,0:T(8,128)S(1)} collective-permute-done((f32[320,256]{1,0:T(8,128)}, f32[320,256]{1,0:T(8,128)S(1)}, u32[]{:S(2)}, u32[]{:S(2)}) %collective-permute-start.12) | collective-permute-done | bytes 327712 | tf_op jit(solution)/shard_map/ppermute | solution.py:628
  77.9 3.1 %collective-permute-done.16.refs_2_ = f32[32,256]{1,0:T(8,128)S(1)} collective-permute-done((f32[32,256]{1,0:T(8,128)S(1)}, f32[32,256]{1,0:T(8,128)S(1)}, u32[]{:S(2)}, u32[]{:S(2)}) %collective-permute-start.16) | collective-permute-done | bytes 32800 | tf_op jit(solution)/shard_map/ppermute | solution.py:624
  83.9 3.3 %collective-permute-start.20 = (f32[64,256]{1,0:T(8,128)S(1)}, f32[64,256]{1,0:T(8,128)S(1)}, u32[]{:S(2)}, u32[]{:S(2)}) collective-permute-start(f32[64,256]{1,0:T(8,128)S(1)} %get-tuple-element.124.refs_16_), channel_id=1, source_target_pairs={{1,2},{3,4},{5,6},{7,8},{9,10},{11,12},{13,14},{15,16},{17,18},{19... | collective-permute-start | bytes 196616 | tf_op jit(solution)/shard_map/ppermute | solution.py:628
  87.2 4.9 %collective-permute-done.20.refs_9_ = f32[64,256]{1,0:T(8,128)S(1)} collective-permute-done((f32[64,256]{1,0:T(8,128)S(1)}, f32[64,256]{1,0:T(8,128)S(1)}, u32[]{:S(2)}, u32[]{:S(2)}) %collective-permute-start.20) | collective-permute-done | bytes 65568 | tf_op jit(solution)/shard_map/ppermute | solution.py:628
  92.1 10.6 %middle.1 = (f32[4,256,256]{2,1,0:T(8,128)}, f32[264,256]{1,0:T(8,128)S(1)}, f32[264,256]{1,0:T(8,128)S(1)}, f32[264,256]{1,0:T(8,128)S(1)}, f32[264,256]{1,0:T(8,128)S(1)}) custom-call(bf16[1024,1024]{1,0:T(8,128)(2,1)S(1)} %get-tuple-element.86.onehot_ref, f32[320,256]{1,0:T(8,128)} %get-tuple-element.111.refs_0_.refs_8_, ...), custom_call_target="tpu_custom_call" | custom-call | flops 6442450944 | bytes 12582912 | tf_op jit(solution)/shard_map/middle/pallas_call | solution.py:67
  102.8 4.0 %collective-permute-start.22 = (f32[264,256]{1,0:T(8,128)S(1)}, f32[264,256]{1,0:T(8,128)S(1)}, u32[]{:S(2)}, u32[]{:S(2)}) collective-permute-start(f32[264,256]{1,0:T(8,128)S(1)} %get-tuple-element.128.refs_1_), channel_id=1, source_target_pairs={{1,2},{3,4},{5,6},{7,8},{9,10},{11,12},{13,14},{15,16},{17,18},{19... | collective-permute-start | bytes 811016 | tf_op jit(solution)/shard_map/ppermute | solution.py:628
  107.0 2.8 %collective-permute-start.24 = (f32[264,256]{1,0:T(8,128)S(1)}, f32[264,256]{1,0:T(8,128)S(1)}, u32[]{:S(2)}, u32[]{:S(2)}) collective-permute-start(f32[264,256]{1,0:T(8,128)S(1)} %get-tuple-element.130.refs_3_), channel_id=1, source_target_pairs={{32,64},{96,128},{160,192},{64,32},{128,96},{192,160},{33,65},{97,... | collective-permute-start | bytes 811016 | tf_op jit(solution)/shard_map/ppermute | solution.py:628
  110.2 4.0 %collective-permute-done.22.refs_5_ = f32[264,256]{1,0:T(8,128)S(1)} collective-permute-done((f32[264,256]{1,0:T(8,128)S(1)}, f32[264,256]{1,0:T(8,128)S(1)}, u32[]{:S(2)}, u32[]{:S(2)}) %collective-permute-start.22) | collective-permute-done | bytes 270368 | tf_op jit(solution)/shard_map/ppermute | solution.py:628
  133.0 8.4 %local.3 = (f32[256,256]{1,0:T(8,128)}, f32[256,256]{1,0:T(8,128)}, f32[256,256]{1,0:T(8,128)}, f32[256,256]{1,0:T(8,128)}) custom-call(bf16[1024,1024]{1,0:T(8,128)(2,1)S(1)} %get-tuple-element.86.onehot_ref, bf16[512,1024]{1,0:T(8,128)(2,1)} %get-tuple-element.133.weighted_in, f32[1024,1024]{1,0:T(8,128)} %bitcast.26, ...), custom_call_target="tpu_custom_call" | custom-call | flops 6442450944 | bytes 8388608 | tf_op jit(solution)/shard_map/local/pallas_call | solution.py:67
  145.2 7.6 %all-to-all-start.1 = ((f32[8,32,256]{2,1,0:T(8,128)}), f32[8,32,256]{2,1,0:T(8,128)S(1)}, u32[]{:S(2)}, u32[]{:S(2)}) async-start(f32[8,32,256]{2,1,0:T(8,128)} %bitcast.22), calls=%async_computation.1 | async-start | bytes 524288 | tf_op jit(solution)/shard_map/all_to_all | solution.py:671
  153.5 5.2 %collective-permute-start.33 = (f32[256,256]{1,0:T(8,128)}, f32[256,256]{1,0:T(8,128)S(1)}, u32[]{:S(2)}, u32[]{:S(2)}) collective-permute-start(f32[256,256]{1,0:T(8,128)} %get-tuple-element.139.refs_1_), channel_id=1, source_target_pairs={{1,2},{3,4},{5,6},{7,8},{9,10},{11,12},{13,14},{15,16},{17,18},{19... | collective-permute-start | bytes 786440 | tf_op jit(solution)/shard_map/ppermute | solution.py:628
  158.8 2.9 %collective-permute-start.35 = (f32[256,256]{1,0:T(8,128)}, f32[256,256]{1,0:T(8,128)}, u32[]{:S(2)}, u32[]{:S(2)}) collective-permute-start(f32[256,256]{1,0:T(8,128)} %get-tuple-element.141.refs_3_), channel_id=1, source_target_pairs={{32,64},{96,128},{160,192},{64,32},{128,96},{192,160},{33,65},{97,... | collective-permute-start | bytes 786440 | tf_op jit(solution)/shard_map/ppermute | solution.py:628
  161.8 6.8 %collective-permute-done.33.refs_5_ = f32[256,256]{1,0:T(8,128)S(1)} collective-permute-done((f32[256,256]{1,0:T(8,128)}, f32[256,256]{1,0:T(8,128)S(1)}, u32[]{:S(2)}, u32[]{:S(2)}) %collective-permute-start.33) | collective-permute-done | bytes 262176 | tf_op jit(solution)/shard_map/ppermute | solution.py:628
  180.6 5.6 %collective-permute-done.41.refs_17_ = f32[64,256]{1,0:T(8,128)S(1)} collective-permute-done((f32[64,256]{1,0:T(8,128)S(1)}, f32[64,256]{1,0:T(8,128)S(1)}, u32[]{:S(2)}, u32[]{:S(2)}) %collective-permute-start.41) | collective-permute-done | bytes 65568 | tf_op jit(solution)/shard_map/ppermute | solution.py:628
  186.2 5.3 %last.1 = f32[1024,256]{1,0:T(8,128)} custom-call(bf16[1024,1024]{1,0:T(8,128)(2,1)S(1)} %get-tuple-element.86.onehot_ref, f32[256,256]{1,0:T(8,128)} %get-tuple-element.138.refs_0_, f32[256,256]{1,0:T(8,128)} %get-tuple-element.139.refs_1_, f32[256,256]{1,0:T(8,128)} %get-tuple-element.140.refs_2_, f32[256,256]{1,0:T(8,128)} %get-tuple-element.141.refs_3_, ...), custom_call_target="tpu_custom_call" | custom-call | flops 1073741824 | bytes 6291456 | tf_op jit(solution)/shard_map/last/pallas_call | solution.py:67
  (110 shorter events, 66.4 us)
Async XLA Ops:
  3.9 10.2 %collective-permute-start = (f32[264,256]{1,0:T(8,128)S(1)}, f32[264,256]{1,0:T(8,128)S(1)}, u32[]{:S(2)}, u32[]{:S(2)}) collective-permute-start(f32[264,256]{1,0:T(8,128)S(1)} %get-tuple-element.91.refs_0_.refs_12_), channel_id=1, source_target_pairs={{0,1},{1,0},{2,3},{3,2},{4,5},{5,4},{6,7},{7,6},{8,9},{9,8},{10,11... | collective-permute-start | bytes 811016 | tf_op jit(solution)/shard_map/ppermute | solution.py:624
  4.8 11.9 %collective-permute-start.1 = (f32[264,256]{1,0:T(8,128)S(1)}, f32[264,256]{1,0:T(8,128)S(1)}, u32[]{:S(2)}, u32[]{:S(2)}) collective-permute-start(f32[264,256]{1,0:T(8,128)S(1)} %get-tuple-element.92.refs_1_.refs_13_), channel_id=1, source_target_pairs={{1,2},{3,4},{5,6},{7,8},{9,10},{11,12},{13,14},{15,16},{17,18},{19... | collective-permute-start | bytes 811016 | tf_op jit(solution)/shard_map/ppermute | solution.py:628
  9.2 7.5 %collective-permute-start.2 = (f32[264,256]{1,0:T(8,128)S(1)}, f32[264,256]{1,0:T(8,128)S(1)}, u32[]{:S(2)}, u32[]{:S(2)}) collective-permute-start(f32[264,256]{1,0:T(8,128)S(1)} %get-tuple-element.93.refs_2_.refs_14_), channel_id=1, source_target_pairs={{0,32},{32,0},{64,96},{96,64},{128,160},{160,128},{192,224},{224,1... | collective-permute-start | bytes 811016 | tf_op jit(solution)/shard_map/ppermute | solution.py:624
  9.3 7.8 %collective-permute-start.3 = (f32[264,256]{1,0:T(8,128)S(1)}, f32[264,256]{1,0:T(8,128)S(1)}, u32[]{:S(2)}, u32[]{:S(2)}) collective-permute-start(f32[264,256]{1,0:T(8,128)S(1)} %get-tuple-element.94.refs_3_.refs_15_), channel_id=1, source_target_pairs={{32,64},{96,128},{160,192},{64,32},{128,96},{192,160},{33,65},{97,... | collective-permute-start | bytes 811016 | tf_op jit(solution)/shard_map/ppermute | solution.py:628
  31.4 12.6 %collective-permute-start.8 = (f32[256,256]{1,0:T(8,128)S(1)}, f32[256,256]{1,0:T(8,128)S(1)}, u32[]{:S(2)}, u32[]{:S(2)}) collective-permute-start(f32[256,256]{1,0:T(8,128)S(1)} %get-tuple-element.116), channel_id=1, source_target_pairs={{0,2},{1,3},{2,0},{3,1},{4,6},{5,7},{6,4},{7,5},{8,10},{9,11},{10,... | collective-permute-start | bytes 786440 | tf_op jit(solution)/shard_map/ppermute | solution.py:624
  32.3 11.8 %collective-permute-start.9 = (f32[256,256]{1,0:T(8,128)S(1)}, f32[256,256]{1,0:T(8,128)S(1)}, u32[]{:S(2)}, u32[]{:S(2)}) collective-permute-start(f32[256,256]{1,0:T(8,128)S(1)} %get-tuple-element.117), channel_id=1, source_target_pairs={{0,1},{1,0},{2,3},{3,2},{4,5},{5,4},{6,7},{7,6},{8,9},{9,8},{10,11... | collective-permute-start | bytes 786440 | tf_op jit(solution)/shard_map/ppermute | solution.py:624
  32.3 14.7 %collective-permute-start.10 = (f32[256,256]{1,0:T(8,128)S(1)}, f32[256,256]{1,0:T(8,128)S(1)}, u32[]{:S(2)}, u32[]{:S(2)}) collective-permute-start(f32[256,256]{1,0:T(8,128)S(1)} %get-tuple-element.118), channel_id=1, source_target_pairs={{0,3},{1,2},{2,1},{3,0},{4,7},{5,6},{6,5},{7,4},{8,11},{9,10},{10,... | collective-permute-start | bytes 786440 | tf_op jit(solution)/shard_map/ppermute | solution.py:624
  47.7 25.8 %all-to-all-start = ((f32[8,32,256]{2,1,0:T(8,128)}), f32[8,32,256]{2,1,0:T(8,128)S(1)}, u32[]{:S(2)}, u32[]{:S(2)}) async-start(f32[8,32,256]{2,1,0:T(8,128)} %bitcast.21), calls=%async_computation | async-start | bytes 524288 | tf_op jit(solution)/shard_map/all_to_all | solution.py:671
  55.6 9.6 %collective-permute-start.11 = (f32[320,256]{1,0:T(8,128)}, f32[320,256]{1,0:T(8,128)S(1)}, u32[]{:S(2)}, u32[]{:S(2)}) collective-permute-start(f32[320,256]{1,0:T(8,128)} %get-tuple-element.111.refs_0_.refs_8_), channel_id=1, source_target_pairs={{0,1},{1,0},{2,3},{3,2},{4,5},{5,4},{6,7},{7,6},{8,9},{9,8},{10,11... | collective-permute-start | bytes 983048 | tf_op jit(solution)/shard_map/ppermute | solution.py:624
  55.6 16.5 %collective-permute-start.12 = (f32[320,256]{1,0:T(8,128)}, f32[320,256]{1,0:T(8,128)S(1)}, u32[]{:S(2)}, u32[]{:S(2)}) collective-permute-start(f32[320,256]{1,0:T(8,128)} %get-tuple-element.112.refs_1_.refs_9_), channel_id=1, source_target_pairs={{1,2},{3,4},{5,6},{7,8},{9,10},{11,12},{13,14},{15,16},{17,18},{19... | collective-permute-start | bytes 983048 | tf_op jit(solution)/shard_map/ppermute | solution.py:628
  60.9 11.2 %collective-permute-start.13 = (f32[320,256]{1,0:T(8,128)}, f32[320,256]{1,0:T(8,128)S(1)}, u32[]{:S(2)}, u32[]{:S(2)}) collective-permute-start(f32[320,256]{1,0:T(8,128)} %get-tuple-element.113.refs_2_.refs_10_), channel_id=1, source_target_pairs={{0,32},{32,0},{64,96},{96,64},{128,160},{160,128},{192,224},{224,1... | collective-permute-start | bytes 983048 | tf_op jit(solution)/shard_map/ppermute | solution.py:624
  61.0 12.6 %collective-permute-start.14 = (f32[320,256]{1,0:T(8,128)}, f32[320,256]{1,0:T(8,128)}, u32[]{:S(2)}, u32[]{:S(2)}) collective-permute-start(f32[320,256]{1,0:T(8,128)} %get-tuple-element.114.refs_3_.refs_11_), channel_id=1, source_target_pairs={{32,64},{96,128},{160,192},{64,32},{128,96},{192,160},{33,65},{97,... | collective-permute-start | bytes 983048 | tf_op jit(solution)/shard_map/ppermute | solution.py:628
  83.9 8.3 %collective-permute-start.20 = (f32[64,256]{1,0:T(8,128)S(1)}, f32[64,256]{1,0:T(8,128)S(1)}, u32[]{:S(2)}, u32[]{:S(2)}) collective-permute-start(f32[64,256]{1,0:T(8,128)S(1)} %get-tuple-element.124.refs_16_), channel_id=1, source_target_pairs={{1,2},{3,4},{5,6},{7,8},{9,10},{11,12},{13,14},{15,16},{17,18},{19... | collective-permute-start | bytes 196616 | tf_op jit(solution)/shard_map/ppermute | solution.py:628
  102.8 11.4 %collective-permute-start.22 = (f32[264,256]{1,0:T(8,128)S(1)}, f32[264,256]{1,0:T(8,128)S(1)}, u32[]{:S(2)}, u32[]{:S(2)}) collective-permute-start(f32[264,256]{1,0:T(8,128)S(1)} %get-tuple-element.128.refs_1_), channel_id=1, source_target_pairs={{1,2},{3,4},{5,6},{7,8},{9,10},{11,12},{13,14},{15,16},{17,18},{19... | collective-permute-start | bytes 811016 | tf_op jit(solution)/shard_map/ppermute | solution.py:628
  107.0 7.8 %collective-permute-start.24 = (f32[264,256]{1,0:T(8,128)S(1)}, f32[264,256]{1,0:T(8,128)S(1)}, u32[]{:S(2)}, u32[]{:S(2)}) collective-permute-start(f32[264,256]{1,0:T(8,128)S(1)} %get-tuple-element.130.refs_3_), channel_id=1, source_target_pairs={{32,64},{96,128},{160,192},{64,32},{128,96},{192,160},{33,65},{97,... | collective-permute-start | bytes 811016 | tf_op jit(solution)/shard_map/ppermute | solution.py:628
  128.8 12.6 %collective-permute-start.29 = (f32[256,256]{1,0:T(8,128)S(1)}, f32[256,256]{1,0:T(8,128)S(1)}, u32[]{:S(2)}, u32[]{:S(2)}) collective-permute-start(f32[256,256]{1,0:T(8,128)S(1)} %get-tuple-element.143), channel_id=1, source_target_pairs={{0,2},{1,3},{2,0},{3,1},{4,6},{5,7},{6,4},{7,5},{8,10},{9,11},{10,... | collective-permute-start | bytes 786440 | tf_op jit(solution)/shard_map/ppermute | solution.py:624
  130.9 11.5 %collective-permute-start.30 = (f32[256,256]{1,0:T(8,128)S(1)}, f32[256,256]{1,0:T(8,128)S(1)}, u32[]{:S(2)}, u32[]{:S(2)}) collective-permute-start(f32[256,256]{1,0:T(8,128)S(1)} %get-tuple-element.144), channel_id=1, source_target_pairs={{0,1},{1,0},{2,3},{3,2},{4,5},{5,4},{6,7},{7,6},{8,9},{9,8},{10,11... | collective-permute-start | bytes 786440 | tf_op jit(solution)/shard_map/ppermute | solution.py:624
  130.9 13.5 %collective-permute-start.31 = (f32[256,256]{1,0:T(8,128)S(1)}, f32[256,256]{1,0:T(8,128)S(1)}, u32[]{:S(2)}, u32[]{:S(2)}) collective-permute-start(f32[256,256]{1,0:T(8,128)S(1)} %get-tuple-element.145), channel_id=1, source_target_pairs={{0,3},{1,2},{2,1},{3,0},{4,7},{5,6},{6,5},{7,4},{8,11},{9,10},{10,... | collective-permute-start | bytes 786440 | tf_op jit(solution)/shard_map/ppermute | solution.py:624
  145.2 23.4 %all-to-all-start.1 = ((f32[8,32,256]{2,1,0:T(8,128)}), f32[8,32,256]{2,1,0:T(8,128)S(1)}, u32[]{:S(2)}, u32[]{:S(2)}) async-start(f32[8,32,256]{2,1,0:T(8,128)} %bitcast.22), calls=%async_computation.1 | async-start | bytes 524288 | tf_op jit(solution)/shard_map/all_to_all | solution.py:671
  152.7 9.0 %collective-permute-start.32 = (f32[256,256]{1,0:T(8,128)}, f32[256,256]{1,0:T(8,128)S(1)}, u32[]{:S(2)}, u32[]{:S(2)}) collective-permute-start(f32[256,256]{1,0:T(8,128)} %get-tuple-element.138.refs_0_), channel_id=1, source_target_pairs={{0,1},{1,0},{2,3},{3,2},{4,5},{5,4},{6,7},{7,6},{8,9},{9,8},{10,11... | collective-permute-start | bytes 786440 | tf_op jit(solution)/shard_map/ppermute | solution.py:624
  153.5 15.0 %collective-permute-start.33 = (f32[256,256]{1,0:T(8,128)}, f32[256,256]{1,0:T(8,128)S(1)}, u32[]{:S(2)}, u32[]{:S(2)}) collective-permute-start(f32[256,256]{1,0:T(8,128)} %get-tuple-element.139.refs_1_), channel_id=1, source_target_pairs={{1,2},{3,4},{5,6},{7,8},{9,10},{11,12},{13,14},{15,16},{17,18},{19... | collective-permute-start | bytes 786440 | tf_op jit(solution)/shard_map/ppermute | solution.py:628
  158.7 9.8 %collective-permute-start.34 = (f32[256,256]{1,0:T(8,128)}, f32[256,256]{1,0:T(8,128)S(1)}, u32[]{:S(2)}, u32[]{:S(2)}) collective-permute-start(f32[256,256]{1,0:T(8,128)} %get-tuple-element.140.refs_2_), channel_id=1, source_target_pairs={{0,32},{32,0},{64,96},{96,64},{128,160},{160,128},{192,224},{224,1... | collective-permute-start | bytes 786440 | tf_op jit(solution)/shard_map/ppermute | solution.py:624
  158.8 9.7 %collective-permute-start.35 = (f32[256,256]{1,0:T(8,128)}, f32[256,256]{1,0:T(8,128)}, u32[]{:S(2)}, u32[]{:S(2)}) collective-permute-start(f32[256,256]{1,0:T(8,128)} %get-tuple-element.141.refs_3_), channel_id=1, source_target_pairs={{32,64},{96,128},{160,192},{64,32},{128,96},{192,160},{33,65},{97,... | collective-permute-start | bytes 786440 | tf_op jit(solution)/shard_map/ppermute | solution.py:628
  178.0 8.3 %collective-permute-start.41 = (f32[64,256]{1,0:T(8,128)S(1)}, f32[64,256]{1,0:T(8,128)S(1)}, u32[]{:S(2)}, u32[]{:S(2)}) collective-permute-start(f32[64,256]{1,0:T(8,128)S(1)} %get-tuple-element.151.refs_20_), channel_id=1, source_target_pairs={{1,2},{3,4},{5,6},{7,8},{9,10},{11,12},{13,14},{15,16},{17,18},{19... | collective-permute-start | bytes 196616 | tf_op jit(solution)/shard_map/ppermute | solution.py:628
  (31 other events, 319.8 us)

commit v3 on v2

--- a/solution.py
+++ b/solution.py
@@ -11,6 +11,7 @@
 FACE_ROWS = 256
 COLUMNS = 256
 OWNED = 32
+SPLIT = False
 LOCAL = 64
 SWEEPS = 2
 X_SIZE = 4
@@ -245,24 +246,22 @@
         weight_ref, lift_out, weighted_ref, sems, lift_ref = refs[2 * FACES + 4 :]
     else:
         weighted_ref, sems = refs[2 * FACES + 4 :]
-    terms = jnp.zeros((LOCAL, COLUMNS), jnp.float32)
     copies = []
     for p in range(FACES):
         mine = here[p][COLUMNS : COLUMNS + 1]
         total = mine + there[p][COLUMNS : COLUMNS + 1]
         weight = jnp.where(total > 0, mine / jnp.maximum(total, 1.0), 0.0)
-        weighted = weight * (here[p][:COLUMNS] + there[p][:COLUMNS])
-        high, low = split(weighted)
-        weighted_ref[:COLUMNS, face_at(p)] = high
-        weighted_ref[COLUMNS:, face_at(p)] = low
+        put(weighted_ref, face_at(p), weight * (here[p][:COLUMNS] + there[p][:COLUMNS]))
         at = (slice(None), face_at(p))
         copies.append(fetched(weighted_ref.at[at], weighted_out.at[at], sems.at[p]))
-        basis = basis_ref[:, face_at(p)]
-        terms = terms + mul3(split(basis), (high, low), NT)
         if first:
             weight_ref[:, face_at(p)] = jnp.broadcast_to(weight, (8, FACE_ROWS))
-            lift_ref[:, face_at(p)] = basis * weight
+            lift_ref[:, face_at(p)] = basis_ref[:, face_at(p)] * weight
             copies.append(fetched(lift_ref.at[at], lift_out.at[at], sems.at[FACES + p]))
+    terms = jnp.zeros((LOCAL, COLUMNS), jnp.float32)
+    for p in range(FACES):
+        right = (weighted_ref[:COLUMNS, face_at(p)], weighted_ref[COLUMNS:, face_at(p)])
+        terms = terms + mul3(split(basis_ref[:, face_at(p)]), right, NT)
     terms_ref[:LOCAL] = terms
     terms_ref[LOCAL:] = map_ref[...]
     for copy in copies:
@@ -288,8 +287,17 @@
 
 def coarse_kernel(n_grp, nz, nx, x_ref, half_ref, other_ref, high_in, low_in, *rest):
     outs, (scratch, right, high_ref, low_ref, sems) = rest[:nx], rest[nx:]
-    high_copy = fetched(high_in, high_ref, sems.at[0])
-    low_copy = fetched(low_in, low_ref, sems.at[1])
+
+    def pieces(step):
+        at = tile_at(step)
+        return (
+            pltpu.make_async_copy(high_in.at[at], high_ref.at[at], sems.at[0, step]),
+            pltpu.make_async_copy(low_in.at[at], low_ref.at[at], sems.at[1, step]),
+        )
+
+    for step in range(STEPS):
+        for copy in pieces(step):
+            copy.start()
     dofs = n_grp * OWNED
     column = jnp.zeros((dofs, 2 * COLUMNS), jnp.float32)
     rows = lax.broadcasted_iota(jnp.int32, (dofs, LOCAL), 0).astype(jnp.float32)
@@ -304,12 +312,12 @@
     chunk = nx * OWNED
     per_step = TILE // chunk
     x_pos = x_ref[0]
-    high_copy.wait()
-    low_copy.wait()
 
     @pl.loop(0, nz // per_step)
     def _(step):
         at = tile_at(step)
+        for copy in pieces(step):
+            copy.wait()
         out = mul(high_ref[at, :], right[...], NN)
         scratch[...] = out[:, :COLUMNS] + (
             out[:, COLUMNS:] + mul(low_ref[at, :], right[:, :COLUMNS], NN)
@@ -334,7 +342,7 @@
             pltpu.VMEM((n_grp * OWNED, 2 * COLUMNS), jnp.bfloat16),
             pltpu.VMEM(high.shape, high.dtype),
             pltpu.VMEM(low.shape, low.dtype),
-            pltpu.SemaphoreType.DMA((2,)),
+            pltpu.SemaphoreType.DMA((2, STEPS)),
         ],
     )(x_pos, half, other, high, low)
 
@@ -418,22 +426,19 @@
     return pltpu.make_async_copy(matrix_in.at[:, at], matrix.at[:, at], sems.at[t])
 
 
-def start_matrix(matrix_in, matrix, sems):
-    for t in range(STEPS):
+def start_matrix(matrix_in, matrix, sems, tiles):
+    for t in tiles:
         matrix_copy(matrix_in, matrix, sems, t).start()
 
 
-def apply(onehot_ref, matrix_in, matrix, sems, value_ref, rows_ref, result_ref):
+def to_rows(onehot_ref, value_ref, rows_ref):
     @pl.loop(0, STEPS)
     def _(t):
         put(rows_ref, tile_at(t), folded(mul(value_ref[...], onehot_ref[tile_at(t), :], NT)))
 
-    @pl.loop(0, STEPS)
-    def _(t):
-        matrix_copy(matrix_in, matrix, sems, t).wait()
-        high, low = split(matrix[:, tile_at(t)])
-        out = folded(mul(rows_ref[...], high, NN)) + mul(rows_ref[:COLUMNS], low, NN)
-        put(result_ref, tile_at(t), out)
+
+def product(rows_ref, high, low):
+    return folded(mul(rows_ref[...], high, NN)) + mul(rows_ref[:COLUMNS], low, NN)
 
 
 MATRIX = [
@@ -446,10 +451,17 @@
     outs = rest[:FACES]
     matrix, matrix_sems, weighted, lift, sems, rows, result, staged = rest[FACES:]
     weighted_copy = fetched(weighted_in, weighted, sems.at[0])
-    start_matrix(matrix_in, matrix, matrix_sems)
+    start_matrix(matrix_in, matrix, matrix_sems, range(2))
+    weighted_copy.wait()
+    start_matrix(matrix_in, matrix, matrix_sems, range(2, STEPS))
     lift_copy = fetched(lift_in, lift, sems.at[1])
-    weighted_copy.wait()
-    apply(onehot_ref, matrix_in, matrix, matrix_sems, weighted, rows, result)
+    to_rows(onehot_ref, weighted, rows)
+
+    @pl.loop(0, STEPS)
+    def _(t):
+        matrix_copy(matrix_in, matrix, matrix_sems, t).wait()
+        put(result, tile_at(t), product(rows, *split(matrix[:, tile_at(t)])))
+
     lift_copy.wait()
     copies = []
     for p in range(FACES):
@@ -480,127 +492,168 @@
 
 BODY = slice(0, COLUMNS)
 LIFT = slice(COLUMNS, LIFT_ROWS)
-
-
-def adjoint_face(p, near, far, lift_near, lift_far, own, around):
-    change = mul3(own, split(lift_near), TN)
-    change = change + mul3(split(around[p][...]), split(lift_far), TN)
-    return near + far + change
-
-
-def middle_kernel(onehot_ref, *refs):
-    groups = [refs[i * FACES : (i + 1) * FACES] for i in range(4)]
-    near_in, far_in, around, gradient_in = groups
-    own_ref, matrix_in, adjoint_out = refs[4 * FACES : 4 * FACES + 3]
-    outs = refs[4 * FACES + 3 : 5 * FACES + 3]
-    matrix, matrix_sems, near, far, gradient, sems, kept, value, rows, result = refs[
-        5 * FACES + 3 :
-    ]
-    copies = [
-        (fetched(near_in[p], near.at[p], sems.at[0, p]), fetched(far_in[p], far.at[p], sems.at[1, p]))
+FACE_BLOCK = pltpu.VMEM((FACES, COLUMNS, FACE_ROWS), jnp.float32)
+
+
+def lift_copies(near_in, far_in, lift_ref, sems):
+    copies = []
+    for p in range(FACES):
+        copies.append(fetched(near_in[p].at[LIFT], lift_ref.at[p, :LOCAL], sems.at[0, p]))
+        copies.append(fetched(far_in[p].at[LIFT], lift_ref.at[p, LOCAL:], sems.at[1, p]))
+    return copies
+
+
+def body_copies(near_in, far_in, near, far, sems):
+    return [
+        (
+            fetched(near_in[p].at[BODY], near.at[p], sems.at[2, p]),
+            fetched(far_in[p].at[BODY], far.at[p], sems.at[3, p]),
+        )
         for p in range(FACES)
     ]
-    start_matrix(matrix_in, matrix, matrix_sems)
-    gradient_copies = [
-        fetched(gradient_in[p], gradient.at[p], sems.at[2, p]) for p in range(FACES)
+
+
+def ready_kernel(*refs):
+    near_in, far_in, gradient_in = (refs[i * FACES : (i + 1) * FACES] for i in range(3))
+    matrix_in, base_ref, lift_ref, gradient_ref, high_ref, low_ref = refs[
+        3 * FACES : 3 * FACES + 6
     ]
-    own = split(own_ref[...])
-    kept_copies = []
-    for p in range(FACES):
-        for copy in copies[p]:
+    matrix, matrix_sems, near, far, sems = refs[3 * FACES + 6 :]
+    bodies = body_copies(near_in, far_in, near, far, sems)
+    start_matrix(matrix_in, matrix, matrix_sems, range(STEPS))
+    copies = lift_copies(near_in, far_in, lift_ref, sems)
+    for p in range(FACES):
+        copies.append(fetched(gradient_in[p], gradient_ref.at[p], sems.at[4, p]))
+    for p in range(FACES):
+        for copy in bodies[p]:
             copy.wait()
-        adjoint = adjoint_face(
-            p, near[p, BODY], far[p, BODY], near[p, LIFT], far[p, LIFT], own, around
-        )
+        base_ref[p] = near[p] + far[p]
+
+    @pl.loop(0, STEPS)
+    def _(t):
+        matrix_copy(matrix_in, matrix, matrix_sems, t).wait()
+        high_ref[:, tile_at(t)], low_ref[:, tile_at(t)] = split(matrix[:, tile_at(t)])
+
+    for copy in copies:
+        copy.wait()
+
+
+def ready_call(near, far, gradient, matrix):
+    half = shaped(INTERFACE, INTERFACE, dtype=jnp.bfloat16)
+    return call(
+        ready_kernel,
+        "ready",
+        [
+            shaped(FACES, COLUMNS, FACE_ROWS),
+            shaped(FACES, 2 * LOCAL, FACE_ROWS),
+            shaped(FACES, MULT_ROWS, FACE_ROWS),
+            half,
+            half,
+        ],
+        4 << 20,
+        8 << 20,
+        [HBM] * (3 * FACES + 1),
+        scratch=MATRIX + [FACE_BLOCK, FACE_BLOCK, pltpu.SemaphoreType.DMA((5, FACES))],
+    )(*near, *far, *gradient, matrix)
+
+
+def ready_last_kernel(*refs):
+    near_in, far_in, lift_near_in, lift_far_in = (
+        refs[i * FACES : (i + 1) * FACES] for i in range(4)
+    )
+    adjoint_in, base_ref, lift_ref, near, far, adjoint, sems = refs[4 * FACES :]
+    bodies = body_copies(near_in, far_in, near, far, sems)
+    kept = [fetched(adjoint_in.at[p], adjoint.at[p], sems.at[4, p]) for p in range(FACES)]
+    copies = lift_copies(lift_near_in, lift_far_in, lift_ref, sems)
+    for p in range(FACES):
+        for copy in bodies[p]:
+            copy.wait()
+        kept[p].wait()
+        base_ref[p] = near[p] + far[p] + adjoint[p]
+    for copy in copies:
+        copy.wait()
+
+
+def ready_last_call(near, far, lift_near, lift_far, adjoint):
+    return call(
+        ready_last_kernel,
+        "ready_last",
+        [shaped(FACES, COLUMNS, FACE_ROWS), shaped(FACES, 2 * LOCAL, FACE_ROWS)],
+        4 << 20,
+        5 << 20,
+        [HBM] * (4 * FACES + 1),
+        scratch=[FACE_BLOCK] * 3 + [pltpu.SemaphoreType.DMA((5, FACES))],
+    )(*near, *far, *lift_near, *lift_far, adjoint)
+
+
+def adjoint_face(base, lift, own, around):
+    both = jnp.concatenate([own[...], around[...]], axis=0)
+    return base + mul3(split(both), split(lift), TN)
+
+
+def middle_kernel(onehot_ref, base_ref, lift_ref, gradient_ref, high_ref, low_ref, *refs):
+    around, own_ref, adjoint_out = refs[:FACES], refs[FACES], refs[FACES + 1]
+    outs, (sems, kept, value, rows, result) = refs[FACES + 2 : 2 * FACES + 2], refs[2 * FACES + 2 :]
+    copies = []
+    for p in range(FACES):
+        adjoint = adjoint_face(base_ref[p], lift_ref[p], own_ref, around[p])
         kept[p] = adjoint
-        kept_copies.append(fetched(kept.at[p], adjoint_out.at[p], sems.at[3, p]))
+        copies.append(fetched(kept.at[p], adjoint_out.at[p], sems.at[p]))
         put(value, face_at(p), adjoint)
-    apply(onehot_ref, matrix_in, matrix, matrix_sems, value, rows, result)
-    for p in range(FACES):
-        gradient_copies[p].wait()
+    to_rows(onehot_ref, value, rows)
+
+    @pl.loop(0, STEPS)
+    def _(t):
+        put(result, tile_at(t), product(rows, high_ref[:, tile_at(t)], low_ref[:, tile_at(t)]))
+
+    for p in range(FACES):
         out = folded(mul(result[...], onehot_ref[:, face_at(p)], NN))
-        outs[p][:COLUMNS] = gradient[p, BODY] - out
-        outs[p][COLUMNS:] = gradient[p, COLUMNS:]
-    for copy in kept_copies:
+        outs[p][:COLUMNS] = gradient_ref[p, BODY] - out
+        outs[p][COLUMNS:] = gradient_ref[p, COLUMNS:]
+    for copy in copies:
         copy.wait()
 
 
-def middle_call(onehot, near, far, around, gradient, own, matrix):
-    lifted = pltpu.VMEM((FACES, LIFT_ROWS, FACE_ROWS), jnp.float32)
+def middle_call(onehot, ready, around, own):
     return call(
         middle_kernel,
         "middle",
         [in_hbm(FACES, COLUMNS, FACE_ROWS)] + [shaped(MULT_ROWS, FACE_ROWS)] * FACES,
         6 << 30,
         12 << 20,
-        [VMEM] + [HBM] * (2 * FACES) + [VMEM] * FACES + [HBM] * FACES + [VMEM, HBM],
-        scratch=MATRIX
-        + [
-            lifted,
-            lifted,
-            pltpu.VMEM((FACES, MULT_ROWS, FACE_ROWS), jnp.float32),
-            pltpu.SemaphoreType.DMA((4, FACES)),
-            pltpu.VMEM((FACES, COLUMNS, FACE_ROWS), jnp.float32),
-        ]
-        + [PAIR] * 3,
-    )(onehot, *near, *far, *around, *gradient, own, matrix)
-
-
-def last_kernel(onehot_ref, *refs):
-    groups = [refs[i * FACES : (i + 1) * FACES] for i in range(5)]
-    near_in, far_in, lift_near_in, lift_far_in, around = groups
-    own_ref, adjoint_in, out_ref = refs[5 * FACES : 5 * FACES + 3]
-    near, far, adjoint, lift_near, lift_far, sems, value, staged, out_sems = refs[5 * FACES + 3 :]
+        [VMEM] * (7 + FACES),
+        scratch=[pltpu.SemaphoreType.DMA((FACES,)), FACE_BLOCK] + [PAIR] * 3,
+    )(onehot, *ready, *around, own)
+
+
+def last_kernel(onehot_ref, base_ref, lift_ref, *refs):
+    around, (own_ref, out_ref, value, staged, sems) = refs[:FACES], refs[FACES:]
+    for p in range(FACES):
+        put(value, face_at(p), adjoint_face(base_ref[p], lift_ref[p], own_ref, around[p]))
     copies = []
-    for p in range(FACES):
-        pieces = (
-            (near_in[p], near.at[p]),
-            (far_in[p], far.at[p]),
-            (adjoint_in.at[p], adjoint.at[p]),
-            (lift_near_in[p].at[LIFT], lift_near.at[p]),
-            (lift_far_in[p].at[LIFT], lift_far.at[p]),
-        )
-        copies.append(
-            [fetched(source, to, sems.at[i, p]) for i, (source, to) in enumerate(pieces)]
-        )
-    own = split(own_ref[...])
-    for p in range(FACES):
-        for copy in copies[p]:
-            copy.wait()
-        out = adjoint_face(p, near[p], far[p], lift_near[p], lift_far[p], own, around)
-        put(value, face_at(p), adjoint[p] + out)
-    out_copies = []
     for t in range(STEPS):
         at = slice(t * TILE, (t + 1) * TILE)
         out = mul(onehot_ref[at, :], value[...], NT)
         staged[t] = out[:, :COLUMNS] + out[:, COLUMNS:]
-        out_copies.append(fetched(staged.at[t], out_ref.at[at], out_sems.at[t]))
-    for copy in out_copies:
+        copies.append(fetched(staged.at[t], out_ref.at[at], sems.at[t]))
+    for copy in copies:
         copy.wait()
 
 
-def last_call(onehot, near, far, lift_near, lift_far, around, own, adjoint):
-    face_block = pltpu.VMEM((FACES, COLUMNS, FACE_ROWS), jnp.float32)
-    lift_block = pltpu.VMEM((FACES, LOCAL, FACE_ROWS), jnp.float32)
+def last_call(onehot, ready, around, own):
     (out,) = call(
         last_kernel,
         "last",
         [in_hbm(INTERFACE, COLUMNS)],
         1 << 30,
         6 << 20,
-        [VMEM] + [HBM] * (4 * FACES) + [VMEM] * FACES + [VMEM, HBM],
+        [VMEM] * (4 + FACES),
         scratch=[
-            face_block,
-            face_block,
-            face_block,
-            lift_block,
-            lift_block,
-            pltpu.SemaphoreType.DMA((5, FACES)),
             PAIR,
             pltpu.VMEM((STEPS, TILE, COLUMNS), jnp.float32),
             pltpu.SemaphoreType.DMA((STEPS,)),
         ],
-    )(onehot, *near, *far, *lift_near, *lift_far, *around, own, adjoint)
+    )(onehot, *ready, *around, own)
     return out
 
 
@@ -634,13 +687,15 @@
         half = join_call(parts)
         return half, swap(half, "grp", 1)
 
+    rounds = [
+        lambda value: swap(value, "dev", 1),
+        lambda value: swap_next(value, "dev"),
+        lambda value: swap(value, "grp", 1),
+        lambda value: swap_next(value, "grp"),
+    ]
+
     def exchange(faces):
-        return [
-            swap(faces[0], "dev", 1),
-            swap_next(faces[1], "dev"),
-            swap(faces[2], "grp", 1),
-            swap_next(faces[3], "grp"),
-        ]
+        return [turn(value) for turn, value in zip(rounds, faces)]
 
     local_map = coarse_map[0, 0]
     basis, onehot, *gradient = pack_call(
@@ -665,24 +720,38 @@
             names = other
         blocks = coarse_call(x_pos, half, other, high, low, n_grp, nz, nx)
         sent = [swap(blocks[k], "dev", k) for k in (2, 1, 3)]
-        near = local_call(onehot, weighted, local_inverse[0, 0], weight, lift, first)
-        mine, *near = lax.optimization_barrier((blocks[0], *near))
+        held, _ = lax.optimization_barrier((weighted, blocks[0]))
+        near = local_call(onehot, held, local_inverse[0, 0], weight, lift, first)
+        if SPLIT:
+            far_grp = [rounds[p](near[p]) for p in (2, 3)]
+            mine, *far_grp = lax.optimization_barrier((blocks[0], *far_grp))
+        else:
+            mine, *near = lax.optimization_barrier((blocks[0], *near))
         total = add_call(mine, *sent)
         total = lax.all_to_all(
             total.reshape(nz, OWNED, COLUMNS), "dev", 0, 0, axis_index_groups=z_groups, tiled=True
         )
-        far = exchange(near)
+        if SPLIT:
+            far = [rounds[p](near[p]) for p in (0, 1)]
+        else:
+            far = exchange(near)
         total, *far = lax.optimization_barrier((total, *far))
+        if SPLIT:
+            far = far + far_grp
         owned = sum_call(total.reshape(nz * OWNED, COLUMNS))
         if first:
             lift_near, lift_far = near, far
         own, core, next_core = fetch_call(at, map_row, names, *group_gather(owned), n_grp)
-        around = [swap(own, "dev", 1), swap_next(own, "dev"), core, next_core]
+        around = [rounds[0](own), rounds[1](own), core, next_core]
         if first:
-            adjoint, *remain = middle_call(onehot, near, far, around, gradient, own, schur[0, 0])
+            matrix, _ = lax.optimization_barrier((schur, own))
+            ready = ready_call(near, far, gradient, matrix[0, 0])
+            adjoint, *remain = middle_call(onehot, ready, around, own)
             weighted, terms = weigh_call(remain, exchange(remain), basis, map_row, False)
         else:
-            out = last_call(onehot, near, far, lift_near, lift_far, around, own, adjoint)
+            kept, _ = lax.optimization_barrier((adjoint, own))
+            ready = ready_last_call(near, far, lift_near, lift_far, kept)
+            out = last_call(onehot, ready, around, own)
     return out[None, None]
 
 

time: 194 us -> 188 us (0.969)
  waiting for transfers between devices: 58.6 us -> 53.4 us
    ppermute x10, waiting for transfers between devices: 31.7 us -> 25.7 us  [swap_next(): lax.ppermute(value, axis, [(i, i + 1) for i in lower] + [(i + 1, i) for i...]
    pallas_call x20 -> x22, Pallas kernels: 50.7 us -> 49.7 us  [run(): return function(*values)]
  transfers between devices with their start and end apart: 44 -> 44, of which waited for: 27 -> 25; matrix products, arithmetic and copies ran while one was open for 0% -> 0% of each run, Pallas kernels for 10% -> 13%
where the time goes in v3:
time: 188 us; the launch traced here: 186 us
  starting transfers between devices  81.2 us (43%)
  waiting for transfers between devices  53.4 us (28%)
  Pallas kernels  49.7 us (26%)
    pallas_call x22, Pallas kernels, run(): return function(*values)  49.7 us
    ppermute x10, starting transfers between devices, swap_next(): lax.ppermute(value, axis, [(i, i + 1) for i in lower] + [(i + 1, i) for i...  38.5 us
    ppermute x32, starting transfers between devices, swap(): return lax.ppermute(value, axis, [(i, i ^ k) for i in range(size)])  27.9 us
    ppermute x32, waiting for transfers between devices, swap(): return lax.ppermute(value, axis, [(i, i ^ k) for i in range(size)])  27.8 us
    ppermute x10, waiting for transfers between devices, swap_next(): lax.ppermute(value, axis, [(i, i + 1) for i in lower] + [(i + 1, i) for i...  25.7 us
    all_to_all x2, starting transfers between devices, on_device(): lax.all_to_all(total.reshape(nz, OWNED, COLUMNS), 'dev', 0, 0, axis_index...  14.8 us
  transfers between devices with their start and end apart: 44, of which 25 were waited for; matrix products, arithmetic and copies ran while one was open for 0% of the time, Pallas kernels for 13%

profile of v3, /device:TPU:14, one launch (start us, length us, event | category | flops | bytes accessed | tf_op | source)
XLA Modules:
  0.0 186.1 jit_solution(3480954770830357784)
XLA Ops:
  0.1 3.7 %pack.1 = (f32[64,1024]{1,0:T(8,128)S(1)}, bf16[1024,1024]{1,0:T(8,128)(2,1)S(1)}, f32[264,256]{1,0:T(8,128)S(1)}, f32[264,256]{1,0:T(8,128)S(1)}, f32[264,256]{1,0:T(8,128)S(1)}, /*index=5*/f32[264,256]{1,0:T(8,128)S(1)}) custom-call(s32[2]{0:T(128)S(1)} %pad_add_fusion.odd_ref, s32[4,256]{1,0:T(4,128)} %bitcast.29, f32[1024,256]{1,0:T(8,128)} %bitcast.27, ...), custom_call_target="tpu_custom_call" | custom-call | flops 2147483648 | bytes 4194304 | tf_op jit(solution)/shard_map/pack/pallas_call | solution.py:68
  4.8 4.4 %collective-permute-start.1 = (f32[264,256]{1,0:T(8,128)S(1)}, f32[264,256]{1,0:T(8,128)S(1)}, u32[]{:S(2)}, u32[]{:S(2)}) collective-permute-start(f32[264,256]{1,0:T(8,128)S(1)} %get-tuple-element.103.refs_1_.refs_9_), channel_id=1, source_target_pairs={{1,2},{3,4},{5,6},{7,8},{9,10},{11,12},{13,14},{15,16},{17,18},{19... | collective-permute-start | bytes 811016 | tf_op jit(solution)/shard_map/ppermute | solution.py:681
  23.2 3.5 %collective-permute-done.5.refs_2_ = f32[72,256]{1,0:T(8,128)S(1)} collective-permute-done((f32[72,256]{1,0:T(8,128)S(1)}, f32[72,256]{1,0:T(8,128)S(1)}, u32[]{:S(2)}, u32[]{:S(2)}) %collective-permute-start.5) | collective-permute-done | bytes 73760 | tf_op jit(solution)/shard_map/ppermute | solution.py:677
  29.3 3.5 %coarse.2 = (f32[256,256]{1,0:T(8,128)S(1)}, f32[256,256]{1,0:T(8,128)S(1)}, f32[256,256]{1,0:T(8,128)S(1)}, f32[256,256]{1,0:T(8,128)S(1)}) custom-call(s32[1]{0:T(128)} %bitcast.6.x_ref, f32[288,256]{1,0:T(8,128)} %join.4.half_ref, f32[288,256]{1,0:T(8,128)S(1)} %collective-permute-done.7.other_ref.names_ref, ...), custom_call_target="tpu_custom_call" | custom-call | flops 629145600 | bytes 3145728 | tf_op jit(solution)/shard_map/coarse/pallas_call | solution.py:68
  33.7 3.3 %collective-permute-start.10 = (f32[256,256]{1,0:T(8,128)S(1)}, f32[256,256]{1,0:T(8,128)S(1)}, u32[]{:S(2)}, u32[]{:S(2)}) collective-permute-start(f32[256,256]{1,0:T(8,128)S(1)} %get-tuple-element.130), channel_id=1, source_target_pairs={{0,3},{1,2},{2,1},{3,0},{4,7},{5,6},{6,5},{7,4},{8,11},{9,10},{10,... | collective-permute-start | bytes 786440 | tf_op jit(solution)/shard_map/ppermute | solution.py:677
  37.1 8.1 %local.2 = (f32[320,256]{1,0:T(8,128)}, f32[320,256]{1,0:T(8,128)}, f32[320,256]{1,0:T(8,128)}, f32[320,256]{1,0:T(8,128)}) custom-call(bf16[1024,1024]{1,0:T(8,128)(2,1)S(1)} %get-tuple-element.97.onehot_ref, bf16[512,1024]{1,0:T(8,128)(2,1)} %get-tuple-element.116.weighted_in, f32[1024,1024]{1,0:T(8,128)} %bitcast.25, ...), custom_call_target="tpu_custom_call" | custom-call | flops 6442450944 | bytes 8388608 | tf_op jit(solution)/shard_map/local/pallas_call | solution.py:68
  45.3 3.2 %collective-permute-done.10.refs_3_ = f32[256,256]{1,0:T(8,128)S(1)} collective-permute-done((f32[256,256]{1,0:T(8,128)S(1)}, f32[256,256]{1,0:T(8,128)S(1)}, u32[]{:S(2)}, u32[]{:S(2)}) %collective-permute-start.10) | collective-permute-done | bytes 262176 | tf_op jit(solution)/shard_map/ppermute | solution.py:677
  49.2 7.8 %all-to-all-start = ((f32[8,32,256]{2,1,0:T(8,128)}), f32[8,32,256]{2,1,0:T(8,128)S(1)}, u32[]{:S(2)}, u32[]{:S(2)}) async-start(f32[8,32,256]{2,1,0:T(8,128)} %bitcast.22), calls=%async_computation | async-start | bytes 524288 | tf_op jit(solution)/shard_map/all_to_all | solution.py:731
  57.0 5.3 %collective-permute-start.12 = (f32[320,256]{1,0:T(8,128)}, f32[320,256]{1,0:T(8,128)S(1)}, u32[]{:S(2)}, u32[]{:S(2)}) collective-permute-start(f32[320,256]{1,0:T(8,128)} %get-tuple-element.124.refs_1_.refs_9_), channel_id=1, source_target_pairs={{1,2},{3,4},{5,6},{7,8},{9,10},{11,12},{13,14},{15,16},{17,18},{19... | collective-permute-start | bytes 983048 | tf_op jit(solution)/shard_map/ppermute | solution.py:681
  62.5 3.8 %collective-permute-start.14 = (f32[320,256]{1,0:T(8,128)}, f32[320,256]{1,0:T(8,128)}, u32[]{:S(2)}, u32[]{:S(2)}) collective-permute-start(f32[320,256]{1,0:T(8,128)} %get-tuple-element.126.refs_3_.refs_11_), channel_id=1, source_target_pairs={{32,64},{96,128},{160,192},{64,32},{128,96},{192,160},{33,65},{97,... | collective-permute-start | bytes 983048 | tf_op jit(solution)/shard_map/ppermute | solution.py:681
  66.6 7.0 %collective-permute-done.12.refs_5_.refs_13_ = f32[320,256]{1,0:T(8,128)S(1)} collective-permute-done((f32[320,256]{1,0:T(8,128)}, f32[320,256]{1,0:T(8,128)S(1)}, u32[]{:S(2)}, u32[]{:S(2)}) %collective-permute-start.12) | collective-permute-done | bytes 327712 | tf_op jit(solution)/shard_map/ppermute | solution.py:681
  84.8 3.3 %collective-permute-start.20 = (f32[64,256]{1,0:T(8,128)S(1)}, f32[64,256]{1,0:T(8,128)S(1)}, u32[]{:S(2)}, u32[]{:S(2)}) collective-permute-start(f32[64,256]{1,0:T(8,128)S(1)} %get-tuple-element.136.refs_4_), channel_id=1, source_target_pairs={{1,2},{3,4},{5,6},{7,8},{9,10},{11,12},{13,14},{15,16},{17,18},{19... | collective-permute-start | bytes 196616 | tf_op jit(solution)/shard_map/ppermute | solution.py:681
  88.2 3.7 %ready.1 = (f32[4,256,256]{2,1,0:T(8,128)S(1)}, f32[4,128,256]{2,1,0:T(8,128)S(1)}, f32[4,264,256]{2,1,0:T(8,128)S(1)}, bf16[1024,1024]{1,0:T(8,128)(2,1)S(1)}, bf16[1024,1024]{1,0:T(8,128)(2,1)S(1)}) custom-call(f32[320,256]{1,0:T(8,128)} %get-tuple-element.123.refs_0_.refs_8_, f32[320,256]{1,0:T(8,128)} %get-tuple-element.124.refs_1_.refs_9_, ...), custom_call_target="tpu_custom_call" | custom-call | flops 4194304 | bytes 8388608 | tf_op jit(solution)/shard_map/ready/pallas_call | solution.py:68
  93.1 6.2 %middle.1 = (f32[4,256,256]{2,1,0:T(8,128)}, f32[264,256]{1,0:T(8,128)S(1)}, f32[264,256]{1,0:T(8,128)S(1)}, f32[264,256]{1,0:T(8,128)S(1)}, f32[264,256]{1,0:T(8,128)S(1)}) custom-call(bf16[1024,1024]{1,0:T(8,128)(2,1)S(1)} %get-tuple-element.97.onehot_ref, f32[4,256,256]{2,1,0:T(8,128)S(1)} %get-tuple-element.138.base_ref, ...), custom_call_target="tpu_custom_call" | custom-call | flops 6442450944 | bytes 12582912 | tf_op jit(solution)/shard_map/middle/pallas_call | solution.py:68
  100.3 4.7 %collective-permute-start.22 = (f32[264,256]{1,0:T(8,128)S(1)}, f32[264,256]{1,0:T(8,128)S(1)}, u32[]{:S(2)}, u32[]{:S(2)}) collective-permute-start(f32[264,256]{1,0:T(8,128)S(1)} %get-tuple-element.146.refs_1_), channel_id=1, source_target_pairs={{1,2},{3,4},{5,6},{7,8},{9,10},{11,12},{13,14},{15,16},{17,18},{19... | collective-permute-start | bytes 811016 | tf_op jit(solution)/shard_map/ppermute | solution.py:681
  107.8 4.1 %collective-permute-done.22.refs_5_ = f32[264,256]{1,0:T(8,128)S(1)} collective-permute-done((f32[264,256]{1,0:T(8,128)S(1)}, f32[264,256]{1,0:T(8,128)S(1)}, u32[]{:S(2)}, u32[]{:S(2)}) %collective-permute-start.22) | collective-permute-done | bytes 270368 | tf_op jit(solution)/shard_map/ppermute | solution.py:681
  127.1 3.6 %collective-permute-start.31 = (f32[256,256]{1,0:T(8,128)S(1)}, f32[256,256]{1,0:T(8,128)S(1)}, u32[]{:S(2)}, u32[]{:S(2)}) collective-permute-start(f32[256,256]{1,0:T(8,128)S(1)} %get-tuple-element.164), channel_id=1, source_target_pairs={{0,3},{1,2},{2,1},{3,0},{4,7},{5,6},{6,5},{7,4},{8,11},{9,10},{10,... | collective-permute-start | bytes 786440 | tf_op jit(solution)/shard_map/ppermute | solution.py:677
  130.7 8.1 %local.3 = (f32[256,256]{1,0:T(8,128)}, f32[256,256]{1,0:T(8,128)}, f32[256,256]{1,0:T(8,128)}, f32[256,256]{1,0:T(8,128)}) custom-call(bf16[1024,1024]{1,0:T(8,128)(2,1)S(1)} %get-tuple-element.97.onehot_ref, bf16[512,1024]{1,0:T(8,128)(2,1)} %get-tuple-element.152.weighted_in, f32[1024,1024]{1,0:T(8,128)} %bitcast.26, ...), custom_call_target="tpu_custom_call" | custom-call | flops 6442450944 | bytes 8388608 | tf_op jit(solution)/shard_map/local/pallas_call | solution.py:68
  138.8 3.3 %collective-permute-done.31.refs_3_ = f32[256,256]{1,0:T(8,128)S(1)} collective-permute-done((f32[256,256]{1,0:T(8,128)S(1)}, f32[256,256]{1,0:T(8,128)S(1)}, u32[]{:S(2)}, u32[]{:S(2)}) %collective-permute-start.31) | collective-permute-done | bytes 262176 | tf_op jit(solution)/shard_map/ppermute | solution.py:677
  142.9 7.0 %all-to-all-start.1 = ((f32[8,32,256]{2,1,0:T(8,128)}), f32[8,32,256]{2,1,0:T(8,128)S(1)}, u32[]{:S(2)}, u32[]{:S(2)}) async-start(f32[8,32,256]{2,1,0:T(8,128)} %bitcast.23), calls=%async_computation.1 | async-start | bytes 524288 | tf_op jit(solution)/shard_map/all_to_all | solution.py:731
  149.8 5.7 %collective-permute-start.33 = (f32[256,256]{1,0:T(8,128)}, f32[256,256]{1,0:T(8,128)S(1)}, u32[]{:S(2)}, u32[]{:S(2)}) collective-permute-start(f32[256,256]{1,0:T(8,128)} %get-tuple-element.158.refs_1_), channel_id=1, source_target_pairs={{1,2},{3,4},{5,6},{7,8},{9,10},{11,12},{13,14},{15,16},{17,18},{19... | collective-permute-start | bytes 786440 | tf_op jit(solution)/shard_map/ppermute | solution.py:681
  155.6 3.3 %collective-permute-start.35 = (f32[256,256]{1,0:T(8,128)}, f32[256,256]{1,0:T(8,128)}, u32[]{:S(2)}, u32[]{:S(2)}) collective-permute-start(f32[256,256]{1,0:T(8,128)} %get-tuple-element.160.refs_3_), channel_id=1, source_target_pairs={{32,64},{96,128},{160,192},{64,32},{128,96},{192,160},{33,65},{97,... | collective-permute-start | bytes 786440 | tf_op jit(solution)/shard_map/ppermute | solution.py:681
  158.9 6.4 %collective-permute-done.33.refs_5_ = f32[256,256]{1,0:T(8,128)S(1)} collective-permute-done((f32[256,256]{1,0:T(8,128)}, f32[256,256]{1,0:T(8,128)S(1)}, u32[]{:S(2)}, u32[]{:S(2)}) %collective-permute-start.33) | collective-permute-done | bytes 262176 | tf_op jit(solution)/shard_map/ppermute | solution.py:681
  180.2 3.2 %collective-permute-done.41.refs_1_ = f32[64,256]{1,0:T(8,128)S(1)} collective-permute-done((f32[64,256]{1,0:T(8,128)S(1)}, f32[64,256]{1,0:T(8,128)S(1)}, u32[]{:S(2)}, u32[]{:S(2)}) %collective-permute-start.41) | collective-permute-done | bytes 65568 | tf_op jit(solution)/shard_map/ppermute | solution.py:681
  (116 shorter events, 69.2 us)
Async XLA Ops:
  3.9 10.2 %collective-permute-start = (f32[264,256]{1,0:T(8,128)S(1)}, f32[264,256]{1,0:T(8,128)S(1)}, u32[]{:S(2)}, u32[]{:S(2)}) collective-permute-start(f32[264,256]{1,0:T(8,128)S(1)} %get-tuple-element.102.refs_0_.refs_8_), channel_id=1, source_target_pairs={{0,1},{1,0},{2,3},{3,2},{4,5},{5,4},{6,7},{7,6},{8,9},{9,8},{10,11... | collective-permute-start | bytes 811016 | tf_op jit(solution)/shard_map/ppermute | solution.py:677
  4.8 11.9 %collective-permute-start.1 = (f32[264,256]{1,0:T(8,128)S(1)}, f32[264,256]{1,0:T(8,128)S(1)}, u32[]{:S(2)}, u32[]{:S(2)}) collective-permute-start(f32[264,256]{1,0:T(8,128)S(1)} %get-tuple-element.103.refs_1_.refs_9_), channel_id=1, source_target_pairs={{1,2},{3,4},{5,6},{7,8},{9,10},{11,12},{13,14},{15,16},{17,18},{19... | collective-permute-start | bytes 811016 | tf_op jit(solution)/shard_map/ppermute | solution.py:681
  9.3 7.8 %collective-permute-start.3 = (f32[264,256]{1,0:T(8,128)S(1)}, f32[264,256]{1,0:T(8,128)S(1)}, u32[]{:S(2)}, u32[]{:S(2)}) collective-permute-start(f32[264,256]{1,0:T(8,128)S(1)} %get-tuple-element.105.refs_3_.refs_11_), channel_id=1, source_target_pairs={{32,64},{96,128},{160,192},{64,32},{128,96},{192,160},{33,65},{97,... | collective-permute-start | bytes 811016 | tf_op jit(solution)/shard_map/ppermute | solution.py:681
  32.9 12.3 %collective-permute-start.8 = (f32[256,256]{1,0:T(8,128)S(1)}, f32[256,256]{1,0:T(8,128)S(1)}, u32[]{:S(2)}, u32[]{:S(2)}) collective-permute-start(f32[256,256]{1,0:T(8,128)S(1)} %get-tuple-element.128), channel_id=1, source_target_pairs={{0,2},{1,3},{2,0},{3,1},{4,6},{5,7},{6,4},{7,5},{8,10},{9,11},{10,... | collective-permute-start | bytes 786440 | tf_op jit(solution)/shard_map/ppermute | solution.py:677
  33.7 11.5 %collective-permute-start.9 = (f32[256,256]{1,0:T(8,128)S(1)}, f32[256,256]{1,0:T(8,128)S(1)}, u32[]{:S(2)}, u32[]{:S(2)}) collective-permute-start(f32[256,256]{1,0:T(8,128)S(1)} %get-tuple-element.129), channel_id=1, source_target_pairs={{0,1},{1,0},{2,3},{3,2},{4,5},{5,4},{6,7},{7,6},{8,9},{9,8},{10,11... | collective-permute-start | bytes 786440 | tf_op jit(solution)/shard_map/ppermute | solution.py:677
  33.7 14.7 %collective-permute-start.10 = (f32[256,256]{1,0:T(8,128)S(1)}, f32[256,256]{1,0:T(8,128)S(1)}, u32[]{:S(2)}, u32[]{:S(2)}) collective-permute-start(f32[256,256]{1,0:T(8,128)S(1)} %get-tuple-element.130), channel_id=1, source_target_pairs={{0,3},{1,2},{2,1},{3,0},{4,7},{5,6},{6,5},{7,4},{8,11},{9,10},{10,... | collective-permute-start | bytes 786440 | tf_op jit(solution)/shard_map/ppermute | solution.py:677
  49.2 25.1 %all-to-all-start = ((f32[8,32,256]{2,1,0:T(8,128)}), f32[8,32,256]{2,1,0:T(8,128)S(1)}, u32[]{:S(2)}, u32[]{:S(2)}) async-start(f32[8,32,256]{2,1,0:T(8,128)} %bitcast.22), calls=%async_computation | async-start | bytes 524288 | tf_op jit(solution)/shard_map/all_to_all | solution.py:731
  57.0 9.6 %collective-permute-start.11 = (f32[320,256]{1,0:T(8,128)}, f32[320,256]{1,0:T(8,128)S(1)}, u32[]{:S(2)}, u32[]{:S(2)}) collective-permute-start(f32[320,256]{1,0:T(8,128)} %get-tuple-element.123.refs_0_.refs_8_), channel_id=1, source_target_pairs={{0,1},{1,0},{2,3},{3,2},{4,5},{5,4},{6,7},{7,6},{8,9},{9,8},{10,11... | collective-permute-start | bytes 983048 | tf_op jit(solution)/shard_map/ppermute | solution.py:677
  57.0 16.5 %collective-permute-start.12 = (f32[320,256]{1,0:T(8,128)}, f32[320,256]{1,0:T(8,128)S(1)}, u32[]{:S(2)}, u32[]{:S(2)}) collective-permute-start(f32[320,256]{1,0:T(8,128)} %get-tuple-element.124.refs_1_.refs_9_), channel_id=1, source_target_pairs={{1,2},{3,4},{5,6},{7,8},{9,10},{11,12},{13,14},{15,16},{17,18},{19... | collective-permute-start | bytes 983048 | tf_op jit(solution)/shard_map/ppermute | solution.py:681
  62.4 11.2 %collective-permute-start.13 = (f32[320,256]{1,0:T(8,128)}, f32[320,256]{1,0:T(8,128)S(1)}, u32[]{:S(2)}, u32[]{:S(2)}) collective-permute-start(f32[320,256]{1,0:T(8,128)} %get-tuple-element.125.refs_2_.refs_10_), channel_id=1, source_target_pairs={{0,32},{32,0},{64,96},{96,64},{128,160},{160,128},{192,224},{224,1... | collective-permute-start | bytes 983048 | tf_op jit(solution)/shard_map/ppermute | solution.py:677
  62.5 11.8 %collective-permute-start.14 = (f32[320,256]{1,0:T(8,128)}, f32[320,256]{1,0:T(8,128)}, u32[]{:S(2)}, u32[]{:S(2)}) collective-permute-start(f32[320,256]{1,0:T(8,128)} %get-tuple-element.126.refs_3_.refs_11_), channel_id=1, source_target_pairs={{32,64},{96,128},{160,192},{64,32},{128,96},{192,160},{33,65},{97,... | collective-permute-start | bytes 983048 | tf_op jit(solution)/shard_map/ppermute | solution.py:681
  84.8 8.3 %collective-permute-start.20 = (f32[64,256]{1,0:T(8,128)S(1)}, f32[64,256]{1,0:T(8,128)S(1)}, u32[]{:S(2)}, u32[]{:S(2)}) collective-permute-start(f32[64,256]{1,0:T(8,128)S(1)} %get-tuple-element.136.refs_4_), channel_id=1, source_target_pairs={{1,2},{3,4},{5,6},{7,8},{9,10},{11,12},{13,14},{15,16},{17,18},{19... | collective-permute-start | bytes 196616 | tf_op jit(solution)/shard_map/ppermute | solution.py:681
  99.3 8.5 %collective-permute-start.21 = (f32[264,256]{1,0:T(8,128)S(1)}, f32[264,256]{1,0:T(8,128)S(1)}, u32[]{:S(2)}, u32[]{:S(2)}) collective-permute-start(f32[264,256]{1,0:T(8,128)S(1)} %get-tuple-element.145.refs_0_), channel_id=1, source_target_pairs={{0,1},{1,0},{2,3},{3,2},{4,5},{5,4},{6,7},{7,6},{8,9},{9,8},{10,11... | collective-permute-start | bytes 811016 | tf_op jit(solution)/shard_map/ppermute | solution.py:677
  100.3 11.7 %collective-permute-start.22 = (f32[264,256]{1,0:T(8,128)S(1)}, f32[264,256]{1,0:T(8,128)S(1)}, u32[]{:S(2)}, u32[]{:S(2)}) collective-permute-start(f32[264,256]{1,0:T(8,128)S(1)} %get-tuple-element.146.refs_1_), channel_id=1, source_target_pairs={{1,2},{3,4},{5,6},{7,8},{9,10},{11,12},{13,14},{15,16},{17,18},{19... | collective-permute-start | bytes 811016 | tf_op jit(solution)/shard_map/ppermute | solution.py:681
  105.0 7.8 %collective-permute-start.24 = (f32[264,256]{1,0:T(8,128)S(1)}, f32[264,256]{1,0:T(8,128)S(1)}, u32[]{:S(2)}, u32[]{:S(2)}) collective-permute-start(f32[264,256]{1,0:T(8,128)S(1)} %get-tuple-element.148.refs_3_), channel_id=1, source_target_pairs={{32,64},{96,128},{160,192},{64,32},{128,96},{192,160},{33,65},{97,... | collective-permute-start | bytes 811016 | tf_op jit(solution)/shard_map/ppermute | solution.py:681
  126.5 12.3 %collective-permute-start.29 = (f32[256,256]{1,0:T(8,128)S(1)}, f32[256,256]{1,0:T(8,128)S(1)}, u32[]{:S(2)}, u32[]{:S(2)}) collective-permute-start(f32[256,256]{1,0:T(8,128)S(1)} %get-tuple-element.162), channel_id=1, source_target_pairs={{0,2},{1,3},{2,0},{3,1},{4,6},{5,7},{6,4},{7,5},{8,10},{9,11},{10,... | collective-permute-start | bytes 786440 | tf_op jit(solution)/shard_map/ppermute | solution.py:677
  127.1 11.7 %collective-permute-start.30 = (f32[256,256]{1,0:T(8,128)S(1)}, f32[256,256]{1,0:T(8,128)S(1)}, u32[]{:S(2)}, u32[]{:S(2)}) collective-permute-start(f32[256,256]{1,0:T(8,128)S(1)} %get-tuple-element.163), channel_id=1, source_target_pairs={{0,1},{1,0},{2,3},{3,2},{4,5},{5,4},{6,7},{7,6},{8,9},{9,8},{10,11... | collective-permute-start | bytes 786440 | tf_op jit(solution)/shard_map/ppermute | solution.py:677
  127.1 15.0 %collective-permute-start.31 = (f32[256,256]{1,0:T(8,128)S(1)}, f32[256,256]{1,0:T(8,128)S(1)}, u32[]{:S(2)}, u32[]{:S(2)}) collective-permute-start(f32[256,256]{1,0:T(8,128)S(1)} %get-tuple-element.164), channel_id=1, source_target_pairs={{0,3},{1,2},{2,1},{3,0},{4,7},{5,6},{6,5},{7,4},{8,11},{9,10},{10,... | collective-permute-start | bytes 786440 | tf_op jit(solution)/shard_map/ppermute | solution.py:677
  142.9 22.5 %all-to-all-start.1 = ((f32[8,32,256]{2,1,0:T(8,128)}), f32[8,32,256]{2,1,0:T(8,128)S(1)}, u32[]{:S(2)}, u32[]{:S(2)}) async-start(f32[8,32,256]{2,1,0:T(8,128)} %bitcast.23), calls=%async_computation.1 | async-start | bytes 524288 | tf_op jit(solution)/shard_map/all_to_all | solution.py:731
  149.8 9.1 %collective-permute-start.32 = (f32[256,256]{1,0:T(8,128)}, f32[256,256]{1,0:T(8,128)S(1)}, u32[]{:S(2)}, u32[]{:S(2)}) collective-permute-start(f32[256,256]{1,0:T(8,128)} %get-tuple-element.157.refs_0_), channel_id=1, source_target_pairs={{0,1},{1,0},{2,3},{3,2},{4,5},{5,4},{6,7},{7,6},{8,9},{9,8},{10,11... | collective-permute-start | bytes 786440 | tf_op jit(solution)/shard_map/ppermute | solution.py:677
  149.8 15.5 %collective-permute-start.33 = (f32[256,256]{1,0:T(8,128)}, f32[256,256]{1,0:T(8,128)S(1)}, u32[]{:S(2)}, u32[]{:S(2)}) collective-permute-start(f32[256,256]{1,0:T(8,128)} %get-tuple-element.158.refs_1_), channel_id=1, source_target_pairs={{1,2},{3,4},{5,6},{7,8},{9,10},{11,12},{13,14},{15,16},{17,18},{19... | collective-permute-start | bytes 786440 | tf_op jit(solution)/shard_map/ppermute | solution.py:681
  155.5 9.8 %collective-permute-start.34 = (f32[256,256]{1,0:T(8,128)}, f32[256,256]{1,0:T(8,128)S(1)}, u32[]{:S(2)}, u32[]{:S(2)}) collective-permute-start(f32[256,256]{1,0:T(8,128)} %get-tuple-element.159.refs_2_), channel_id=1, source_target_pairs={{0,32},{32,0},{64,96},{96,64},{128,160},{160,128},{192,224},{224,1... | collective-permute-start | bytes 786440 | tf_op jit(solution)/shard_map/ppermute | solution.py:677
  155.6 9.7 %collective-permute-start.35 = (f32[256,256]{1,0:T(8,128)}, f32[256,256]{1,0:T(8,128)}, u32[]{:S(2)}, u32[]{:S(2)}) collective-permute-start(f32[256,256]{1,0:T(8,128)} %get-tuple-element.160.refs_3_), channel_id=1, source_target_pairs={{32,64},{96,128},{160,192},{64,32},{128,96},{192,160},{33,65},{97,... | collective-permute-start | bytes 786440 | tf_op jit(solution)/shard_map/ppermute | solution.py:681
  175.1 8.3 %collective-permute-start.41 = (f32[64,256]{1,0:T(8,128)S(1)}, f32[64,256]{1,0:T(8,128)S(1)}, u32[]{:S(2)}, u32[]{:S(2)}) collective-permute-start(f32[64,256]{1,0:T(8,128)S(1)} %get-tuple-element.171.refs_4_), channel_id=1, source_target_pairs={{1,2},{3,4},{5,6},{7,8},{9,10},{11,12},{13,14},{15,16},{17,18},{19... | collective-permute-start | bytes 196616 | tf_op jit(solution)/shard_map/ppermute | solution.py:681
  (33 other events, 325.7 us)

commit v4 on v3

--- a/solution.py
+++ b/solution.py
@@ -11,7 +11,6 @@
 FACE_ROWS = 256
 COLUMNS = 256
 OWNED = 32
-SPLIT = False
 LOCAL = 64
 SWEEPS = 2
 X_SIZE = 4
@@ -19,7 +18,6 @@
 FACES = 4
 TERM_ROWS = LOCAL + 8
 MULT_ROWS = COLUMNS + 8
-LIFT_ROWS = COLUMNS + LOCAL
 
 NN = (((1,), (0,)), ((), ()))
 NT = (((1,), (1,)), ((), ()))
@@ -286,7 +284,7 @@
 
 
 def coarse_kernel(n_grp, nz, nx, x_ref, half_ref, other_ref, high_in, low_in, *rest):
-    outs, (scratch, right, high_ref, low_ref, sems) = rest[:nx], rest[nx:]
+    outs, (scratch, right, high_ref, low_ref, sems) = rest[: 2 * nx], rest[2 * nx :]
 
     def pieces(step):
         at = tile_at(step)
@@ -325,15 +323,25 @@
         for i in range(per_step):
             for k in range(nx):
                 start = pl.multiple_of(i * chunk + (x_pos ^ k) * OWNED, OWNED)
-                to = pl.multiple_of((step * per_step + i) * OWNED, OWNED)
-                outs[k][pl.ds(to, OWNED), :] = scratch[pl.ds(start, OWNED), :]
+                value = scratch[pl.ds(start, OWNED), :]
+                z = step * per_step + i
+                half = nz // 2
+
+                @pl.when(z < half)
+                def _():
+                    outs[2 * k][pl.ds(pl.multiple_of(z * OWNED, OWNED), OWNED), :] = value
+
+                @pl.when(z >= half)
+                def _():
+                    to = pl.multiple_of((z - half) * OWNED, OWNED)
+                    outs[2 * k + 1][pl.ds(to, OWNED), :] = value
 
 
 def coarse_call(x_pos, half, other, high, low, n_grp, nz, nx):
     return call(
         functools.partial(coarse_kernel, n_grp, nz, nx),
         "coarse",
-        [shaped(nz * OWNED, COLUMNS)] * nx,
+        [shaped(nz // 2 * OWNED, COLUMNS)] * (2 * nx),
         600 << 20,
         3 << 20,
         [SMEM] + [VMEM] * 2 + [HBM] * 2,
@@ -347,26 +355,39 @@
     )(x_pos, half, other, high, low)
 
 
+def merge_kernel(left_ref, right_ref, out_ref):
+    out_ref[...] = left_ref[...] + right_ref[...]
+
+
+def merge_call(left, right):
+    (out,) = call(
+        merge_kernel, "merge", [shaped(*left.shape)], 1 << 18, 1 << 18, [VMEM] * 2
+    )(left, right)
+    return out
+
+
 def add_kernel(*refs):
-    count = len(refs) - 3
-    out_ref, staged, sem = refs[count:]
-    value = refs[0][...]
-    for ref in refs[1:count]:
-        value = value + ref[...]
-    staged[...] = value
-    fetched(staged, out_ref, sem).wait()
+    out_ref, staged, sems = refs[6:]
+    rows = refs[0].shape[0]
+    copies = []
+    for i in range(2):
+        at = slice(i * rows, (i + 1) * rows)
+        staged[at] = refs[3 * i][...] + refs[3 * i + 1][...] + refs[3 * i + 2][...]
+        copies.append(fetched(staged.at[at], out_ref.at[at], sems.at[i]))
+    for copy in copies:
+        copy.wait()
 
 
 def add_call(*values):
-    shape = values[0].shape
+    rows, width = values[0].shape
     (out,) = call(
         add_kernel,
         "add",
-        [in_hbm(*shape)],
+        [in_hbm(2 * rows, width)],
         1 << 20,
         1 << 20,
         [VMEM] * len(values),
-        scratch=[pltpu.VMEM(shape, jnp.float32), pltpu.SemaphoreType.DMA],
+        scratch=[pltpu.VMEM((2 * rows, width), jnp.float32), pltpu.SemaphoreType.DMA((2,))],
     )(*values)
     return out
 
@@ -390,7 +411,11 @@
     return out
 
 
-def fetch_kernel(n_grp, at_ref, map_ref, names_ref, half_ref, other_ref, *outs):
+def update_kernel(n_grp, at_ref, map_ref, half_ref, other_ref, lift_in, *rest):
+    near_in, outs = rest[:FACES], rest[FACES : 2 * FACES]
+    lift, near, sems = rest[2 * FACES :]
+    lift_copy = fetched(lift_in, lift, sems.at[FACES])
+    copies = [fetched(near_in[p], near.at[p], sems.at[p]) for p in range(FACES)]
     dofs = n_grp * OWNED
     index = lax.broadcasted_iota(jnp.int32, (dofs, LOCAL), 0)
     block, inside = index // OWNED, index % OWNED
@@ -398,27 +423,29 @@
     ids = ((block ^ at_ref[0]) * OWNED + inside).astype(jnp.float32)
     value = jnp.concatenate([half_ref[...], other_ref[...]], axis=0)
     both = jnp.concatenate(split(value), axis=1)
-    start = pl.multiple_of(at_ref[1] * TERM_ROWS + LOCAL, 8)
-    names = [
-        map_ref[:1, :LOCAL],
-        names_ref[LOCAL : LOCAL + 1, :LOCAL],
-        names_ref[pl.ds(start, 8), :][:1, :LOCAL],
-    ]
-    for name, out in zip(names, outs):
-        onehot = (ids == name).astype(jnp.float32).astype(jnp.bfloat16)
-        pair = mul(onehot, both, TN)
-        out[...] = pair[:, :COLUMNS] + pair[:, COLUMNS:]
-
-
-def fetch_call(at, map_row, names, half, other, n_grp):
+    onehot = (ids == map_ref[:1, :LOCAL]).astype(jnp.float32).astype(jnp.bfloat16)
+    pair = mul(onehot, both, TN)
+    own = split(pair[:, :COLUMNS] + pair[:, COLUMNS:])
+    lift_copy.wait()
+    for p in range(FACES):
+        copies[p].wait()
+        outs[p][...] = near[p] + mul3(own, split(lift[:, face_at(p)]), TN)
+
+
+def update_call(at, map_row, half, other, lift, near, n_grp):
     return call(
-        functools.partial(fetch_kernel, n_grp),
-        "fetch",
-        [shaped(LOCAL, COLUMNS)] * 3,
-        100 << 20,
-        1 << 20,
-        [SMEM] + [VMEM] * 4,
-    )(at, map_row, names, half, other)
+        functools.partial(update_kernel, n_grp),
+        "update",
+        [shaped(COLUMNS, FACE_ROWS)] * FACES,
+        300 << 20,
+        3 << 20,
+        [SMEM] + [VMEM] * 3 + [HBM] * (1 + FACES),
+        scratch=[
+            pltpu.VMEM((LOCAL, INTERFACE), jnp.float32),
+            pltpu.VMEM((FACES, COLUMNS, FACE_ROWS), jnp.float32),
+            pltpu.SemaphoreType.DMA((FACES + 1,)),
+        ],
+    )(at, map_row, half, other, lift, *near)
 
 
 def matrix_copy(matrix_in, matrix, sems, t):
@@ -447,14 +474,13 @@
 ]
 
 
-def local_kernel(first, onehot_ref, weighted_in, matrix_in, weight_ref, lift_in, *rest):
+def local_kernel(onehot_ref, weighted_in, matrix_in, weight_ref, *rest):
     outs = rest[:FACES]
-    matrix, matrix_sems, weighted, lift, sems, rows, result, staged = rest[FACES:]
+    matrix, matrix_sems, weighted, sems, rows, result, staged = rest[FACES:]
     weighted_copy = fetched(weighted_in, weighted, sems.at[0])
     start_matrix(matrix_in, matrix, matrix_sems, range(2))
     weighted_copy.wait()
     start_matrix(matrix_in, matrix, matrix_sems, range(2, STEPS))
-    lift_copy = fetched(lift_in, lift, sems.at[1])
     to_rows(onehot_ref, weighted, rows)
 
     @pl.loop(0, STEPS)
@@ -462,72 +488,39 @@
         matrix_copy(matrix_in, matrix, matrix_sems, t).wait()
         put(result, tile_at(t), product(rows, *split(matrix[:, tile_at(t)])))
 
-    lift_copy.wait()
     copies = []
     for p in range(FACES):
         out = folded(mul(result[...], onehot_ref[:, face_at(p)], NN))
-        staged[p, :COLUMNS] = weight_ref[:1, face_at(p)] * out
-        if first:
-            staged[p, COLUMNS:] = lift[:, face_at(p)]
-        copies.append(fetched(staged.at[p], outs[p], sems.at[2 + p]))
+        staged[p] = weight_ref[:1, face_at(p)] * out
+        copies.append(fetched(staged.at[p], outs[p], sems.at[1 + p]))
     for copy in copies:
         copy.wait()
 
 
-def local_call(onehot, weighted, matrix, weight, lift, first):
-    rows = LIFT_ROWS if first else COLUMNS
+def local_call(onehot, weighted, matrix, weight):
     return call(
-        functools.partial(local_kernel, first),
+        local_kernel,
         "local",
-        [in_hbm(rows, FACE_ROWS)] * FACES,
+        [in_hbm(COLUMNS, FACE_ROWS)] * FACES,
         6 << 30,
         8 << 20,
-        [VMEM, HBM, HBM, VMEM, HBM],
+        [VMEM, HBM, HBM, VMEM],
         scratch=MATRIX
-        + [PAIR, pltpu.VMEM((LOCAL, INTERFACE), jnp.float32), pltpu.SemaphoreType.DMA((6,))]
+        + [PAIR, pltpu.SemaphoreType.DMA((1 + FACES,))]
         + [PAIR] * 2
-        + [pltpu.VMEM((FACES, rows, FACE_ROWS), jnp.float32)],
-    )(onehot, weighted, matrix, weight, lift)
+        + [pltpu.VMEM((FACES, COLUMNS, FACE_ROWS), jnp.float32)],
+    )(onehot, weighted, matrix, weight)
 
 
 BODY = slice(0, COLUMNS)
-LIFT = slice(COLUMNS, LIFT_ROWS)
 FACE_BLOCK = pltpu.VMEM((FACES, COLUMNS, FACE_ROWS), jnp.float32)
 
 
-def lift_copies(near_in, far_in, lift_ref, sems):
-    copies = []
-    for p in range(FACES):
-        copies.append(fetched(near_in[p].at[LIFT], lift_ref.at[p, :LOCAL], sems.at[0, p]))
-        copies.append(fetched(far_in[p].at[LIFT], lift_ref.at[p, LOCAL:], sems.at[1, p]))
-    return copies
-
-
-def body_copies(near_in, far_in, near, far, sems):
-    return [
-        (
-            fetched(near_in[p].at[BODY], near.at[p], sems.at[2, p]),
-            fetched(far_in[p].at[BODY], far.at[p], sems.at[3, p]),
-        )
-        for p in range(FACES)
-    ]
-
-
 def ready_kernel(*refs):
-    near_in, far_in, gradient_in = (refs[i * FACES : (i + 1) * FACES] for i in range(3))
-    matrix_in, base_ref, lift_ref, gradient_ref, high_ref, low_ref = refs[
-        3 * FACES : 3 * FACES + 6
-    ]
-    matrix, matrix_sems, near, far, sems = refs[3 * FACES + 6 :]
-    bodies = body_copies(near_in, far_in, near, far, sems)
+    gradient_in, matrix_in = refs[:FACES], refs[FACES]
+    gradient_ref, high_ref, low_ref, matrix, matrix_sems, sems = refs[FACES + 1 :]
     start_matrix(matrix_in, matrix, matrix_sems, range(STEPS))
-    copies = lift_copies(near_in, far_in, lift_ref, sems)
-    for p in range(FACES):
-        copies.append(fetched(gradient_in[p], gradient_ref.at[p], sems.at[4, p]))
-    for p in range(FACES):
-        for copy in bodies[p]:
-            copy.wait()
-        base_ref[p] = near[p] + far[p]
+    copies = [fetched(gradient_in[p], gradient_ref.at[p], sems.at[p]) for p in range(FACES)]
 
     @pl.loop(0, STEPS)
     def _(t):
@@ -538,65 +531,43 @@
         copy.wait()
 
 
-def ready_call(near, far, gradient, matrix):
+def ready_call(gradient, matrix):
     half = shaped(INTERFACE, INTERFACE, dtype=jnp.bfloat16)
     return call(
         ready_kernel,
         "ready",
-        [
-            shaped(FACES, COLUMNS, FACE_ROWS),
-            shaped(FACES, 2 * LOCAL, FACE_ROWS),
-            shaped(FACES, MULT_ROWS, FACE_ROWS),
-            half,
-            half,
-        ],
+        [shaped(FACES, MULT_ROWS, FACE_ROWS), half, half],
         4 << 20,
         8 << 20,
-        [HBM] * (3 * FACES + 1),
-        scratch=MATRIX + [FACE_BLOCK, FACE_BLOCK, pltpu.SemaphoreType.DMA((5, FACES))],
-    )(*near, *far, *gradient, matrix)
-
-
-def ready_last_kernel(*refs):
-    near_in, far_in, lift_near_in, lift_far_in = (
-        refs[i * FACES : (i + 1) * FACES] for i in range(4)
-    )
-    adjoint_in, base_ref, lift_ref, near, far, adjoint, sems = refs[4 * FACES :]
-    bodies = body_copies(near_in, far_in, near, far, sems)
-    kept = [fetched(adjoint_in.at[p], adjoint.at[p], sems.at[4, p]) for p in range(FACES)]
-    copies = lift_copies(lift_near_in, lift_far_in, lift_ref, sems)
-    for p in range(FACES):
-        for copy in bodies[p]:
-            copy.wait()
-        kept[p].wait()
-        base_ref[p] = near[p] + far[p] + adjoint[p]
-    for copy in copies:
-        copy.wait()
-
-
-def ready_last_call(near, far, lift_near, lift_far, adjoint):
-    return call(
+        [HBM] * (FACES + 1),
+        scratch=MATRIX + [pltpu.SemaphoreType.DMA((FACES,))],
+    )(*gradient, matrix)
+
+
+def ready_last_kernel(adjoint_in, adjoint_ref, sem):
+    fetched(adjoint_in, adjoint_ref, sem).wait()
+
+
+def ready_last_call(adjoint):
+    (out,) = call(
         ready_last_kernel,
         "ready_last",
-        [shaped(FACES, COLUMNS, FACE_ROWS), shaped(FACES, 2 * LOCAL, FACE_ROWS)],
-        4 << 20,
-        5 << 20,
-        [HBM] * (4 * FACES + 1),
-        scratch=[FACE_BLOCK] * 3 + [pltpu.SemaphoreType.DMA((5, FACES))],
-    )(*near, *far, *lift_near, *lift_far, adjoint)
-
-
-def adjoint_face(base, lift, own, around):
-    both = jnp.concatenate([own[...], around[...]], axis=0)
-    return base + mul3(split(both), split(lift), TN)
-
-
-def middle_kernel(onehot_ref, base_ref, lift_ref, gradient_ref, high_ref, low_ref, *refs):
-    around, own_ref, adjoint_out = refs[:FACES], refs[FACES], refs[FACES + 1]
-    outs, (sems, kept, value, rows, result) = refs[FACES + 2 : 2 * FACES + 2], refs[2 * FACES + 2 :]
+        [shaped(FACES, COLUMNS, FACE_ROWS)],
+        1 << 20,
+        2 << 20,
+        [HBM],
+        scratch=[pltpu.SemaphoreType.DMA],
+    )(adjoint)
+    return out
+
+
+def middle_kernel(onehot_ref, gradient_ref, high_ref, low_ref, *refs):
+    near, far, adjoint_out = refs[:FACES], refs[FACES : 2 * FACES], refs[2 * FACES]
+    outs = refs[2 * FACES + 1 : 3 * FACES + 1]
+    sems, kept, value, rows, result = refs[3 * FACES + 1 :]
     copies = []
     for p in range(FACES):
-        adjoint = adjoint_face(base_ref[p], lift_ref[p], own_ref, around[p])
+        adjoint = near[p][...] + far[p][...]
         kept[p] = adjoint
         copies.append(fetched(kept.at[p], adjoint_out.at[p], sems.at[p]))
         put(value, face_at(p), adjoint)
@@ -614,22 +585,23 @@
         copy.wait()
 
 
-def middle_call(onehot, ready, around, own):
+def middle_call(onehot, ready, near, far):
     return call(
         middle_kernel,
         "middle",
         [in_hbm(FACES, COLUMNS, FACE_ROWS)] + [shaped(MULT_ROWS, FACE_ROWS)] * FACES,
         6 << 30,
         12 << 20,
-        [VMEM] * (7 + FACES),
+        [VMEM] * (4 + 2 * FACES),
         scratch=[pltpu.SemaphoreType.DMA((FACES,)), FACE_BLOCK] + [PAIR] * 3,
-    )(onehot, *ready, *around, own)
-
-
-def last_kernel(onehot_ref, base_ref, lift_ref, *refs):
-    around, (own_ref, out_ref, value, staged, sems) = refs[:FACES], refs[FACES:]
-    for p in range(FACES):
-        put(value, face_at(p), adjoint_face(base_ref[p], lift_ref[p], own_ref, around[p]))
+    )(onehot, *ready, *near, *far)
+
+
+def last_kernel(onehot_ref, adjoint_ref, *refs):
+    near, far = refs[:FACES], refs[FACES : 2 * FACES]
+    out_ref, value, staged, sems = refs[2 * FACES :]
+    for p in range(FACES):
+        put(value, face_at(p), adjoint_ref[p] + near[p][...] + far[p][...])
     copies = []
     for t in range(STEPS):
         at = slice(t * TILE, (t + 1) * TILE)
@@ -640,20 +612,20 @@
         copy.wait()
 
 
-def last_call(onehot, ready, around, own):
+def last_call(onehot, adjoint, near, far):
     (out,) = call(
         last_kernel,
         "last",
         [in_hbm(INTERFACE, COLUMNS)],
         1 << 30,
         6 << 20,
-        [VMEM] * (4 + FACES),
+        [VMEM] * (2 + 2 * FACES),
         scratch=[
             PAIR,
             pltpu.VMEM((STEPS, TILE, COLUMNS), jnp.float32),
             pltpu.SemaphoreType.DMA((STEPS,)),
         ],
-    )(onehot, *ready, *around, own)
+    )(onehot, adjoint, *near, *far)
     return out
 
 
@@ -668,9 +640,7 @@
     x_pos = (dev % nx).reshape(1)
     z_groups = [[z * nx + x for z in range(nz)] for x in range(nx)]
     odd = jnp.stack([dev % 2, grp % 2])
-    beyond = jnp.where(grp % 2 == 1, grp + 1, grp - 1)
-    beyond = jnp.where((beyond < 0) | (beyond >= n_grp), grp ^ 1, beyond)
-    at = jnp.stack([grp, (grp ^ beyond) // 2])
+    at = grp.reshape(1)
 
     def swap(value, axis, k):
         size = lax.axis_size(axis)
@@ -683,7 +653,8 @@
         )
 
     def group_gather(value):
-        parts = [value] + [swap(value, "grp", k) for k in range(2, n_grp, 2)]
+        parts = {k: swap(value, "grp", k) for k in (2, 6, 4)}
+        parts = [value] + [parts[k] for k in range(2, n_grp, 2)]
         half = join_call(parts)
         return half, swap(half, "grp", 1)
 
@@ -710,48 +681,36 @@
     high, low, map_row = lax.optimization_barrier((high, low, map_row))
 
     weighted, terms, weight, lift = weigh_call(gradient, arrived, basis, map_row, True)
-    names = None
     adjoint = None
-    lift_near = lift_far = None
     for sweep in range(SWEEPS):
         first = sweep == 0
         half, other = group_gather(terms)
-        if first:
-            names = other
         blocks = coarse_call(x_pos, half, other, high, low, n_grp, nz, nx)
-        sent = [swap(blocks[k], "dev", k) for k in (2, 1, 3)]
-        held, _ = lax.optimization_barrier((weighted, blocks[0]))
-        near = local_call(onehot, held, local_inverse[0, 0], weight, lift, first)
-        if SPLIT:
-            far_grp = [rounds[p](near[p]) for p in (2, 3)]
-            mine, *far_grp = lax.optimization_barrier((blocks[0], *far_grp))
-        else:
-            mine, *near = lax.optimization_barrier((blocks[0], *near))
-        total = add_call(mine, *sent)
+        through = [swap(blocks[4], "dev", 1), swap(blocks[5], "dev", 3)]
+        direct = [swap(blocks[2], "dev", 1), swap(blocks[7], "dev", 3)]
+        passed = [
+            swap(merge_call(blocks[6], through[0]), "dev", 3),
+            swap(merge_call(blocks[3], through[1]), "dev", 1),
+        ]
+        total = add_call(blocks[0], direct[0], passed[0], blocks[1], passed[1], direct[1])
         total = lax.all_to_all(
             total.reshape(nz, OWNED, COLUMNS), "dev", 0, 0, axis_index_groups=z_groups, tiled=True
         )
-        if SPLIT:
-            far = [rounds[p](near[p]) for p in (0, 1)]
-        else:
-            far = exchange(near)
-        total, *far = lax.optimization_barrier((total, *far))
-        if SPLIT:
-            far = far + far_grp
+        held, _ = lax.optimization_barrier((weighted, direct[0]))
+        near = local_call(onehot, held, local_inverse[0, 0], weight)
+        total, *near = lax.optimization_barrier((total, *near))
         owned = sum_call(total.reshape(nz * OWNED, COLUMNS))
+        half, other = group_gather(owned)
+        near = update_call(at, map_row, half, other, lift, near, n_grp)
+        far = exchange(near)
         if first:
-            lift_near, lift_far = near, far
-        own, core, next_core = fetch_call(at, map_row, names, *group_gather(owned), n_grp)
-        around = [rounds[0](own), rounds[1](own), core, next_core]
-        if first:
-            matrix, _ = lax.optimization_barrier((schur, own))
-            ready = ready_call(near, far, gradient, matrix[0, 0])
-            adjoint, *remain = middle_call(onehot, ready, around, own)
+            matrix, _ = lax.optimization_barrier((schur, near[0]))
+            ready = ready_call(gradient, matrix[0, 0])
+            adjoint, *remain = middle_call(onehot, ready, near, far)
             weighted, terms = weigh_call(remain, exchange(remain), basis, map_row, False)
         else:
-            kept, _ = lax.optimization_barrier((adjoint, own))
-            ready = ready_last_call(near, far, lift_near, lift_far, kept)
-            out = last_call(onehot, ready, around, own)
+            kept, _ = lax.optimization_barrier((adjoint, near[0]))
+            out = last_call(onehot, ready_last_call(kept), near, far)
     return out[None, None]
 
 

time: 188 us -> 184 us (0.979)
  starting transfers between devices: 81.2 us -> 71 us
  waiting for transfers between devices: 53.4 us -> 60.3 us
    ppermute x10 -> x8, starting transfers between devices: 38.5 us -> 25.9 us  [swap_next(): lax.ppermute(value, axis, [(i, i + 1) for i in lower] + [(i + 1, i) for i...]
    ppermute x32 -> x36, waiting for transfers between devices: 27.8 us -> 39.2 us  [swap(): return lax.ppermute(value, axis, [(i, i ^ k) for i in range(size)])]
    ppermute x10 -> x8, waiting for transfers between devices: 25.7 us -> 16.2 us  [swap_next(): lax.ppermute(value, axis, [(i, i + 1) for i in lower] + [(i + 1, i) for i...]
    all_to_all x2, waiting for transfers between devices: 0.01 us -> 4.83 us  [on_device(): lax.all_to_all(total.reshape(nz, OWNED, COLUMNS), 'dev', 0, 0, axis_index...]
    ppermute x32 -> x36, starting transfers between devices: 27.9 us -> 30.6 us  [swap(): return lax.ppermute(value, axis, [(i, i ^ k) for i in range(size)])]
    pallas_call x22 -> x26, Pallas kernels: 49.7 us -> 50.5 us  [run(): return function(*values)]
  transfers between devices with their start and end apart: 44 -> 46, of which waited for: 25 -> 33; matrix products, arithmetic and copies ran while one was open for 0% -> 0% of each run, Pallas kernels for 13% -> 12%
where the time goes in v4:
time: 184 us; the launch traced here: 183 us
  starting transfers between devices  71 us (39%)
  waiting for transfers between devices  60.3 us (33%)
  Pallas kernels  50.5 us (27%)
    pallas_call x26, Pallas kernels, run(): return function(*values)  50.5 us
    ppermute x36, waiting for transfers between devices, swap(): return lax.ppermute(value, axis, [(i, i ^ k) for i in range(size)])  39.2 us
    ppermute x36, starting transfers between devices, swap(): return lax.ppermute(value, axis, [(i, i ^ k) for i in range(size)])  30.6 us
    ppermute x8, starting transfers between devices, swap_next(): lax.ppermute(value, axis, [(i, i + 1) for i in lower] + [(i + 1, i) for i...  25.9 us
    ppermute x8, waiting for transfers between devices, swap_next(): lax.ppermute(value, axis, [(i, i + 1) for i in lower] + [(i + 1, i) for i...  16.2 us
    all_to_all x2, starting transfers between devices, on_device(): lax.all_to_all(total.reshape(nz, OWNED, COLUMNS), 'dev', 0, 0, axis_index...  14.5 us
    all_to_all x2, waiting for transfers between devices, on_device(): lax.all_to_all(total.reshape(nz, OWNED, COLUMNS), 'dev', 0, 0, axis_index...  4.83 us
  transfers between devices with their start and end apart: 46, of which 33 were waited for; matrix products, arithmetic and copies ran while one was open for 0% of the time, Pallas kernels for 12%

profile of v4, /device:TPU:14, one launch (start us, length us, event | category | flops | bytes accessed | tf_op | source)
XLA Modules:
  0.0 182.5 jit_solution(15283677922216031459)
XLA Ops:
  0.1 3.7 %pack.1 = (f32[64,1024]{1,0:T(8,128)S(1)}, bf16[1024,1024]{1,0:T(8,128)(2,1)S(1)}, f32[264,256]{1,0:T(8,128)S(1)}, f32[264,256]{1,0:T(8,128)S(1)}, f32[264,256]{1,0:T(8,128)S(1)}, /*index=5*/f32[264,256]{1,0:T(8,128)S(1)}) custom-call(s32[2]{0:T(128)S(1)} %pad_add_fusion.odd_ref, s32[4,256]{1,0:T(4,128)} %bitcast.28, f32[1024,256]{1,0:T(8,128)} %bitcast.26, ...), custom_call_target="tpu_custom_call" | custom-call | flops 2147483648 | bytes 4194304 | tf_op jit(solution)/shard_map/pack/pallas_call | solution.py:66
  4.8 4.4 %collective-permute-start.1 = (f32[264,256]{1,0:T(8,128)S(1)}, f32[264,256]{1,0:T(8,128)S(1)}, u32[]{:S(2)}, u32[]{:S(2)}) collective-permute-start(f32[264,256]{1,0:T(8,128)S(1)} %get-tuple-element.99.refs_1_), channel_id=1, source_target_pairs={{1,2},{3,4},{5,6},{7,8},{9,10},{11,12},{13,14},{15,16},{17,18},{19... | collective-permute-start | bytes 811016 | tf_op jit(solution)/shard_map/ppermute | solution.py:651
  23.2 3.5 %collective-permute-done.5.refs_2_ = f32[72,256]{1,0:T(8,128)S(1)} collective-permute-done((f32[72,256]{1,0:T(8,128)S(1)}, f32[72,256]{1,0:T(8,128)S(1)}, u32[]{:S(2)}, u32[]{:S(2)}) %collective-permute-start.5) | collective-permute-done | bytes 73760 | tf_op jit(solution)/shard_map/ppermute | solution.py:647
  29.4 3.5 %coarse.2 = (f32[128,256]{1,0:T(8,128)S(1)}, f32[128,256]{1,0:T(8,128)S(1)}, f32[128,256]{1,0:T(8,128)S(1)}, f32[128,256]{1,0:T(8,128)S(1)}, f32[128,256]{1,0:T(...) custom-call(s32[1]{0:T(128)} %bitcast.9.x_ref, f32[288,256]{1,0:T(8,128)} %join.4.half_ref, ...), custom_call_target="tpu_custom_call" | custom-call | flops 629145600 | bytes 3145728 | tf_op jit(solution)/shard_map/coarse/pallas_call | solution.py:66
  46.5 8.5 %all-to-all-start = ((f32[8,32,256]{2,1,0:T(8,128)}), f32[8,32,256]{2,1,0:T(8,128)S(1)}, u32[]{:S(2)}, u32[]{:S(2)}) async-start(f32[8,32,256]{2,1,0:T(8,128)} %bitcast.22), calls=%async_computation | async-start | bytes 524288 | tf_op jit(solution)/shard_map/all_to_all | solution.py:696
  55.0 8.1 %local.2 = (f32[256,256]{1,0:T(8,128)}, f32[256,256]{1,0:T(8,128)}, f32[256,256]{1,0:T(8,128)}, f32[256,256]{1,0:T(8,128)}) custom-call(bf16[1024,1024]{1,0:T(8,128)(2,1)S(1)} %get-tuple-element.93.onehot_ref, bf16[512,1024]{1,0:T(8,128)(2,1)} %get-tuple-element.119.weighted_in, f32[1024,1024]{1,0:T(8,128)} %bitcast.24, ...), custom_call_target="tpu_custom_call" | custom-call | flops 6442450944 | bytes 8388608 | tf_op jit(solution)/shard_map/local/pallas_call | solution.py:66
  69.9 3.2 %collective-permute-done.15.refs_2_ = f32[32,256]{1,0:T(8,128)S(1)} collective-permute-done((f32[32,256]{1,0:T(8,128)S(1)}, f32[32,256]{1,0:T(8,128)S(1)}, u32[]{:S(2)}, u32[]{:S(2)}) %collective-permute-start.15) | collective-permute-done | bytes 32800 | tf_op jit(solution)/shard_map/ppermute | solution.py:647
  77.6 3.1 %collective-permute-start.19 = (f32[256,256]{1,0:T(8,128)S(1)}, f32[256,256]{1,0:T(8,128)S(1)}, u32[]{:S(2)}, u32[]{:S(2)}) collective-permute-start(f32[256,256]{1,0:T(8,128)S(1)} %get-tuple-element.136.refs_1_), channel_id=1, source_target_pairs={{1,2},{3,4},{5,6},{7,8},{9,10},{11,12},{13,14},{15,16},{17,18},{19... | collective-permute-start | bytes 786440 | tf_op jit(solution)/shard_map/ppermute | solution.py:651
  80.8 2.8 %collective-permute-start.21 = (f32[256,256]{1,0:T(8,128)S(1)}, f32[256,256]{1,0:T(8,128)S(1)}, u32[]{:S(2)}, u32[]{:S(2)}) collective-permute-start(f32[256,256]{1,0:T(8,128)S(1)} %get-tuple-element.138.refs_3_), channel_id=1, source_target_pairs={{32,64},{96,128},{160,192},{64,32},{128,96},{192,160},{33,65},{97,... | collective-permute-start | bytes 786440 | tf_op jit(solution)/shard_map/ppermute | solution.py:651
  83.8 2.7 %ready.1 = (f32[4,264,256]{2,1,0:T(8,128)S(1)}, bf16[1024,1024]{1,0:T(8,128)(2,1)S(1)}, bf16[1024,1024]{1,0:T(8,128)(2,1)S(1)}) custom-call(f32[264,256]{1,0:T(8,128)} %copy-done, f32[264,256]{1,0:T(8,128)} %copy-done.1, f32[264,256]{1,0:T(8,128)} %copy-done.2, f32[264,256]{1,0:T(8,128)} %copy-done.3, f32[1024,1024]{1,0:T(8,128)} %bitcast.20), custom_call_target="tpu_custom_call" | custom-call | flops 4194304 | bytes 8388608 | tf_op jit(solution)/shard_map/ready/pallas_call | solution.py:66
  86.6 3.4 %collective-permute-done.19.refs_5_ = f32[256,256]{1,0:T(8,128)S(1)} collective-permute-done((f32[256,256]{1,0:T(8,128)S(1)}, f32[256,256]{1,0:T(8,128)S(1)}, u32[]{:S(2)}, u32[]{:S(2)}) %collective-permute-start.19) | collective-permute-done | bytes 262176 | tf_op jit(solution)/shard_map/ppermute | solution.py:651
  91.9 5.9 %middle.1 = (f32[4,256,256]{2,1,0:T(8,128)}, f32[264,256]{1,0:T(8,128)S(1)}, f32[264,256]{1,0:T(8,128)S(1)}, f32[264,256]{1,0:T(8,128)S(1)}, f32[264,256]{1,0:T(8,128)S(1)}) custom-call(bf16[1024,1024]{1,0:T(8,128)(2,1)S(1)} %get-tuple-element.93.onehot_ref, f32[4,264,256]{2,1,0:T(8,128)S(1)} %get-tuple-element.133.gradient_ref, ...), custom_call_target="tpu_custom_call" | custom-call | flops 6442450944 | bytes 12582912 | tf_op jit(solution)/shard_map/middle/pallas_call | solution.py:66
  98.1 4.8 %collective-permute-start.23 = (f32[264,256]{1,0:T(8,128)S(1)}, f32[264,256]{1,0:T(8,128)S(1)}, u32[]{:S(2)}, u32[]{:S(2)}) collective-permute-start(f32[264,256]{1,0:T(8,128)S(1)} %get-tuple-element.141.refs_1_), channel_id=1, source_target_pairs={{1,2},{3,4},{5,6},{7,8},{9,10},{11,12},{13,14},{15,16},{17,18},{19... | collective-permute-start | bytes 811016 | tf_op jit(solution)/shard_map/ppermute | solution.py:651
  105.3 4.2 %collective-permute-done.23.refs_5_ = f32[264,256]{1,0:T(8,128)S(1)} collective-permute-done((f32[264,256]{1,0:T(8,128)S(1)}, f32[264,256]{1,0:T(8,128)S(1)}, u32[]{:S(2)}, u32[]{:S(2)}) %collective-permute-start.23) | collective-permute-done | bytes 270368 | tf_op jit(solution)/shard_map/ppermute | solution.py:651
  113.6 2.8 %collective-permute-start.26 = (f32[72,256]{1,0:T(8,128)S(1)}, f32[72,256]{1,0:T(8,128)S(1)}, u32[]{:S(2)}, u32[]{:S(2)}) collective-permute-start(f32[72,256]{1,0:T(8,128)S(1)} %get-tuple-element.144.refs_0_), channel_id=1, source_target_pairs={{0,64},{32,96},{64,0},{96,32},{128,192},{160,224},{192,128},{224,1... | collective-permute-start | bytes 221192 | tf_op jit(solution)/shard_map/ppermute | solution.py:647
  116.9 3.3 %collective-permute-done.27.refs_2_ = f32[72,256]{1,0:T(8,128)S(1)} collective-permute-done((f32[72,256]{1,0:T(8,128)S(1)}, f32[72,256]{1,0:T(8,128)S(1)}, u32[]{:S(2)}, u32[]{:S(2)}) %collective-permute-start.27) | collective-permute-done | bytes 73760 | tf_op jit(solution)/shard_map/ppermute | solution.py:647
  122.0 2.8 %coarse.3 = (f32[128,256]{1,0:T(8,128)S(1)}, f32[128,256]{1,0:T(8,128)S(1)}, f32[128,256]{1,0:T(8,128)S(1)}, f32[128,256]{1,0:T(8,128)S(1)}, f32[128,256]{1,0:T(...) custom-call(s32[1]{0:T(128)} %bitcast.9.x_ref, f32[288,256]{1,0:T(8,128)S(1)} %join.6.half_ref, ...), custom_call_target="tpu_custom_call" | custom-call | flops 629145600 | bytes 3145728 | tf_op jit(solution)/shard_map/coarse/pallas_call | solution.py:66
  126.9 2.6 %collective-permute-start.35 = (f32[128,256]{1,0:T(8,128)S(1)}, f32[128,256]{1,0:T(8,128)S(1)}, u32[]{:S(2)}, u32[]{:S(2)}) collective-permute-start(f32[128,256]{1,0:T(8,128)S(1)} %get-tuple-element.152), channel_id=1, source_target_pairs={{0,3},{1,2},{2,1},{3,0},{4,7},{5,6},{6,5},{7,4},{8,11},{9,10},{10,... | collective-permute-start | bytes 393224 | tf_op jit(solution)/shard_map/ppermute | solution.py:647
  138.4 6.0 %all-to-all-start.1 = ((f32[8,32,256]{2,1,0:T(8,128)}), f32[8,32,256]{2,1,0:T(8,128)S(1)}, u32[]{:S(2)}, u32[]{:S(2)}) async-start(f32[8,32,256]{2,1,0:T(8,128)} %bitcast.23), calls=%async_computation.1 | async-start | bytes 524288 | tf_op jit(solution)/shard_map/all_to_all | solution.py:696
  144.3 8.1 %local.3 = (f32[256,256]{1,0:T(8,128)}, f32[256,256]{1,0:T(8,128)}, f32[256,256]{1,0:T(8,128)}, f32[256,256]{1,0:T(8,128)}) custom-call(bf16[1024,1024]{1,0:T(8,128)(2,1)S(1)} %get-tuple-element.93.onehot_ref, bf16[512,1024]{1,0:T(8,128)(2,1)} %get-tuple-element.154.weighted_in, f32[1024,1024]{1,0:T(8,128)} %bitcast.25, ...), custom_call_target="tpu_custom_call" | custom-call | flops 6442450944 | bytes 8388608 | tf_op jit(solution)/shard_map/local/pallas_call | solution.py:66
  159.0 2.7 %collective-permute-done.37.refs_2_ = f32[32,256]{1,0:T(8,128)S(1)} collective-permute-done((f32[32,256]{1,0:T(8,128)S(1)}, f32[32,256]{1,0:T(8,128)S(1)}, u32[]{:S(2)}, u32[]{:S(2)}) %collective-permute-start.37) | collective-permute-done | bytes 32800 | tf_op jit(solution)/shard_map/ppermute | solution.py:647
  165.6 3.1 %collective-permute-start.41 = (f32[256,256]{1,0:T(8,128)S(1)}, f32[256,256]{1,0:T(8,128)S(1)}, u32[]{:S(2)}, u32[]{:S(2)}) collective-permute-start(f32[256,256]{1,0:T(8,128)S(1)} %get-tuple-element.166.refs_1_), channel_id=1, source_target_pairs={{1,2},{3,4},{5,6},{7,8},{9,10},{11,12},{13,14},{15,16},{17,18},{19... | collective-permute-start | bytes 786440 | tf_op jit(solution)/shard_map/ppermute | solution.py:651
  168.9 3.2 %collective-permute-start.43 = (f32[256,256]{1,0:T(8,128)S(1)}, f32[256,256]{1,0:T(8,128)S(1)}, u32[]{:S(2)}, u32[]{:S(2)}) collective-permute-start(f32[256,256]{1,0:T(8,128)S(1)} %get-tuple-element.168.refs_3_), channel_id=1, source_target_pairs={{32,64},{96,128},{160,192},{64,32},{128,96},{192,160},{33,65},{97,... | collective-permute-start | bytes 786440 | tf_op jit(solution)/shard_map/ppermute | solution.py:651
  173.6 4.4 %collective-permute-done.41.refs_5_ = f32[256,256]{1,0:T(8,128)S(1)} collective-permute-done((f32[256,256]{1,0:T(8,128)S(1)}, f32[256,256]{1,0:T(8,128)S(1)}, u32[]{:S(2)}, u32[]{:S(2)}) %collective-permute-start.41) | collective-permute-done | bytes 262176 | tf_op jit(solution)/shard_map/ppermute | solution.py:651
  (107 shorter events, 81.2 us)
Async XLA Ops:
  3.9 10.3 %collective-permute-start = (f32[264,256]{1,0:T(8,128)S(1)}, f32[264,256]{1,0:T(8,128)S(1)}, u32[]{:S(2)}, u32[]{:S(2)}) collective-permute-start(f32[264,256]{1,0:T(8,128)S(1)} %get-tuple-element.98.refs_0_), channel_id=1, source_target_pairs={{0,1},{1,0},{2,3},{3,2},{4,5},{5,4},{6,7},{7,6},{8,9},{9,8},{10,11... | collective-permute-start | bytes 811016 | tf_op jit(solution)/shard_map/ppermute | solution.py:647
  4.8 11.9 %collective-permute-start.1 = (f32[264,256]{1,0:T(8,128)S(1)}, f32[264,256]{1,0:T(8,128)S(1)}, u32[]{:S(2)}, u32[]{:S(2)}) collective-permute-start(f32[264,256]{1,0:T(8,128)S(1)} %get-tuple-element.99.refs_1_), channel_id=1, source_target_pairs={{1,2},{3,4},{5,6},{7,8},{9,10},{11,12},{13,14},{15,16},{17,18},{19... | collective-permute-start | bytes 811016 | tf_op jit(solution)/shard_map/ppermute | solution.py:651
  9.2 7.5 %collective-permute-start.2 = (f32[264,256]{1,0:T(8,128)S(1)}, f32[264,256]{1,0:T(8,128)S(1)}, u32[]{:S(2)}, u32[]{:S(2)}) collective-permute-start(f32[264,256]{1,0:T(8,128)S(1)} %get-tuple-element.100.refs_2_), channel_id=1, source_target_pairs={{0,32},{32,0},{64,96},{96,64},{128,160},{160,128},{192,224},{224,1... | collective-permute-start | bytes 811016 | tf_op jit(solution)/shard_map/ppermute | solution.py:647
  9.3 7.8 %collective-permute-start.3 = (f32[264,256]{1,0:T(8,128)S(1)}, f32[264,256]{1,0:T(8,128)S(1)}, u32[]{:S(2)}, u32[]{:S(2)}) collective-permute-start(f32[264,256]{1,0:T(8,128)S(1)} %get-tuple-element.101.refs_3_), channel_id=1, source_target_pairs={{32,64},{96,128},{160,192},{64,32},{128,96},{192,160},{33,65},{97,... | collective-permute-start | bytes 811016 | tf_op jit(solution)/shard_map/ppermute | solution.py:651
  33.0 7.6 %collective-permute-start.11 = (f32[128,256]{1,0:T(8,128)S(1)}, f32[128,256]{1,0:T(8,128)S(1)}, u32[]{:S(2)}, u32[]{:S(2)}) collective-permute-start(f32[128,256]{1,0:T(8,128)S(1)} %get-tuple-element.116), channel_id=1, source_target_pairs={{0,3},{1,2},{2,1},{3,0},{4,7},{5,6},{6,5},{7,4},{8,11},{9,10},{10,... | collective-permute-start | bytes 393224 | tf_op jit(solution)/shard_map/ppermute | solution.py:647
  34.3 7.2 %collective-permute-start.8 = (f32[128,256]{1,0:T(8,128)S(1)}, f32[128,256]{1,0:T(8,128)S(1)}, u32[]{:S(2)}, u32[]{:S(2)}) collective-permute-start(f32[128,256]{1,0:T(8,128)S(1)} %get-tuple-element.111), channel_id=1, source_target_pairs={{0,1},{1,0},{2,3},{3,2},{4,5},{5,4},{6,7},{7,6},{8,9},{9,8},{10,11... | collective-permute-start | bytes 393224 | tf_op jit(solution)/shard_map/ppermute | solution.py:647
  35.0 8.4 %collective-permute-start.13 = (f32[128,256]{1,0:T(8,128)S(1)}, f32[128,256]{1,0:T(8,128)S(1)}, u32[]{:S(2)}, u32[]{:S(2)}) collective-permute-start(f32[128,256]{1,0:T(8,128)S(1)} %get-tuple-element.117), channel_id=1, source_target_pairs={{0,3},{1,2},{2,1},{3,0},{4,7},{5,6},{6,5},{7,4},{8,11},{9,10},{10,... | collective-permute-start | bytes 393224 | tf_op jit(solution)/shard_map/ppermute | solution.py:647
  46.5 19.0 %all-to-all-start = ((f32[8,32,256]{2,1,0:T(8,128)}), f32[8,32,256]{2,1,0:T(8,128)S(1)}, u32[]{:S(2)}, u32[]{:S(2)}) async-start(f32[8,32,256]{2,1,0:T(8,128)} %bitcast.22), calls=%async_computation | async-start | bytes 524288 | tf_op jit(solution)/shard_map/all_to_all | solution.py:696
  77.6 12.4 %collective-permute-start.19 = (f32[256,256]{1,0:T(8,128)S(1)}, f32[256,256]{1,0:T(8,128)S(1)}, u32[]{:S(2)}, u32[]{:S(2)}) collective-permute-start(f32[256,256]{1,0:T(8,128)S(1)} %get-tuple-element.136.refs_1_), channel_id=1, source_target_pairs={{1,2},{3,4},{5,6},{7,8},{9,10},{11,12},{13,14},{15,16},{17,18},{19... | collective-permute-start | bytes 786440 | tf_op jit(solution)/shard_map/ppermute | solution.py:651
  80.7 9.3 %collective-permute-start.20 = (f32[256,256]{1,0:T(8,128)S(1)}, f32[256,256]{1,0:T(8,128)S(1)}, u32[]{:S(2)}, u32[]{:S(2)}) collective-permute-start(f32[256,256]{1,0:T(8,128)S(1)} %get-tuple-element.137.refs_2_), channel_id=1, source_target_pairs={{0,32},{32,0},{64,96},{96,64},{128,160},{160,128},{192,224},{224,1... | collective-permute-start | bytes 786440 | tf_op jit(solution)/shard_map/ppermute | solution.py:647
  80.8 9.2 %collective-permute-start.21 = (f32[256,256]{1,0:T(8,128)S(1)}, f32[256,256]{1,0:T(8,128)S(1)}, u32[]{:S(2)}, u32[]{:S(2)}) collective-permute-start(f32[256,256]{1,0:T(8,128)S(1)} %get-tuple-element.138.refs_3_), channel_id=1, source_target_pairs={{32,64},{96,128},{160,192},{64,32},{128,96},{192,160},{33,65},{97,... | collective-permute-start | bytes 786440 | tf_op jit(solution)/shard_map/ppermute | solution.py:651
  83.6 8.3 %collective-permute-start.18 = (f32[256,256]{1,0:T(8,128)S(1)}, f32[256,256]{1,0:T(8,128)S(1)}, u32[]{:S(2)}, u32[]{:S(2)}) collective-permute-start(f32[256,256]{1,0:T(8,128)S(1)} %get-tuple-element.131.refs_0_), channel_id=1, source_target_pairs={{0,1},{1,0},{2,3},{3,2},{4,5},{5,4},{6,7},{7,6},{8,9},{9,8},{10,11... | collective-permute-start | bytes 786440 | tf_op jit(solution)/shard_map/ppermute | solution.py:647
  97.7 7.6 %collective-permute-start.22 = (f32[264,256]{1,0:T(8,128)S(1)}, f32[264,256]{1,0:T(8,128)S(1)}, u32[]{:S(2)}, u32[]{:S(2)}) collective-permute-start(f32[264,256]{1,0:T(8,128)S(1)} %get-tuple-element.140.refs_0_), channel_id=1, source_target_pairs={{0,1},{1,0},{2,3},{3,2},{4,5},{5,4},{6,7},{7,6},{8,9},{9,8},{10,11... | collective-permute-start | bytes 811016 | tf_op jit(solution)/shard_map/ppermute | solution.py:647
  98.1 11.4 %collective-permute-start.23 = (f32[264,256]{1,0:T(8,128)S(1)}, f32[264,256]{1,0:T(8,128)S(1)}, u32[]{:S(2)}, u32[]{:S(2)}) collective-permute-start(f32[264,256]{1,0:T(8,128)S(1)} %get-tuple-element.141.refs_1_), channel_id=1, source_target_pairs={{1,2},{3,4},{5,6},{7,8},{9,10},{11,12},{13,14},{15,16},{17,18},{19... | collective-permute-start | bytes 811016 | tf_op jit(solution)/shard_map/ppermute | solution.py:651
  103.0 7.8 %collective-permute-start.25 = (f32[264,256]{1,0:T(8,128)S(1)}, f32[264,256]{1,0:T(8,128)S(1)}, u32[]{:S(2)}, u32[]{:S(2)}) collective-permute-start(f32[264,256]{1,0:T(8,128)S(1)} %get-tuple-element.143.refs_3_), channel_id=1, source_target_pairs={{32,64},{96,128},{160,192},{64,32},{128,96},{192,160},{33,65},{97,... | collective-permute-start | bytes 811016 | tf_op jit(solution)/shard_map/ppermute | solution.py:651
  113.6 6.7 %collective-permute-start.26 = (f32[72,256]{1,0:T(8,128)S(1)}, f32[72,256]{1,0:T(8,128)S(1)}, u32[]{:S(2)}, u32[]{:S(2)}) collective-permute-start(f32[72,256]{1,0:T(8,128)S(1)} %get-tuple-element.144.refs_0_), channel_id=1, source_target_pairs={{0,64},{32,96},{64,0},{96,32},{128,192},{160,224},{192,128},{224,1... | collective-permute-start | bytes 221192 | tf_op jit(solution)/shard_map/ppermute | solution.py:647
  124.9 7.6 %collective-permute-start.33 = (f32[128,256]{1,0:T(8,128)S(1)}, f32[128,256]{1,0:T(8,128)S(1)}, u32[]{:S(2)}, u32[]{:S(2)}) collective-permute-start(f32[128,256]{1,0:T(8,128)S(1)} %get-tuple-element.151), channel_id=1, source_target_pairs={{0,3},{1,2},{2,1},{3,0},{4,7},{5,6},{6,5},{7,4},{8,11},{9,10},{10,... | collective-permute-start | bytes 393224 | tf_op jit(solution)/shard_map/ppermute | solution.py:647
  126.3 7.1 %collective-permute-start.30 = (f32[128,256]{1,0:T(8,128)S(1)}, f32[128,256]{1,0:T(8,128)S(1)}, u32[]{:S(2)}, u32[]{:S(2)}) collective-permute-start(f32[128,256]{1,0:T(8,128)S(1)} %get-tuple-element.146), channel_id=1, source_target_pairs={{0,1},{1,0},{2,3},{3,2},{4,5},{5,4},{6,7},{7,6},{8,9},{9,8},{10,11... | collective-permute-start | bytes 393224 | tf_op jit(solution)/shard_map/ppermute | solution.py:647
  126.9 8.4 %collective-permute-start.35 = (f32[128,256]{1,0:T(8,128)S(1)}, f32[128,256]{1,0:T(8,128)S(1)}, u32[]{:S(2)}, u32[]{:S(2)}) collective-permute-start(f32[128,256]{1,0:T(8,128)S(1)} %get-tuple-element.152), channel_id=1, source_target_pairs={{0,3},{1,2},{2,1},{3,0},{4,7},{5,6},{6,5},{7,4},{8,11},{9,10},{10,... | collective-permute-start | bytes 393224 | tf_op jit(solution)/shard_map/ppermute | solution.py:647
  138.4 16.5 %all-to-all-start.1 = ((f32[8,32,256]{2,1,0:T(8,128)}), f32[8,32,256]{2,1,0:T(8,128)S(1)}, u32[]{:S(2)}, u32[]{:S(2)}) async-start(f32[8,32,256]{2,1,0:T(8,128)} %bitcast.23), calls=%async_computation.1 | async-start | bytes 524288 | tf_op jit(solution)/shard_map/all_to_all | solution.py:696
  165.6 12.4 %collective-permute-start.41 = (f32[256,256]{1,0:T(8,128)S(1)}, f32[256,256]{1,0:T(8,128)S(1)}, u32[]{:S(2)}, u32[]{:S(2)}) collective-permute-start(f32[256,256]{1,0:T(8,128)S(1)} %get-tuple-element.166.refs_1_), channel_id=1, source_target_pairs={{1,2},{3,4},{5,6},{7,8},{9,10},{11,12},{13,14},{15,16},{17,18},{19... | collective-permute-start | bytes 786440 | tf_op jit(solution)/shard_map/ppermute | solution.py:651
  168.8 9.2 %collective-permute-start.42 = (f32[256,256]{1,0:T(8,128)S(1)}, f32[256,256]{1,0:T(8,128)S(1)}, u32[]{:S(2)}, u32[]{:S(2)}) collective-permute-start(f32[256,256]{1,0:T(8,128)S(1)} %get-tuple-element.167.refs_2_), channel_id=1, source_target_pairs={{0,32},{32,0},{64,96},{96,64},{128,160},{160,128},{192,224},{224,1... | collective-permute-start | bytes 786440 | tf_op jit(solution)/shard_map/ppermute | solution.py:647
  168.9 9.1 %collective-permute-start.43 = (f32[256,256]{1,0:T(8,128)S(1)}, f32[256,256]{1,0:T(8,128)S(1)}, u32[]{:S(2)}, u32[]{:S(2)}) collective-permute-start(f32[256,256]{1,0:T(8,128)S(1)} %get-tuple-element.168.refs_3_), channel_id=1, source_target_pairs={{32,64},{96,128},{160,192},{64,32},{128,96},{192,160},{33,65},{97,... | collective-permute-start | bytes 786440 | tf_op jit(solution)/shard_map/ppermute | solution.py:651
  172.1 8.1 %collective-permute-start.40 = (f32[256,256]{1,0:T(8,128)S(1)}, f32[256,256]{1,0:T(8,128)S(1)}, u32[]{:S(2)}, u32[]{:S(2)}) collective-permute-start(f32[256,256]{1,0:T(8,128)S(1)} %get-tuple-element.164.refs_0_), channel_id=1, source_target_pairs={{0,1},{1,0},{2,3},{3,2},{4,5},{5,4},{6,7},{7,6},{8,9},{9,8},{10,11... | collective-permute-start | bytes 786440 | tf_op jit(solution)/shard_map/ppermute | solution.py:647
  (27 other events, 232.4 us)

commit v5 on v4

--- a/solution.py
+++ b/solution.py
@@ -411,11 +411,27 @@
     return out
 
 
-def update_kernel(n_grp, at_ref, map_ref, half_ref, other_ref, lift_in, *rest):
-    near_in, outs = rest[:FACES], rest[FACES : 2 * FACES]
-    lift, near, sems = rest[2 * FACES :]
-    lift_copy = fetched(lift_in, lift, sems.at[FACES])
-    copies = [fetched(near_in[p], near.at[p], sems.at[p]) for p in range(FACES)]
+def bring_kernel(lift_in, *refs):
+    near_in, (lift_ref, near_ref, sems) = refs[:FACES], refs[FACES:]
+    copies = [fetched(lift_in, lift_ref, sems.at[FACES])]
+    copies += [fetched(near_in[p], near_ref.at[p], sems.at[p]) for p in range(FACES)]
+    for copy in copies:
+        copy.wait()
+
+
+def bring_call(lift, near):
+    return call(
+        bring_kernel,
+        "bring",
+        [shaped(LOCAL, INTERFACE), shaped(FACES, COLUMNS, FACE_ROWS)],
+        1 << 20,
+        2 << 20,
+        [HBM] * (1 + FACES),
+        scratch=[pltpu.SemaphoreType.DMA((FACES + 1,))],
+    )(lift, *near)
+
+
+def update_kernel(n_grp, at_ref, map_ref, half_ref, other_ref, lift, near, *outs):
     dofs = n_grp * OWNED
     index = lax.broadcasted_iota(jnp.int32, (dofs, LOCAL), 0)
     block, inside = index // OWNED, index % OWNED
@@ -426,9 +442,7 @@
     onehot = (ids == map_ref[:1, :LOCAL]).astype(jnp.float32).astype(jnp.bfloat16)
     pair = mul(onehot, both, TN)
     own = split(pair[:, :COLUMNS] + pair[:, COLUMNS:])
-    lift_copy.wait()
-    for p in range(FACES):
-        copies[p].wait()
+    for p in range(FACES):
         outs[p][...] = near[p] + mul3(own, split(lift[:, face_at(p)]), TN)
 
 
@@ -439,13 +453,8 @@
         [shaped(COLUMNS, FACE_ROWS)] * FACES,
         300 << 20,
         3 << 20,
-        [SMEM] + [VMEM] * 3 + [HBM] * (1 + FACES),
-        scratch=[
-            pltpu.VMEM((LOCAL, INTERFACE), jnp.float32),
-            pltpu.VMEM((FACES, COLUMNS, FACE_ROWS), jnp.float32),
-            pltpu.SemaphoreType.DMA((FACES + 1,)),
-        ],
-    )(at, map_row, half, other, lift, *near)
+        [SMEM] + [VMEM] * 5,
+    )(at, map_row, half, other, lift, near)
 
 
 def matrix_copy(matrix_in, matrix, sems, t):
@@ -701,7 +710,8 @@
         total, *near = lax.optimization_barrier((total, *near))
         owned = sum_call(total.reshape(nz * OWNED, COLUMNS))
         half, other = group_gather(owned)
-        near = update_call(at, map_row, half, other, lift, near, n_grp)
+        *near, _ = lax.optimization_barrier((*near, half))
+        near = update_call(at, map_row, half, other, *bring_call(lift, near), n_grp)
         far = exchange(near)
         if first:
             matrix, _ = lax.optimization_barrier((schur, near[0]))

time: 184 us -> 182 us (0.989)
  waiting for transfers between devices: 60.3 us -> 58.1 us
    ppermute x36, waiting for transfers between devices: 39.2 us -> 36.5 us  [swap(): return lax.ppermute(value, axis, [(i, i ^ k) for i in range(size)])]
    pallas_call x26 -> x28, Pallas kernels: 50.5 us -> 49.8 us  [run(): return function(*values)]
  transfers between devices with their start and end apart: 46 -> 46, of which waited for: 33 -> 31; matrix products, arithmetic and copies ran while one was open for 0% -> 0% of each run, Pallas kernels for 12% -> 14%
where the time goes in v5:
time: 182 us; the launch traced here: 180 us
  starting transfers between devices  71.1 us (39%)
  waiting for transfers between devices  58.1 us (32%)
  Pallas kernels  49.8 us (27%)
    pallas_call x28, Pallas kernels, run(): return function(*values)  49.8 us
    ppermute x36, waiting for transfers between devices, swap(): return lax.ppermute(value, axis, [(i, i ^ k) for i in range(size)])  36.5 us
    ppermute x36, starting transfers between devices, swap(): return lax.ppermute(value, axis, [(i, i ^ k) for i in range(size)])  31.1 us
    ppermute x8, starting transfers between devices, swap_next(): lax.ppermute(value, axis, [(i, i + 1) for i in lower] + [(i + 1, i) for i...  25.5 us
    ppermute x8, waiting for transfers between devices, swap_next(): lax.ppermute(value, axis, [(i, i + 1) for i in lower] + [(i + 1, i) for i...  16.7 us
    all_to_all x2, starting transfers between devices, on_device(): lax.all_to_all(total.reshape(nz, OWNED, COLUMNS), 'dev', 0, 0, axis_index...  14.5 us
    all_to_all x2, waiting for transfers between devices, on_device(): lax.all_to_all(total.reshape(nz, OWNED, COLUMNS), 'dev', 0, 0, axis_index...  4.89 us
  transfers between devices with their start and end apart: 46, of which 31 were waited for; matrix products, arithmetic and copies ran while one was open for 0% of the time, Pallas kernels for 14%

profile of v5, /device:TPU:14, one launch (start us, length us, event | category | flops | bytes accessed | tf_op | source)
XLA Modules:
  0.0 179.7 jit_solution(9118405818002947491)
XLA Ops:
  0.1 3.7 %pack.1 = (f32[64,1024]{1,0:T(8,128)S(1)}, bf16[1024,1024]{1,0:T(8,128)(2,1)S(1)}, f32[264,256]{1,0:T(8,128)S(1)}, f32[264,256]{1,0:T(8,128)S(1)}, f32[264,256]{1,0:T(8,128)S(1)}, /*index=5*/f32[264,256]{1,0:T(8,128)S(1)}) custom-call(s32[2]{0:T(128)S(1)} %pad_add_fusion.odd_ref, s32[4,256]{1,0:T(4,128)} %bitcast.28, f32[1024,256]{1,0:T(8,128)} %bitcast.26, ...), custom_call_target="tpu_custom_call" | custom-call | flops 2147483648 | bytes 4194304 | tf_op jit(solution)/shard_map/pack/pallas_call | solution.py:66
  4.8 4.4 %collective-permute-start.1 = (f32[264,256]{1,0:T(8,128)S(1)}, f32[264,256]{1,0:T(8,128)S(1)}, u32[]{:S(2)}, u32[]{:S(2)}) collective-permute-start(f32[264,256]{1,0:T(8,128)S(1)} %get-tuple-element.111.refs_1_), channel_id=1, source_target_pairs={{1,2},{3,4},{5,6},{7,8},{9,10},{11,12},{13,14},{15,16},{17,18},{19... | collective-permute-start | bytes 811016 | tf_op jit(solution)/shard_map/ppermute | solution.py:660
  23.2 3.5 %collective-permute-done.5.refs_2_ = f32[72,256]{1,0:T(8,128)S(1)} collective-permute-done((f32[72,256]{1,0:T(8,128)S(1)}, f32[72,256]{1,0:T(8,128)S(1)}, u32[]{:S(2)}, u32[]{:S(2)}) %collective-permute-start.5) | collective-permute-done | bytes 73760 | tf_op jit(solution)/shard_map/ppermute | solution.py:656
  29.4 3.5 %coarse.2 = (f32[128,256]{1,0:T(8,128)S(1)}, f32[128,256]{1,0:T(8,128)S(1)}, f32[128,256]{1,0:T(8,128)S(1)}, f32[128,256]{1,0:T(8,128)S(1)}, f32[128,256]{1,0:T(...) custom-call(s32[1]{0:T(128)} %bitcast.9.x_ref, f32[288,256]{1,0:T(8,128)} %join.4.half_ref, ...), custom_call_target="tpu_custom_call" | custom-call | flops 629145600 | bytes 3145728 | tf_op jit(solution)/shard_map/coarse/pallas_call | solution.py:66
  35.1 2.6 %collective-permute-start.13 = (f32[128,256]{1,0:T(8,128)S(1)}, f32[128,256]{1,0:T(8,128)S(1)}, u32[]{:S(2)}, u32[]{:S(2)}) collective-permute-start(f32[128,256]{1,0:T(8,128)S(1)} %get-tuple-element.129), channel_id=1, source_target_pairs={{0,3},{1,2},{2,1},{3,0},{4,7},{5,6},{6,5},{7,4},{8,11},{9,10},{10,... | collective-permute-start | bytes 393224 | tf_op jit(solution)/shard_map/ppermute | solution.py:656
  46.5 8.5 %all-to-all-start = ((f32[8,32,256]{2,1,0:T(8,128)}), f32[8,32,256]{2,1,0:T(8,128)S(1)}, u32[]{:S(2)}, u32[]{:S(2)}) async-start(f32[8,32,256]{2,1,0:T(8,128)} %bitcast.22), calls=%async_computation | async-start | bytes 524288 | tf_op jit(solution)/shard_map/all_to_all | solution.py:705
  55.0 8.0 %local.2 = (f32[256,256]{1,0:T(8,128)}, f32[256,256]{1,0:T(8,128)}, f32[256,256]{1,0:T(8,128)}, f32[256,256]{1,0:T(8,128)}) custom-call(bf16[1024,1024]{1,0:T(8,128)(2,1)S(1)} %get-tuple-element.105.onehot_ref, bf16[512,1024]{1,0:T(8,128)(2,1)} %get-tuple-element.131.weighted_in, f32[1024,1024]{1,0:T(8,128)} %bitcast.24, ...), custom_call_target="tpu_custom_call" | custom-call | flops 6442450944 | bytes 8388608 | tf_op jit(solution)/shard_map/local/pallas_call | solution.py:66
  69.7 3.2 %collective-permute-done.15.refs_2_ = f32[32,256]{1,0:T(8,128)S(1)} collective-permute-done((f32[32,256]{1,0:T(8,128)S(1)}, f32[32,256]{1,0:T(8,128)S(1)}, u32[]{:S(2)}, u32[]{:S(2)}) %collective-permute-start.15) | collective-permute-done | bytes 32800 | tf_op jit(solution)/shard_map/ppermute | solution.py:656
  75.8 3.1 %collective-permute-start.19 = (f32[256,256]{1,0:T(8,128)S(1)}, f32[256,256]{1,0:T(8,128)S(1)}, u32[]{:S(2)}, u32[]{:S(2)}) collective-permute-start(f32[256,256]{1,0:T(8,128)S(1)} %get-tuple-element.154.refs_1_), channel_id=1, source_target_pairs={{1,2},{3,4},{5,6},{7,8},{9,10},{11,12},{13,14},{15,16},{17,18},{19... | collective-permute-start | bytes 786440 | tf_op jit(solution)/shard_map/ppermute | solution.py:660
  82.1 2.7 %ready.1 = (f32[4,264,256]{2,1,0:T(8,128)S(1)}, bf16[1024,1024]{1,0:T(8,128)(2,1)S(1)}, bf16[1024,1024]{1,0:T(8,128)(2,1)S(1)}) custom-call(f32[264,256]{1,0:T(8,128)} %copy-done, f32[264,256]{1,0:T(8,128)} %copy-done.1, f32[264,256]{1,0:T(8,128)} %copy-done.2, f32[264,256]{1,0:T(8,128)} %copy-done.3, f32[1024,1024]{1,0:T(8,128)} %bitcast.20), custom_call_target="tpu_custom_call" | custom-call | flops 4194304 | bytes 8388608 | tf_op jit(solution)/shard_map/ready/pallas_call | solution.py:66
  84.8 3.7 %collective-permute-done.19.refs_5_ = f32[256,256]{1,0:T(8,128)S(1)} collective-permute-done((f32[256,256]{1,0:T(8,128)S(1)}, f32[256,256]{1,0:T(8,128)S(1)}, u32[]{:S(2)}, u32[]{:S(2)}) %collective-permute-start.19) | collective-permute-done | bytes 262176 | tf_op jit(solution)/shard_map/ppermute | solution.py:660
  90.3 5.8 %middle.1 = (f32[4,256,256]{2,1,0:T(8,128)}, f32[264,256]{1,0:T(8,128)S(1)}, f32[264,256]{1,0:T(8,128)S(1)}, f32[264,256]{1,0:T(8,128)S(1)}, f32[264,256]{1,0:T(8,128)S(1)}) custom-call(bf16[1024,1024]{1,0:T(8,128)(2,1)S(1)} %get-tuple-element.105.onehot_ref, f32[4,264,256]{2,1,0:T(8,128)S(1)} %get-tuple-element.151.gradient_ref, ...), custom_call_target="tpu_custom_call" | custom-call | flops 6442450944 | bytes 12582912 | tf_op jit(solution)/shard_map/middle/pallas_call | solution.py:66
  96.5 4.8 %collective-permute-start.23 = (f32[264,256]{1,0:T(8,128)S(1)}, f32[264,256]{1,0:T(8,128)S(1)}, u32[]{:S(2)}, u32[]{:S(2)}) collective-permute-start(f32[264,256]{1,0:T(8,128)S(1)} %get-tuple-element.159.refs_1_), channel_id=1, source_target_pairs={{1,2},{3,4},{5,6},{7,8},{9,10},{11,12},{13,14},{15,16},{17,18},{19... | collective-permute-start | bytes 811016 | tf_op jit(solution)/shard_map/ppermute | solution.py:660
  104.0 4.1 %collective-permute-done.23.refs_5_ = f32[264,256]{1,0:T(8,128)S(1)} collective-permute-done((f32[264,256]{1,0:T(8,128)S(1)}, f32[264,256]{1,0:T(8,128)S(1)}, u32[]{:S(2)}, u32[]{:S(2)}) %collective-permute-start.23) | collective-permute-done | bytes 270368 | tf_op jit(solution)/shard_map/ppermute | solution.py:660
  112.0 2.8 %collective-permute-start.26 = (f32[72,256]{1,0:T(8,128)S(1)}, f32[72,256]{1,0:T(8,128)S(1)}, u32[]{:S(2)}, u32[]{:S(2)}) collective-permute-start(f32[72,256]{1,0:T(8,128)S(1)} %get-tuple-element.162.refs_0_), channel_id=1, source_target_pairs={{0,64},{32,96},{64,0},{96,32},{128,192},{160,224},{192,128},{224,1... | collective-permute-start | bytes 221192 | tf_op jit(solution)/shard_map/ppermute | solution.py:656
  115.3 3.3 %collective-permute-done.27.refs_2_ = f32[72,256]{1,0:T(8,128)S(1)} collective-permute-done((f32[72,256]{1,0:T(8,128)S(1)}, f32[72,256]{1,0:T(8,128)S(1)}, u32[]{:S(2)}, u32[]{:S(2)}) %collective-permute-start.27) | collective-permute-done | bytes 73760 | tf_op jit(solution)/shard_map/ppermute | solution.py:656
  120.6 2.8 %coarse.3 = (f32[128,256]{1,0:T(8,128)S(1)}, f32[128,256]{1,0:T(8,128)S(1)}, f32[128,256]{1,0:T(8,128)S(1)}, f32[128,256]{1,0:T(8,128)S(1)}, f32[128,256]{1,0:T(...) custom-call(s32[1]{0:T(128)} %bitcast.9.x_ref, f32[288,256]{1,0:T(8,128)S(1)} %join.6.half_ref, ...), custom_call_target="tpu_custom_call" | custom-call | flops 629145600 | bytes 3145728 | tf_op jit(solution)/shard_map/coarse/pallas_call | solution.py:66
  125.5 2.6 %collective-permute-start.35 = (f32[128,256]{1,0:T(8,128)S(1)}, f32[128,256]{1,0:T(8,128)S(1)}, u32[]{:S(2)}, u32[]{:S(2)}) collective-permute-start(f32[128,256]{1,0:T(8,128)S(1)} %get-tuple-element.170), channel_id=1, source_target_pairs={{0,3},{1,2},{2,1},{3,0},{4,7},{5,6},{6,5},{7,4},{8,11},{9,10},{10,... | collective-permute-start | bytes 393224 | tf_op jit(solution)/shard_map/ppermute | solution.py:656
  137.0 6.0 %all-to-all-start.1 = ((f32[8,32,256]{2,1,0:T(8,128)}), f32[8,32,256]{2,1,0:T(8,128)S(1)}, u32[]{:S(2)}, u32[]{:S(2)}) async-start(f32[8,32,256]{2,1,0:T(8,128)} %bitcast.23), calls=%async_computation.1 | async-start | bytes 524288 | tf_op jit(solution)/shard_map/all_to_all | solution.py:705
  143.0 8.0 %local.3 = (f32[256,256]{1,0:T(8,128)}, f32[256,256]{1,0:T(8,128)}, f32[256,256]{1,0:T(8,128)}, f32[256,256]{1,0:T(8,128)}) custom-call(bf16[1024,1024]{1,0:T(8,128)(2,1)S(1)} %get-tuple-element.105.onehot_ref, bf16[512,1024]{1,0:T(8,128)(2,1)} %get-tuple-element.172.weighted_in, f32[1024,1024]{1,0:T(8,128)} %bitcast.25, ...), custom_call_target="tpu_custom_call" | custom-call | flops 6442450944 | bytes 8388608 | tf_op jit(solution)/shard_map/local/pallas_call | solution.py:66
  157.7 2.6 %collective-permute-done.37.refs_2_ = f32[32,256]{1,0:T(8,128)S(1)} collective-permute-done((f32[32,256]{1,0:T(8,128)S(1)}, f32[32,256]{1,0:T(8,128)S(1)}, u32[]{:S(2)}, u32[]{:S(2)}) %collective-permute-start.37) | collective-permute-done | bytes 32800 | tf_op jit(solution)/shard_map/ppermute | solution.py:656
  162.6 3.1 %collective-permute-start.41 = (f32[256,256]{1,0:T(8,128)S(1)}, f32[256,256]{1,0:T(8,128)S(1)}, u32[]{:S(2)}, u32[]{:S(2)}) collective-permute-start(f32[256,256]{1,0:T(8,128)S(1)} %get-tuple-element.190.refs_1_), channel_id=1, source_target_pairs={{1,2},{3,4},{5,6},{7,8},{9,10},{11,12},{13,14},{15,16},{17,18},{19... | collective-permute-start | bytes 786440 | tf_op jit(solution)/shard_map/ppermute | solution.py:660
  166.1 3.1 %collective-permute-start.43 = (f32[256,256]{1,0:T(8,128)S(1)}, f32[256,256]{1,0:T(8,128)S(1)}, u32[]{:S(2)}, u32[]{:S(2)}) collective-permute-start(f32[256,256]{1,0:T(8,128)S(1)} %get-tuple-element.192.refs_3_), channel_id=1, source_target_pairs={{32,64},{96,128},{160,192},{64,32},{128,96},{192,160},{33,65},{97,... | collective-permute-start | bytes 786440 | tf_op jit(solution)/shard_map/ppermute | solution.py:660
  170.6 4.7 %collective-permute-done.41.refs_5_ = f32[256,256]{1,0:T(8,128)S(1)} collective-permute-done((f32[256,256]{1,0:T(8,128)S(1)}, f32[256,256]{1,0:T(8,128)S(1)}, u32[]{:S(2)}, u32[]{:S(2)}) %collective-permute-start.41) | collective-permute-done | bytes 262176 | tf_op jit(solution)/shard_map/ppermute | solution.py:660
  (109 shorter events, 78.1 us)
Async XLA Ops:
  3.9 10.2 %collective-permute-start = (f32[264,256]{1,0:T(8,128)S(1)}, f32[264,256]{1,0:T(8,128)S(1)}, u32[]{:S(2)}, u32[]{:S(2)}) collective-permute-start(f32[264,256]{1,0:T(8,128)S(1)} %get-tuple-element.110.refs_0_), channel_id=1, source_target_pairs={{0,1},{1,0},{2,3},{3,2},{4,5},{5,4},{6,7},{7,6},{8,9},{9,8},{10,11... | collective-permute-start | bytes 811016 | tf_op jit(solution)/shard_map/ppermute | solution.py:656
  4.8 11.9 %collective-permute-start.1 = (f32[264,256]{1,0:T(8,128)S(1)}, f32[264,256]{1,0:T(8,128)S(1)}, u32[]{:S(2)}, u32[]{:S(2)}) collective-permute-start(f32[264,256]{1,0:T(8,128)S(1)} %get-tuple-element.111.refs_1_), channel_id=1, source_target_pairs={{1,2},{3,4},{5,6},{7,8},{9,10},{11,12},{13,14},{15,16},{17,18},{19... | collective-permute-start | bytes 811016 | tf_op jit(solution)/shard_map/ppermute | solution.py:660
  9.2 7.5 %collective-permute-start.2 = (f32[264,256]{1,0:T(8,128)S(1)}, f32[264,256]{1,0:T(8,128)S(1)}, u32[]{:S(2)}, u32[]{:S(2)}) collective-permute-start(f32[264,256]{1,0:T(8,128)S(1)} %get-tuple-element.112.refs_2_), channel_id=1, source_target_pairs={{0,32},{32,0},{64,96},{96,64},{128,160},{160,128},{192,224},{224,1... | collective-permute-start | bytes 811016 | tf_op jit(solution)/shard_map/ppermute | solution.py:656
  9.3 7.8 %collective-permute-start.3 = (f32[264,256]{1,0:T(8,128)S(1)}, f32[264,256]{1,0:T(8,128)S(1)}, u32[]{:S(2)}, u32[]{:S(2)}) collective-permute-start(f32[264,256]{1,0:T(8,128)S(1)} %get-tuple-element.113.refs_3_), channel_id=1, source_target_pairs={{32,64},{96,128},{160,192},{64,32},{128,96},{192,160},{33,65},{97,... | collective-permute-start | bytes 811016 | tf_op jit(solution)/shard_map/ppermute | solution.py:660
  33.0 7.6 %collective-permute-start.11 = (f32[128,256]{1,0:T(8,128)S(1)}, f32[128,256]{1,0:T(8,128)S(1)}, u32[]{:S(2)}, u32[]{:S(2)}) collective-permute-start(f32[128,256]{1,0:T(8,128)S(1)} %get-tuple-element.128), channel_id=1, source_target_pairs={{0,3},{1,2},{2,1},{3,0},{4,7},{5,6},{6,5},{7,4},{8,11},{9,10},{10,... | collective-permute-start | bytes 393224 | tf_op jit(solution)/shard_map/ppermute | solution.py:656
  34.4 7.2 %collective-permute-start.8 = (f32[128,256]{1,0:T(8,128)S(1)}, f32[128,256]{1,0:T(8,128)S(1)}, u32[]{:S(2)}, u32[]{:S(2)}) collective-permute-start(f32[128,256]{1,0:T(8,128)S(1)} %get-tuple-element.123), channel_id=1, source_target_pairs={{0,1},{1,0},{2,3},{3,2},{4,5},{5,4},{6,7},{7,6},{8,9},{9,8},{10,11... | collective-permute-start | bytes 393224 | tf_op jit(solution)/shard_map/ppermute | solution.py:656
  35.1 8.4 %collective-permute-start.13 = (f32[128,256]{1,0:T(8,128)S(1)}, f32[128,256]{1,0:T(8,128)S(1)}, u32[]{:S(2)}, u32[]{:S(2)}) collective-permute-start(f32[128,256]{1,0:T(8,128)S(1)} %get-tuple-element.129), channel_id=1, source_target_pairs={{0,3},{1,2},{2,1},{3,0},{4,7},{5,6},{6,5},{7,4},{8,11},{9,10},{10,... | collective-permute-start | bytes 393224 | tf_op jit(solution)/shard_map/ppermute | solution.py:656
  46.5 19.0 %all-to-all-start = ((f32[8,32,256]{2,1,0:T(8,128)}), f32[8,32,256]{2,1,0:T(8,128)S(1)}, u32[]{:S(2)}, u32[]{:S(2)}) async-start(f32[8,32,256]{2,1,0:T(8,128)} %bitcast.22), calls=%async_computation | async-start | bytes 524288 | tf_op jit(solution)/shard_map/all_to_all | solution.py:705
  75.8 12.7 %collective-permute-start.19 = (f32[256,256]{1,0:T(8,128)S(1)}, f32[256,256]{1,0:T(8,128)S(1)}, u32[]{:S(2)}, u32[]{:S(2)}) collective-permute-start(f32[256,256]{1,0:T(8,128)S(1)} %get-tuple-element.154.refs_1_), channel_id=1, source_target_pairs={{1,2},{3,4},{5,6},{7,8},{9,10},{11,12},{13,14},{15,16},{17,18},{19... | collective-permute-start | bytes 786440 | tf_op jit(solution)/shard_map/ppermute | solution.py:660
  79.0 9.6 %collective-permute-start.20 = (f32[256,256]{1,0:T(8,128)S(1)}, f32[256,256]{1,0:T(8,128)S(1)}, u32[]{:S(2)}, u32[]{:S(2)}) collective-permute-start(f32[256,256]{1,0:T(8,128)S(1)} %get-tuple-element.155.refs_2_), channel_id=1, source_target_pairs={{0,32},{32,0},{64,96},{96,64},{128,160},{160,128},{192,224},{224,1... | collective-permute-start | bytes 786440 | tf_op jit(solution)/shard_map/ppermute | solution.py:656
  79.3 9.3 %collective-permute-start.21 = (f32[256,256]{1,0:T(8,128)S(1)}, f32[256,256]{1,0:T(8,128)S(1)}, u32[]{:S(2)}, u32[]{:S(2)}) collective-permute-start(f32[256,256]{1,0:T(8,128)S(1)} %get-tuple-element.156.refs_3_), channel_id=1, source_target_pairs={{32,64},{96,128},{160,192},{64,32},{128,96},{192,160},{33,65},{97,... | collective-permute-start | bytes 786440 | tf_op jit(solution)/shard_map/ppermute | solution.py:660
  81.9 8.5 %collective-permute-start.18 = (f32[256,256]{1,0:T(8,128)S(1)}, f32[256,256]{1,0:T(8,128)S(1)}, u32[]{:S(2)}, u32[]{:S(2)}) collective-permute-start(f32[256,256]{1,0:T(8,128)S(1)} %get-tuple-element.149.refs_0_), channel_id=1, source_target_pairs={{0,1},{1,0},{2,3},{3,2},{4,5},{5,4},{6,7},{7,6},{8,9},{9,8},{10,11... | collective-permute-start | bytes 786440 | tf_op jit(solution)/shard_map/ppermute | solution.py:656
  96.2 7.8 %collective-permute-start.22 = (f32[264,256]{1,0:T(8,128)S(1)}, f32[264,256]{1,0:T(8,128)S(1)}, u32[]{:S(2)}, u32[]{:S(2)}) collective-permute-start(f32[264,256]{1,0:T(8,128)S(1)} %get-tuple-element.158.refs_0_), channel_id=1, source_target_pairs={{0,1},{1,0},{2,3},{3,2},{4,5},{5,4},{6,7},{7,6},{8,9},{9,8},{10,11... | collective-permute-start | bytes 811016 | tf_op jit(solution)/shard_map/ppermute | solution.py:656
  96.5 11.6 %collective-permute-start.23 = (f32[264,256]{1,0:T(8,128)S(1)}, f32[264,256]{1,0:T(8,128)S(1)}, u32[]{:S(2)}, u32[]{:S(2)}) collective-permute-start(f32[264,256]{1,0:T(8,128)S(1)} %get-tuple-element.159.refs_1_), channel_id=1, source_target_pairs={{1,2},{3,4},{5,6},{7,8},{9,10},{11,12},{13,14},{15,16},{17,18},{19... | collective-permute-start | bytes 811016 | tf_op jit(solution)/shard_map/ppermute | solution.py:660
  101.4 6.8 %collective-permute-start.24 = (f32[264,256]{1,0:T(8,128)S(1)}, f32[264,256]{1,0:T(8,128)S(1)}, u32[]{:S(2)}, u32[]{:S(2)}) collective-permute-start(f32[264,256]{1,0:T(8,128)S(1)} %get-tuple-element.160.refs_2_), channel_id=1, source_target_pairs={{0,32},{32,0},{64,96},{96,64},{128,160},{160,128},{192,224},{224,1... | collective-permute-start | bytes 811016 | tf_op jit(solution)/shard_map/ppermute | solution.py:656
  101.5 7.8 %collective-permute-start.25 = (f32[264,256]{1,0:T(8,128)S(1)}, f32[264,256]{1,0:T(8,128)S(1)}, u32[]{:S(2)}, u32[]{:S(2)}) collective-permute-start(f32[264,256]{1,0:T(8,128)S(1)} %get-tuple-element.161.refs_3_), channel_id=1, source_target_pairs={{32,64},{96,128},{160,192},{64,32},{128,96},{192,160},{33,65},{97,... | collective-permute-start | bytes 811016 | tf_op jit(solution)/shard_map/ppermute | solution.py:660
  123.5 7.6 %collective-permute-start.33 = (f32[128,256]{1,0:T(8,128)S(1)}, f32[128,256]{1,0:T(8,128)S(1)}, u32[]{:S(2)}, u32[]{:S(2)}) collective-permute-start(f32[128,256]{1,0:T(8,128)S(1)} %get-tuple-element.169), channel_id=1, source_target_pairs={{0,3},{1,2},{2,1},{3,0},{4,7},{5,6},{6,5},{7,4},{8,11},{9,10},{10,... | collective-permute-start | bytes 393224 | tf_op jit(solution)/shard_map/ppermute | solution.py:656
  125.0 7.1 %collective-permute-start.30 = (f32[128,256]{1,0:T(8,128)S(1)}, f32[128,256]{1,0:T(8,128)S(1)}, u32[]{:S(2)}, u32[]{:S(2)}) collective-permute-start(f32[128,256]{1,0:T(8,128)S(1)} %get-tuple-element.164), channel_id=1, source_target_pairs={{0,1},{1,0},{2,3},{3,2},{4,5},{5,4},{6,7},{7,6},{8,9},{9,8},{10,11... | collective-permute-start | bytes 393224 | tf_op jit(solution)/shard_map/ppermute | solution.py:656
  125.5 8.4 %collective-permute-start.35 = (f32[128,256]{1,0:T(8,128)S(1)}, f32[128,256]{1,0:T(8,128)S(1)}, u32[]{:S(2)}, u32[]{:S(2)}) collective-permute-start(f32[128,256]{1,0:T(8,128)S(1)} %get-tuple-element.170), channel_id=1, source_target_pairs={{0,3},{1,2},{2,1},{3,0},{4,7},{5,6},{6,5},{7,4},{8,11},{9,10},{10,... | collective-permute-start | bytes 393224 | tf_op jit(solution)/shard_map/ppermute | solution.py:656
  137.0 16.5 %all-to-all-start.1 = ((f32[8,32,256]{2,1,0:T(8,128)}), f32[8,32,256]{2,1,0:T(8,128)S(1)}, u32[]{:S(2)}, u32[]{:S(2)}) async-start(f32[8,32,256]{2,1,0:T(8,128)} %bitcast.23), calls=%async_computation.1 | async-start | bytes 524288 | tf_op jit(solution)/shard_map/all_to_all | solution.py:705
  162.6 12.7 %collective-permute-start.41 = (f32[256,256]{1,0:T(8,128)S(1)}, f32[256,256]{1,0:T(8,128)S(1)}, u32[]{:S(2)}, u32[]{:S(2)}) collective-permute-start(f32[256,256]{1,0:T(8,128)S(1)} %get-tuple-element.190.refs_1_), channel_id=1, source_target_pairs={{1,2},{3,4},{5,6},{7,8},{9,10},{11,12},{13,14},{15,16},{17,18},{19... | collective-permute-start | bytes 786440 | tf_op jit(solution)/shard_map/ppermute | solution.py:660
  165.8 9.6 %collective-permute-start.42 = (f32[256,256]{1,0:T(8,128)S(1)}, f32[256,256]{1,0:T(8,128)S(1)}, u32[]{:S(2)}, u32[]{:S(2)}) collective-permute-start(f32[256,256]{1,0:T(8,128)S(1)} %get-tuple-element.191.refs_2_), channel_id=1, source_target_pairs={{0,32},{32,0},{64,96},{96,64},{128,160},{160,128},{192,224},{224,1... | collective-permute-start | bytes 786440 | tf_op jit(solution)/shard_map/ppermute | solution.py:656
  166.1 9.3 %collective-permute-start.43 = (f32[256,256]{1,0:T(8,128)S(1)}, f32[256,256]{1,0:T(8,128)S(1)}, u32[]{:S(2)}, u32[]{:S(2)}) collective-permute-start(f32[256,256]{1,0:T(8,128)S(1)} %get-tuple-element.192.refs_3_), channel_id=1, source_target_pairs={{32,64},{96,128},{160,192},{64,32},{128,96},{192,160},{33,65},{97,... | collective-permute-start | bytes 786440 | tf_op jit(solution)/shard_map/ppermute | solution.py:660
  169.1 8.2 %collective-permute-start.40 = (f32[256,256]{1,0:T(8,128)S(1)}, f32[256,256]{1,0:T(8,128)S(1)}, u32[]{:S(2)}, u32[]{:S(2)}) collective-permute-start(f32[256,256]{1,0:T(8,128)S(1)} %get-tuple-element.188.refs_0_), channel_id=1, source_target_pairs={{0,1},{1,0},{2,3},{3,2},{4,5},{5,4},{6,7},{7,6},{8,9},{9,8},{10,11... | collective-permute-start | bytes 786440 | tf_op jit(solution)/shard_map/ppermute | solution.py:656
  (27 other events, 232.7 us)
